TPU v7x, 512 devices: a whole 4x4x16 slice. The times are simulated.
512 devices in a mesh: lat: 16 (over z), lon: 32 (over x, y, core).
Axes of the slice: x: 4, y: 4, z: 16, core: 2. Of those that a mesh axis runs over, the one named last changes fastest.
Arguments:
- winds: float32 [2, 1024, 23040], P(None, 'lat', 'lon'), may hold values from -6 to 6
- thickness: float32 [1024, 23040], P('lat', 'lon'), may hold values from 0.5 to 1.5
- tracer: float32 [1024, 23040], P('lat', 'lon'), may hold values from -6 to 6
- cutoff: int32 [1024], P('lat'), may hold values from 1 to 1440, as said below
- damping: float32 [1024], P('lat'), may hold values from 0.2 to 1
Outputs:
- new_winds: float32 [2, 1024, 23040], P(None, 'lat', 'lon')
- new_thickness: float32 [1024, 23040], P('lat', 'lon')
- new_tracer: float32 [1024, 23040], P('lat', 'lon')
Inputs may be any that keep to these rules, and one draw needn't show every extreme that they name: cutoff is a wavenumber of 1 to 1440.
All inputs are finite; a program needn't handle non-finite values.
Results may differ from a plain program's by a relative error of at most 0.0003.
Values sent between devices are 32-bit elements; how exact they have to be, the bound alone decides.
No kernel may reach another device: no remote copies, remote signals or barrier semaphores. Data moves between devices by JAX's collectives and lax.ppermute only.
A program may use at most 128 MiB of HBM per device.

v0:
```python
import math

import jax
import jax.numpy as jnp
from jax import lax
from jax.sharding import PartitionSpec as P

LEV = 8


def from_partner(block, axis, stride):
    count = lax.axis_size(axis)
    route = []
    for low in range(count):
        high = low | 1 << stride
        if high != low and high < count:
            route += [(low, high), (high, low)]
    return lax.ppermute(block, axis, route)


def extended(block, sides, width, periodic):
    for axis, dim in sides:
        count = lax.axis_size(axis)
        forward = [(i, i + 1) for i in range(count - 1)]
        if periodic:
            forward.append((count - 1, 0))
        backward = [(target, source) for source, target in forward]
        low = lax.ppermute(
            lax.slice_in_dim(block, block.shape[dim] - width, None, axis=dim), axis, forward
        )
        high = lax.ppermute(lax.slice_in_dim(block, 0, width, axis=dim), axis, backward)
        block = jnp.concatenate([low, block, high], axis=dim)
    return block


def transform(values, cutoffs, damping):
    row_total = values.shape[0]
    length = values.shape[1] // LEV
    shaped = values.reshape(row_total, length, LEV)
    modes = length // 2 + 1
    block_size = min(512, modes)
    positions = jnp.arange(length, dtype=jnp.int32)
    result = shaped
    for start in range(0, modes, block_size):
        wavenumber = start + jnp.arange(block_size, dtype=jnp.int32)
        phases = (positions[:, None] * wavenumber[None, :] % length).astype(jnp.float32) * (
            2.0 * math.pi / length
        )
        cosines = jnp.cos(phases)
        sines = jnp.sin(phases)
        wave_float = wavenumber.astype(jnp.float32)
        mode_scale = jnp.where(
            (wavenumber == 0) | (wavenumber * 2 == length), 1.0 / length, 2.0 / length
        )
        ratios = cutoffs[:, None] / jnp.maximum(wave_float, 1.0)[None, :]
        active = (wavenumber[None, :] < modes) & (wave_float[None, :] > cutoffs[:, None])
        weights = jnp.where(
            active, (1.0 - damping[:, None] * ratios * ratios) * mode_scale[None, :], 0.0
        )
        cos_part = jnp.einsum("rnl,nk->rlk", shaped, cosines, precision=lax.Precision.HIGHEST)
        sin_part = jnp.einsum("rnl,nk->rlk", shaped, sines, precision=lax.Precision.HIGHEST)
        result = result - jnp.einsum(
            "rlk,nk->rnl", cos_part * weights[:, None, :], cosines, precision=lax.Precision.HIGHEST
        )
        result = result - jnp.einsum(
            "rlk,nk->rnl", sin_part * weights[:, None, :], sines, precision=lax.Precision.HIGHEST
        )
    return result.reshape(row_total, length * LEV)


def filter_band(flat_rows, row_params, is_polar):
    owned_rows = lax.all_to_all(flat_rows, "lon", split_axis=0, concat_axis=1, tiled=True)
    owned = owned_rows.shape[0]
    lat_count = row_params.shape[1]
    owner_index = lax.axis_index("lon")
    flat_index = owner_index * owned + jnp.arange(owned, dtype=jnp.int32)
    local_lat = flat_index % lat_count
    select = (local_lat[:, None] == jnp.arange(lat_count, dtype=jnp.int32)[None, :]).astype(
        jnp.float32
    )
    cutoffs = jnp.sum(select * row_params[0][None, :], axis=1)
    damping = jnp.sum(select * row_params[1][None, :], axis=1)

    def apply_filter(values):
        return transform(values, cutoffs, damping)

    def keep_rows(values):
        return values

    filtered = lax.cond(is_polar, apply_filter, keep_rows, owned_rows)
    return lax.all_to_all(filtered, "lon", split_axis=1, concat_axis=0, tiled=True)


def per_device(winds, thickness, tracer, cutoff, damping):
    lat_size = lax.axis_size("lat")
    lon_size = lax.axis_size("lon")
    band_index = lax.axis_index("lat")
    row_count, width = thickness.shape
    columns = width // LEV
    nlon_total = columns * lon_size
    nlat_total = row_count * lat_size
    fields = jnp.concatenate([winds, thickness[None], tracer[None]], axis=0)
    flat_rows = fields.reshape(4 * row_count, width)
    is_polar = (band_index < lat_size // 4) | (band_index >= lat_size - lat_size // 4)
    row_params = jnp.stack([cutoff.astype(jnp.float32), damping])
    filtered = filter_band(flat_rows, row_params, is_polar)
    filtered = filtered.reshape(4, row_count, width)
    zonal = filtered[0]
    meridional = filtered[1]
    layer = filtered[2]
    tracer_mass = filtered[3]
    edge_pair = jnp.stack([layer[0], layer[-1]])
    partner_edges = from_partner(edge_pair, "lon", lon_size.bit_length() - 2)
    padded = extended(jnp.stack([meridional, layer, tracer_mass]), (("lat", 1),), 1, False)
    south_rim = jnp.where(band_index == 0, partner_edges[0], padded[1][0])
    north_rim = jnp.where(band_index == lat_size - 1, partner_edges[1], padded[1][-1])
    wind_pad = padded[0]
    layer_pad = jnp.concatenate([south_rim[None], padded[1][1:-1], north_rim[None]], axis=0)
    tracer_pad = padded[2]
    sides = extended(jnp.stack([zonal, layer, tracer_mass]), (("lon", 2),), LEV, True)
    lon_step = 2.0 * math.pi / nlon_total
    lat_step = math.pi / nlat_total
    global_rows = (band_index * row_count + jnp.arange(row_count, dtype=jnp.int32)).astype(
        jnp.float32
    )
    cos_center = jnp.cos(-math.pi / 2 + (global_rows + 0.5) * lat_step)[:, None]
    face_index = band_index * row_count + jnp.arange(row_count + 1, dtype=jnp.int32)
    face_float = face_index.astype(jnp.float32)
    cos_face = jnp.where(
        (face_index == 0) | (face_index == nlat_total),
        0.0,
        jnp.cos(-math.pi / 2 + face_float * lat_step),
    )[:, None]
    reach = 2 * LEV
    zonal_east = sides[0][:, reach:]
    zonal_west = sides[0][:, :-reach]
    layer_east = sides[1][:, reach:]
    layer_west = sides[1][:, :-reach]
    tracer_east_cell = sides[2][:, reach:]
    tracer_west_cell = sides[2][:, :-reach]
    flux_east = 0.25 * (zonal + zonal_east) * (layer + layer_east)
    flux_west = 0.25 * (zonal_west + zonal) * (layer_west + layer)
    tracer_east = 0.25 * (zonal + zonal_east) * (tracer_mass + tracer_east_cell)
    tracer_west = 0.25 * (zonal_west + zonal) * (tracer_west_cell + tracer_mass)
    wind_face = wind_pad[:-1] + wind_pad[1:]
    flux_north = 0.25 * wind_face * (layer_pad[:-1] + layer_pad[1:]) * cos_face
    tracer_north = 0.25 * wind_face * (tracer_pad[:-1] + tracer_pad[1:]) * cos_face
    layer_div = (
        (flux_east - flux_west) / lon_step + (flux_north[1:] - flux_north[:-1]) / lat_step
    ) / cos_center
    tracer_div = (
        (tracer_east - tracer_west) / lon_step + (tracer_north[1:] - tracer_north[:-1]) / lat_step
    ) / cos_center
    new_layer = layer - lon_step * layer_div
    new_tracer = tracer_mass - lon_step * tracer_div
    new_zonal = zonal - lon_step * (layer_east - layer_west) / (2.0 * lon_step * cos_center)
    new_meridional = meridional - lon_step * (layer_pad[2:] - layer_pad[:-2]) / (2.0 * lat_step)
    return (jnp.stack([new_zonal, new_meridional]), new_layer, new_tracer)


def solution(mesh):
    placed = (P(None, "lat", "lon"), P("lat", "lon"), P("lat", "lon"), P("lat"), P("lat"))
    return jax.shard_map(
        per_device,
        mesh=mesh,
        in_specs=placed,
        out_specs=(P(None, "lat", "lon"), P("lat", "lon"), P("lat", "lon")),
        check_vma=False,
    )
```

profile of v0, /device:TPU:1, one launch (start us, length us, event | category | flops | bytes accessed | tf_op | source)
XLA Modules:
  0.0 437.2 jit_solution(916312962819128761)
XLA Ops:
  2.8 10.4 %all-to-all-start = ((f32[32,8,720]{2,1,0:T(8,128)}), f32[32,8,720]{2,1,0:T(8,128)S(1)}, u32[]{:S(2)}, u32[]{:S(2)}) async-start(f32[32,8,720]{2,1,0:T(8,128)} %bitcast.2), calls=%async_computation | async-start | bytes 1572864 | tf_op jit(solution)/shard_map/all_to_all | solution.py:72
  13.9 13.7 %all-to-all-done = f32[32,8,720]{2,1,0:T(8,128)S(1)} async-done(((f32[32,8,720]{2,1,0:T(8,128)}), f32[32,8,720]{2,1,0:T(8,128)S(1)}, u32[]{:S(2)}, u32[]{:S(2)}) %all-to-all-start) | async-done | bytes 737312 | tf_op jit(solution)/shard_map/all_to_all | solution.py:72
  28.3 371.4 %conditional.1 = (f32[8,23040]{1,0:T(8,128)S(1)}) conditional(s32[]{:T(128)} %convert_element_type.111, f32[8,23040]{1,0:T(8,128)S(1)} %all_to_all.32, (f32[8,23040]{1,0:T(8,128)S(1)}, s32[]{:T(128)}, s32[8]{0:T(128)S(1)}, s32[]{:T(128)}, s32[8,64]{1,0:T(8,128)S(1)}, /*index=5*/f32[64]{0:T(128)S(1)}, f32[64]{0:T(128)S(1)}) %tuple.53), branch_computations={%region_0.1_spmd, %region_1.0_spmd.clone.clone} | conditional | flops 13750219776 | bytes 20952828 | solution.py:90
  28.3 10.7 %reshape.432 = f32[8,2880,8]{2,1,0:T(8,128)} reshape(f32[8,23040]{1,0:T(8,128)S(1)} %get-tuple-element.174) | data formatting | bytes 1474560 | tf_op jit(solution)/shard_map/cond/branch_1_fun/reshape | solution.py:39
  39.0 6.4 %copy.35 = f32[8,2880,8]{1,2,0:T(8,128)S(1)} copy(f32[8,2880,8]{2,1,0:T(8,128)} %reshape.432) | data formatting | bytes 1474560 | tf_op jit(solution)/shard_map/cond/branch_1_fun/reshape | solution.py:39
  45.8 26.6 %fusion.152 = f32[8,8,512]{2,1,0:T(8,128)S(1)} fusion(s32[512]{0:T(512)S(1)} %iota_add_fusion, f32[8,2880,8]{1,2,0:T(8,128)S(1)} %copy.35, f32[8,512]{1,0:T(8,128)S(1)} %get-tuple-element.192), kind=kOutput, calls=%fused_computation.96 | convolution fusion | flops 1145765888 | bytes 886784 | tf_op jit(solution)/shard_map/cond
  72.4 29.0 %fusion.66 = f32[8,2880,8]{1,2,0:T(8,128)S(1)} fusion(f32[8,8,512]{2,1,0:T(8,128)S(1)} %fusion.152, s32[512]{0:T(512)S(1)} %iota_add_fusion), kind=kOutput, calls=%fused_computation.50 | convolution fusion | flops 1145733120 | bytes 870400 | tf_op jit(solution)/shard_map/cond/branch_1_fun/rlk,nk->rnl/dot_general | solution.py:65
  101.5 26.3 %fusion.149 = f32[8,8,512]{2,1,0:T(8,128)S(1)} fusion(s32[512]{0:T(512)S(1)} %iota_add_fusion, f32[8,2880,8]{1,2,0:T(8,128)S(1)} %copy.35, f32[8,512]{1,0:T(8,128)S(1)} %get-tuple-element.192), kind=kOutput, calls=%fused_computation.95 | convolution fusion | flops 1145765888 | bytes 886784 | tf_op jit(solution)/shard_map/cond
  127.8 28.9 %fusion.63 = f32[8,2880,8]{1,2,0:T(8,128)S(1)} fusion(f32[8,8,512]{2,1,0:T(8,128)S(1)} %fusion.149, s32[512]{0:T(512)S(1)} %iota_add_fusion), kind=kOutput, calls=%fused_computation.49 | convolution fusion | flops 1145733120 | bytes 870400 | tf_op jit(solution)/shard_map/cond/branch_1_fun/rlk,nk->rnl/dot_general | solution.py:62
  156.7 26.5 %fusion.158 = f32[8,8,512]{2,1,0:T(8,128)S(1)} fusion(s32[512]{0:T(512)S(1)} %iota_add_fusion.1, f32[8,2880,8]{1,2,0:T(8,128)S(1)} %copy.35, f32[8,512]{1,0:T(8,128)S(1)} %get-tuple-element.191), kind=kOutput, calls=%fused_computation.98 | convolution fusion | flops 1145765888 | bytes 886784 | tf_op jit(solution)/shard_map/cond
  183.1 29.0 %fusion.60 = f32[8,2880,8]{1,2,0:T(8,128)S(1)} fusion(f32[8,8,512]{2,1,0:T(8,128)S(1)} %fusion.158, s32[512]{0:T(512)S(1)} %iota_add_fusion.1), kind=kOutput, calls=%fused_computation.48 | convolution fusion | flops 1145733120 | bytes 870400 | tf_op jit(solution)/shard_map/cond/branch_1_fun/rlk,nk->rnl/dot_general | solution.py:65
  212.2 26.3 %fusion.155 = f32[8,8,512]{2,1,0:T(8,128)S(1)} fusion(s32[512]{0:T(512)S(1)} %iota_add_fusion.1, f32[8,2880,8]{1,2,0:T(8,128)S(1)} %copy.35, f32[8,512]{1,0:T(8,128)S(1)} %get-tuple-element.191), kind=kOutput, calls=%fused_computation.97 | convolution fusion | flops 1145765888 | bytes 886784 | tf_op jit(solution)/shard_map/cond
  238.5 28.9 %fusion.57 = f32[8,2880,8]{1,2,0:T(8,128)S(1)} fusion(f32[8,8,512]{2,1,0:T(8,128)S(1)} %fusion.155, s32[512]{0:T(512)S(1)} %iota_add_fusion.1), kind=kOutput, calls=%fused_computation.47 | convolution fusion | flops 1145733120 | bytes 870400 | tf_op jit(solution)/shard_map/cond/branch_1_fun/rlk,nk->rnl/dot_general | solution.py:62
  267.3 26.4 %fusion.161 = f32[8,8,512]{2,1,0:T(8,128)S(1)} fusion(f32[8,2880,8]{1,2,0:T(8,128)S(1)} %copy.35, f32[8,512]{1,0:T(8,128)S(1)} %get-tuple-element.190), kind=kOutput, calls=%fused_computation.99 | convolution fusion | flops 1145765888 | bytes 884736 | tf_op jit(solution)/shard_map/cond
  293.7 29.0 %fusion.81 = f32[8,2880,8]{1,2,0:T(8,128)S(1)} fusion(f32[8,2880,8]{1,2,0:T(8,128)S(1)} %copy.35, f32[8,8,512]{2,1,0:T(8,128)S(1)} %fusion.161), kind=kOutput, calls=%fused_computation.55 | convolution fusion | flops 1145917440 | bytes 1605632 | tf_op jit(solution)/shard_map/cond/branch_1_fun/rlk,nk->rnl/dot_general | solution.py:62
  322.7 26.6 %fusion.164 = f32[8,8,512]{2,1,0:T(8,128)S(1)} fusion(f32[8,2880,8]{1,2,0:T(8,128)S(1)} %copy.35, f32[8,512]{1,0:T(8,128)S(1)} %get-tuple-element.190), kind=kOutput, calls=%fused_computation.100 | convolution fusion | flops 1145765888 | bytes 884736 | tf_op jit(solution)/shard_map/cond
  349.3 29.3 %fusion.84 = f32[8,2880,8]{1,2,0:T(8,128)S(1)} fusion(f32[8,2880,8]{1,2,0:T(8,128)S(1)} %fusion.66, f32[8,2880,8]{1,2,0:T(8,128)S(1)} %fusion.63, f32[8,2880,8]{1,2,0:T(8,128)S(1)} %fusion.60, f32[8,2880,8]{1,2,0:T(8,128)S(1)} %fusion.57, f32[8,2880,8]{1,2,0:T(8,128)S(1)} %fusion.81, f32[8,8,512]{2,1,0:T(8,128)S(1)} %fusion.164), kind=kOutput, calls=%fused_computation.56 | convolution fusion | flops 1146654720 | bytes 4554752 | tf_op jit(solution)/shard_map/cond/branch_1_fun/rlk,nk->rnl/dot_general | solution.py:65
  378.6 5.8 %copy.36 = f32[8,2880,8]{2,1,0:T(8,128)} copy(f32[8,2880,8]{1,2,0:T(8,128)S(1)} %fusion.84) | data formatting | bytes 1474560 | tf_op jit(solution)/shard_map/cond/branch_1_fun/sub | solution.py:65
  384.4 15.0 %reshape.433 = f32[8,23040]{1,0:T(8,128)S(1)} reshape(f32[8,2880,8]{2,1,0:T(8,128)} %copy.36) | data formatting | bytes 1474560 | tf_op jit(solution)/shard_map/cond/branch_1_fun/reshape | solution.py:68
  401.7 3.8 all-to-all-start.1
  405.6 14.1 %all-to-all-done.1 = f32[8,32,720]{2,0,1:T(8,128)S(1)} async-done(((f32[8,32,720]{2,0,1:T(8,128)}), f32[8,32,720]{2,0,1:T(8,128)S(1)}, u32[]{:S(2)}, u32[]{:S(2)}) %all-to-all-start.1) | async-done | bytes 737312 | tf_op jit(solution)/shard_map/all_to_all | solution.py:91
  421.9 3.6 collective-permute-start
  426.9 3.1 collective-permute-start.2
  430.0 4.0 collective-permute-start.4
  (46 shorter events, 12.4 us)
Async XLA Ops:
  0.6 27.6 %copy-start = (f32[64]{0:T(128)S(1)}, f32[64]{0:T(128)}, u32[]{:S(2)}) copy-start(f32[64]{0:T(128)} %param.11) | copy-start | bytes 772
  2.8 24.8 %all-to-all-start = ((f32[32,8,720]{2,1,0:T(8,128)}), f32[32,8,720]{2,1,0:T(8,128)S(1)}, u32[]{:S(2)}, u32[]{:S(2)}) async-start(f32[32,8,720]{2,1,0:T(8,128)} %bitcast.2), calls=%async_computation | async-start | bytes 1572864 | tf_op jit(solution)/shard_map/all_to_all | solution.py:72
  401.7 18.0 %all-to-all-start.1 = ((f32[8,32,720]{2,0,1:T(8,128)}), f32[8,32,720]{2,0,1:T(8,128)S(1)}, u32[]{:S(2)}, u32[]{:S(2)}) async-start(f32[8,32,720]{2,0,1:T(8,128)} %copy.34), calls=%async_computation.1 | async-start | bytes 1572864 | tf_op jit(solution)/shard_map/all_to_all | solution.py:91
  419.9 14.1 %collective-permute-start.1 = (f32[3,64,8]{2,1,0:T(8,128)S(1)}, f32[3,64,8]{2,1,0:T(8,128)S(1)}, u32[]{:S(2)}, u32[]{:S(2)}) collective-permute-start(f32[3,64,8]{2,1,0:T(8,128)S(1)} %get-tuple-element.216), channel_id=1, source_target_pairs={{1,0},{2,1},{3,2},{4,3},{5,4},{6,5},{7,6},{8,7},{9,8},{10,9},{11,1... | collective-permute-start | bytes 18440 | tf_op jit(solution)/shard_map/ppermute | solution.py:31
  421.9 12.1 %collective-permute-start = (f32[3,64,8]{2,1,0:T(8,128)S(1)}, f32[3,64,8]{2,1,0:T(8,128)S(1)}, u32[]{:S(2)}, u32[]{:S(2)}) collective-permute-start(f32[3,64,8]{2,1,0:T(8,128)S(1)} %get-tuple-element.215), channel_id=1, source_target_pairs={{0,1},{1,2},{2,3},{3,4},{4,5},{5,6},{6,7},{7,8},{8,9},{9,10},{10,1... | collective-permute-start | bytes 18440 | tf_op jit(solution)/shard_map/ppermute | solution.py:28
  425.5 8.8 %collective-permute-start.3 = (f32[3,1,720]{2,1,0:T(1,128)S(1)}, f32[3,1,720]{2,1,0:T(1,128)S(1)}, u32[]{:S(2)}, u32[]{:S(2)}) collective-permute-start(f32[3,1,720]{2,1,0:T(1,128)S(1)} %get-tuple-element.217), channel_id=1, source_target_pairs={{32,0},{64,32},{96,64},{128,96},{160,128},{192,160},{224,192},{256... | collective-permute-start | bytes 25928 | tf_op jit(solution)/shard_map/ppermute | solution.py:31
  426.9 7.4 %collective-permute-start.2 = (f32[2,720]{1,0:T(2,128)S(1)}, f32[2,720]{1,0:T(2,128)S(1)}, u32[]{:S(2)}, u32[]{:S(2)}) collective-permute-start(f32[2,720]{1,0:T(2,128)S(1)} %pad_maximum_fusion.15), channel_id=1, source_target_pairs={{0,16},{16,0},{1,17},{17,1},{2,18},{18,2},{3,19},{19,3},{4,20},{20... | collective-permute-start | bytes 17288 | tf_op jit(solution)/shard_map/ppermute | solution.py:18
  430.0 4.8 %collective-permute-start.4 = (f32[3,1,720]{2,1,0:T(1,128)S(1)}, f32[3,1,720]{2,1,0:T(1,128)S(1)}, u32[]{:S(2)}, u32[]{:S(2)}) collective-permute-start(f32[3,1,720]{2,1,0:T(1,128)S(1)} %get-tuple-element.218), channel_id=1, source_target_pairs={{0,32},{32,64},{64,96},{96,128},{128,160},{160,192},{192,224},{224... | collective-permute-start | bytes 25928 | tf_op jit(solution)/shard_map/ppermute | solution.py:28
where the time goes:
time: 443 us; the launch traced here: 437 us
  matrix products  333 us (75%)
  local copies, waits for them, and re-layouts  40.9 us (9%)
  waiting for transfers between devices  28.2 us (6%)
  starting transfers between devices  28.1 us (6%)
  other arithmetic  5.78 us (1%)
    cond x6, matrix products  159 us
    dot_general x3, matrix products, transform(): jnp.einsum('rlk,nk->rnl', sin_part * weights[:, None, :], sines, precisio...  87.4 us
    dot_general x3, matrix products, transform(): jnp.einsum('rlk,nk->rnl', cos_part * weights[:, None, :], cosines, precis...  86.7 us
    reshape x2, local copies, waits for them, and re-layouts, transform(): shaped = values.reshape(row_total, length, LEV)  17.1 us
    reshape x1, local copies, waits for them, and re-layouts, transform(): return result.reshape(row_total, length * LEV)  15 us
    all_to_all x1, waiting for transfers between devices, filter_band(): lax.all_to_all(filtered, 'lon', split_axis=1, concat_axis=0, tiled=True)  14.1 us
    all_to_all x1, waiting for transfers between devices, filter_band(): lax.all_to_all(flat_rows, 'lon', split_axis=0, concat_axis=1, tiled=True)  13.7 us
    all_to_all x1, starting transfers between devices, filter_band(): lax.all_to_all(flat_rows, 'lon', split_axis=0, concat_axis=1, tiled=True)  10.4 us
  transfers between devices with their start and end apart: 7, of which 3 were waited for; matrix products, arithmetic and copies ran while one was open for 0% of the time, Pallas kernels for 0%

commit v1 on v0

v1 whole, which is shorter than its diff:
```python
import functools
import math

import jax
import jax.numpy as jnp
import numpy as np
from jax import lax
from jax.experimental import pallas as pl
from jax.experimental.pallas import tpu as pltpu
from jax.sharding import PartitionSpec as P

LEV = 8
NLON = 2880
LANE = 128
TILES = NLON * LEV // LANE
STEP = LANE // LEV
WIDE = 768


def _lin(terms):
    total = None
    for weight, value in terms:
        if value is None or abs(weight) < 1e-12:
            continue
        if abs(weight - 1.0) < 1e-12:
            item = value
        else:
            item = value * np.float32(weight)
        total = item if total is None else total + item
    return total


def _odd_tables(size):
    half = (size - 1) // 2
    angle = [[2.0 * math.pi * ((j * k) % size) / size for j in range(half + 1)] for k in range(half + 1)]
    return half, angle


def odd_real_forward(values):
    size = len(values)
    half, angle = _odd_tables(size)
    plus = [values[j] + values[size - j] for j in range(1, half + 1)]
    minus = [values[j] - values[size - j] for j in range(1, half + 1)]
    out = [(_lin([(1.0, values[0])] + [(1.0, t) for t in plus]), None)]
    for k in range(1, half + 1):
        real = _lin([(1.0, values[0])] + [(math.cos(angle[k][j]), plus[j - 1]) for j in range(1, half + 1)])
        imag = _lin([(-math.sin(angle[k][j]), minus[j - 1]) for j in range(1, half + 1)])
        out.append((real, imag))
    return out


def odd_real_inverse(bins):
    half = len(bins) - 1
    size = 2 * half + 1
    _, angle = _odd_tables(size)
    doubled = [(b[0] * np.float32(2.0), b[1] * np.float32(2.0)) for b in bins[1:]]
    out = [None] * size
    out[0] = _lin([(1.0, bins[0][0])] + [(1.0, b[0]) for b in doubled])
    for n in range(1, half + 1):
        even = _lin([(1.0, bins[0][0])] + [(math.cos(angle[n][k]), doubled[k - 1][0]) for k in range(1, half + 1)])
        odd = _lin([(math.sin(angle[n][k]), doubled[k - 1][1]) for k in range(1, half + 1)])
        out[n] = even - odd
        out[size - n] = even + odd
    return out


def odd_complex(values, sign):
    size = len(values)
    half, angle = _odd_tables(size)
    out = [None] * size
    plus = [(values[j][0] + values[size - j][0], values[j][1] + values[size - j][1]) for j in range(1, half + 1)]
    minus = [(values[j][0] - values[size - j][0], values[j][1] - values[size - j][1]) for j in range(1, half + 1)]
    out[0] = tuple(_lin([(1.0, values[0][part])] + [(1.0, t[part]) for t in plus]) for part in (0, 1))
    for k in range(1, half + 1):
        base = [
            _lin([(1.0, values[0][part])] + [(math.cos(angle[k][j]), plus[j - 1][part]) for j in range(1, half + 1)])
            for part in (0, 1)
        ]
        turn = [_lin([(math.sin(angle[k][j]), minus[j - 1][part]) for j in range(1, half + 1)]) for part in (0, 1)]
        low = (base[0] + turn[1], base[1] - turn[0])
        high = (base[0] - turn[1], base[1] + turn[0])
        if sign < 0:
            out[k], out[size - k] = low, high
        else:
            out[k], out[size - k] = high, low
    return out


COMPLEX_CLASSES = [(0, 1), (0, 2), (2, 1), (2, 2), (1, 0), (1, 1), (1, 2), (1, 3), (1, 4)]


def _tile_of(a, b, c):
    return (45 * a + 36 * b + 20 * c) % TILES


def _bin_of(alpha, beta, gamma):
    for kappa in range(TILES):
        if kappa % 4 == alpha and kappa % 5 == beta and kappa % 9 == gamma:
            return kappa
    raise ValueError


def _bin_list():
    bins = []
    for alpha in (0, 2):
        bins += [(alpha, 0, gamma) for gamma in range(5)]
    for alpha, beta in COMPLEX_CLASSES:
        bins += [(alpha, beta, gamma) for gamma in range(9)]
    return bins


BINS = _bin_list()
COUNT = len(BINS)
SLOT = {key: index for index, key in enumerate(BINS)}
REAL_ROWS = {(0, 0): 0, (2, 0): 1}
COMPLEX_ROWS = {key: 2 + 2 * index for index, key in enumerate(COMPLEX_CLASSES)}


@functools.lru_cache(maxsize=1)
def tables():
    kappa = np.array([_bin_of(*key) for key in BINS])
    phase = (np.arange(LANE) // LEV)[None, :]
    turn = 2.0 * np.pi * ((kappa[:, None] * phase) % NLON) / NLON
    wave = kappa[:, None] + TILES * phase
    wave = np.minimum(wave, NLON - wave).astype(np.float64)
    rows = np.stack(
        [np.cos(turn), np.sin(turn), wave, 1.0 / (np.maximum(wave, 1.0) ** 2 * NLON)], axis=0
    ).astype(np.float32)
    s = np.arange(LANE) // LEV
    level = np.arange(LANE) % LEV
    same = (level[:, None] == level[None, :]).astype(np.float64)
    angle = 2.0 * np.pi * ((s[:, None] * s[None, :]) % STEP) / STEP
    cosines = np.cos(angle) * same
    sines = np.sin(angle) * same
    forward = np.block([[cosines, -sines], [sines, cosines]]).astype(np.float32)
    return rows, forward, forward.T.copy()


GROUP = 13


def filter_kernel(x_ref, cut_ref, rows_ref, forward_ref, inverse_ref, out_ref, full, mid, stage):
    sectors = x_ref.shape[0]
    span = x_ref.shape[2]
    for d in range(sectors):
        full[:, LANE + d * span : LANE + (d + 1) * span] = x_ref[d]

    def tile(p):
        return slice(LANE * (p + 1), LANE * (p + 2))

    for c in range(9):
        quarter = []
        for b in range(5):
            v = [full[:, tile(_tile_of(a, b, c))] for a in range(4)]
            even, odd = v[0] + v[2], v[1] + v[3]
            quarter.append((even + odd, even - odd, v[0] - v[2], v[3] - v[1]))
        zero = odd_real_forward([q[0] for q in quarter])
        two = odd_real_forward([q[1] for q in quarter])
        one = odd_complex([(q[2], q[3]) for q in quarter], -1)
        mid[0, c] = zero[0][0]
        mid[1, c] = two[0][0]
        pieces = {(0, 1): zero[1], (0, 2): zero[2], (2, 1): two[1], (2, 2): two[2]}
        for beta in range(5):
            pieces[(1, beta)] = one[beta]
        for key, value in pieces.items():
            row = COMPLEX_ROWS[key]
            mid[row, c] = value[0]
            mid[row + 1, c] = value[1]

    def put(slot, value):
        cos_row = rows_ref[0, slot : slot + 1, :]
        sin_row = rows_ref[1, slot : slot + 1, :]
        where = slice(8 * slot, 8 * slot + 8)
        if value[1] is None:
            stage[where, :LANE] = value[0] * cos_row
            stage[where, LANE:] = -(value[0] * sin_row)
        else:
            stage[where, :LANE] = value[0] * cos_row + value[1] * sin_row
            stage[where, LANE:] = value[1] * cos_row - value[0] * sin_row

    for key, row in REAL_ROWS.items():
        for gamma, value in enumerate(odd_real_forward([mid[row, c] for c in range(9)])):
            put(SLOT[(key[0], key[1], gamma)], value)
    for key, row in COMPLEX_ROWS.items():
        for gamma, value in enumerate(odd_complex([(mid[row, c], mid[row + 1, c]) for c in range(9)], -1)):
            put(SLOT[(key[0], key[1], gamma)], value)

    cut = cut_ref[0]
    gain = cut_ref[1]
    for start in range(0, COUNT, GROUP):
        where = slice(8 * start, 8 * (start + GROUP))
        spectrum = jnp.dot(
            stage[where, :], forward_ref[...], precision=lax.Precision.HIGHEST, preferred_element_type=jnp.float32
        )
        scaled = []
        for index in range(GROUP):
            slot = start + index
            wave = rows_ref[2, slot : slot + 1, :]
            decay = rows_ref[3, slot : slot + 1, :]
            factor = jnp.where(wave > cut, gain * decay, np.float32(1.0 / NLON))
            part = spectrum[8 * index : 8 * index + 8, :]
            scaled.append(part * jnp.concatenate([factor, factor], axis=1))
        stage[where, :] = jnp.dot(
            jnp.concatenate(scaled, axis=0),
            inverse_ref[...],
            precision=lax.Precision.HIGHEST,
            preferred_element_type=jnp.float32,
        )

    def take(slot, real):
        cos_row = rows_ref[0, slot : slot + 1, :]
        sin_row = rows_ref[1, slot : slot + 1, :]
        where = slice(8 * slot, 8 * slot + 8)
        re, im = stage[where, :LANE], stage[where, LANE:]
        if real:
            return (re * cos_row - im * sin_row, None)
        return (re * cos_row - im * sin_row, im * cos_row + re * sin_row)

    for key, row in REAL_ROWS.items():
        values = odd_real_inverse([take(SLOT[(key[0], key[1], gamma)], gamma == 0) for gamma in range(5)])
        for c in range(9):
            mid[row, c] = values[c]
    for key, row in COMPLEX_ROWS.items():
        values = odd_complex([take(SLOT[(key[0], key[1], gamma)], False) for gamma in range(9)], 1)
        for c in range(9):
            mid[row, c] = values[c][0]
            mid[row + 1, c] = values[c][1]

    for c in range(9):

        def piece(key):
            row = COMPLEX_ROWS[key]
            return (mid[row, c], mid[row + 1, c])

        zero = odd_real_inverse([(mid[0, c], None), piece((0, 1)), piece((0, 2))])
        two = odd_real_inverse([(mid[1, c], None), piece((2, 1)), piece((2, 2))])
        one = odd_complex([piece((1, beta)) for beta in range(5)], 1)
        for b in range(5):
            even, odd = zero[b] + two[b], zero[b] - two[b]
            re2, im2 = one[b][0] + one[b][0], one[b][1] + one[b][1]
            values = (even + re2, odd - im2, even - re2, odd + im2)
            for a in range(4):
                p = _tile_of(a, b, c)
                full[:, tile(p)] = values[a]
                if p == 0:
                    full[:, tile(TILES)] = values[a]
                if p == TILES - 1:
                    full[:, tile(-1)] = values[a]

    for d in range(sectors):
        first = LANE + d * span
        out_ref[d, :, 0 : span + LEV] = full[:, first : first + span + LEV]
        out_ref[d, :, span + LEV : WIDE - LEV] = jnp.zeros((8, WIDE - span - 2 * LEV), jnp.float32)
        out_ref[d, :, WIDE - LEV : WIDE] = full[:, first - LEV : first]


def filter_rows(blocks, cuts):
    rows, forward, inverse = tables()
    return pl.pallas_call(
        filter_kernel,
        out_shape=jax.ShapeDtypeStruct((blocks.shape[0], 8, WIDE), jnp.float32),
        in_specs=[pl.BlockSpec(memory_space=pltpu.VMEM)] * 5,
        out_specs=pl.BlockSpec(memory_space=pltpu.VMEM),
        scratch_shapes=[
            pltpu.VMEM((8, (TILES + 2) * LANE), jnp.float32),
            pltpu.VMEM((20, 9, 8, LANE), jnp.float32),
            pltpu.VMEM((8 * COUNT, 2 * LANE), jnp.float32),
        ],
        name="polar_filter",
    )(blocks, cuts, jnp.asarray(rows), jnp.asarray(forward), jnp.asarray(inverse))


def stencil_kernel(ratio, even_ref, field_ref, first_ref, second_ref, coef_ref, winds_ref, layer_ref, tracer_ref, tall):
    is_even = even_ref[0] > 0
    first = first_ref[...]
    second = second_ref[...]
    south = jnp.where(is_even, second, first)
    north = jnp.where(is_even, first, second)
    for f in range(3):
        tall[f, 7:8, :] = south[f : f + 1, :]
        tall[f, 72:73, :] = north[f : f + 1, :]
        for g in range(8):
            tall[f, 8 + 8 * g : 16 + 8 * g, :] = field_ref[8 * (f + 1) + g]

    def east(x):
        return pltpu.roll(x, WIDE - LEV, 1)

    def west(x):
        return pltpu.roll(x, LEV, 1)

    span = layer_ref.shape[1]
    for g in range(8):
        rows = slice(8 * g, 8 * g + 8)
        at = 8 + 8 * g
        u = field_ref[g]
        v, h, q = (tall[f, at : at + 8, :] for f in range(3))
        v_s, h_s, q_s = (tall[f, at - 1 : at + 7, :] for f in range(3))
        v_n, h_n, q_n = (tall[f, at + 1 : at + 9, :] for f in range(3))
        zonal = coef_ref[rows, 0:1]
        to_north = coef_ref[rows, 1:2]
        to_south = coef_ref[rows, 2:3]
        slope = coef_ref[rows, 3:4]
        h_e = east(h)
        su = u + east(u)
        fx = su * (h + h_e)
        gx = su * (q + east(q))
        wind_n = (v + v_n) * to_north
        wind_s = (v_s + v) * to_south
        new_h = h - (zonal * (fx - west(fx)) + (wind_n * (h + h_n) - wind_s * (h_s + h)))
        new_q = q - (zonal * (gx - west(gx)) + (wind_n * (q + q_n) - wind_s * (q_s + q)))
        new_u = u - slope * (h_e - west(h))
        new_v = v - np.float32(ratio) * (h_n - h_s)
        winds_ref[0, rows, :] = new_u[:, :span]
        winds_ref[1, rows, :] = new_v[:, :span]
        layer_ref[rows, :] = new_h[:, :span]
        tracer_ref[rows, :] = new_q[:, :span]


def stencil(even, fields, first, second, coef, ratio, row_count, width):
    vmem = pl.BlockSpec(memory_space=pltpu.VMEM)
    return pl.pallas_call(
        functools.partial(stencil_kernel, ratio),
        out_shape=(
            jax.ShapeDtypeStruct((2, row_count, width), jnp.float32),
            jax.ShapeDtypeStruct((row_count, width), jnp.float32),
            jax.ShapeDtypeStruct((row_count, width), jnp.float32),
        ),
        in_specs=[pl.BlockSpec(memory_space=pltpu.SMEM), vmem, vmem, vmem, vmem],
        out_specs=(vmem, vmem, vmem),
        scratch_shapes=[pltpu.VMEM((3, row_count + 16, WIDE), jnp.float32)],
        name="stencil",
    )(even, fields, first, second, coef)


def per_device(winds, thickness, tracer, cutoff, damping):
    lat_size = lax.axis_size("lat")
    lon_size = lax.axis_size("lon")
    band = lax.axis_index("lat")
    sector = lax.axis_index("lon")
    row_count, width = thickness.shape
    nlat = row_count * lat_size

    flat = jnp.concatenate([winds.reshape(2 * row_count, width), thickness, tracer], axis=0)
    blocks = flat.reshape(lon_size, 4 * row_count // lon_size, width)
    owned = lax.all_to_all(blocks, "lon", split_axis=0, concat_axis=0, tiled=True)

    is_polar = (band < lat_size // 4) | (band >= lat_size - lat_size // 4)
    group = sector % (row_count // 8)
    cut = lax.dynamic_slice_in_dim(cutoff.astype(jnp.float32), group * 8, 8)
    damp = lax.dynamic_slice_in_dim(damping, group * 8, 8)
    gain = damp * cut * cut
    cut = jnp.where(is_polar, cut, jnp.float32(NLON))
    cuts = jnp.broadcast_to(jnp.stack([cut, gain])[:, :, None], (2, 8, LANE))

    filtered = filter_rows(owned, cuts)
    fields = lax.all_to_all(filtered, "lon", split_axis=0, concat_axis=0, tiled=True)

    even = band % 2 == 0
    groups = row_count // 8
    low = jnp.stack([fields[f * groups, 0] for f in (1, 2, 3)])
    high = jnp.stack([fields[f * groups + groups - 1, 7] for f in (1, 2, 3)])
    pairs = {0: [], 1: []}
    for z in range(lat_size):
        for e in range(lon_size):
            here = z * lon_size + e
            across = z * lon_size + (e + lon_size // 2) % lon_size
            up = here + lon_size if z < lat_size - 1 else across
            down = here - lon_size if z > 0 else across
            pairs[0].append((here, up if z % 2 == 0 else down))
            pairs[1].append((here, down if z % 2 == 0 else up))
    first = lax.ppermute(jnp.where(even, high, low), ("lat", "lon"), pairs[0])
    second = lax.ppermute(jnp.where(even, low, high), ("lat", "lon"), pairs[1])

    lon_step = 2.0 * math.pi / NLON
    lat_step = math.pi / nlat
    rows = (band * row_count + jnp.arange(row_count, dtype=jnp.int32)).astype(jnp.float32)
    center = jnp.cos(-math.pi / 2 + (rows + 0.5) * lat_step)
    face = band * row_count + jnp.arange(row_count + 1, dtype=jnp.int32)
    cos_face = jnp.where(
        (face == 0) | (face == nlat), 0.0, jnp.cos(-math.pi / 2 + face.astype(jnp.float32) * lat_step)
    )
    quarter = 0.25 / center
    aspect = lon_step / lat_step
    coef = jnp.stack(
        [quarter, aspect * quarter * cos_face[1:], aspect * quarter * cos_face[:-1], 2.0 * quarter], axis=1
    )
    coef = jnp.pad(coef, ((0, 0), (0, LANE - 4)))
    return stencil(
        even.astype(jnp.int32)[None], fields, first, second, coef, lon_step / (2.0 * lat_step), row_count, width
    )


def solution(mesh):
    placed = (P(None, "lat", "lon"), P("lat", "lon"), P("lat", "lon"), P("lat"), P("lat"))
    return jax.shard_map(
        per_device,
        mesh=mesh,
        in_specs=placed,
        out_specs=(P(None, "lat", "lon"), P("lat", "lon"), P("lat", "lon")),
        check_vma=False,
    )
```

time: 443 us -> 63.4 us (0.14); the launches traced: 437 us -> 62.9 us
  matrix products: 333 us -> 0 us
  local copies, waits for them, and re-layouts: 40.9 us -> 3.54 us
  starting transfers between devices: 28.1 us -> 19.3 us
  Pallas kernels: 0 us -> 8.3 us
    dot_general x6 -> x0, matrix products: 174 us -> none  [the longest x3 87.4 us: transform(): jnp.einsum('rlk,nk->rnl', sin_part * weights[:, None, :], sines, precisio...]
    cond x6 -> x0, matrix products: 159 us -> none
    reshape x3 -> x0, local copies, waits for them, and re-layouts: 32.1 us -> none  [the longest x2 17.1 us: transform(): shaped = values.reshape(row_total, length, LEV)]
    ppermute x5 -> x2, starting transfers between devices: 14 us -> 5.19 us  [the longest x1 3.11 us: per_device(): second = lax.ppermute(jnp.where(even, low, high), ('lat', 'lon'), pairs[1])]
    pallas_call x0 -> x2, Pallas kernels: none -> 8.3 us  [the longest x1 5.51 us: filter_rows(): pl.pallas_call(filter_kernel, out_shape=jax.ShapeDtypeStruct((blocks.shap...]
    sub x1 -> x0, local copies, waits for them, and re-layouts: 5.85 us -> none  [transform(): result - jnp.einsum('rlk,nk->rnl', sin_part * weights[:, None, :], sines,...]
  transfers between devices with their start and end apart: 7 -> 4, of which waited for: 3 -> 3; matrix products, arithmetic and copies ran while one was open for 0% -> 2% of each run, Pallas kernels for 0% -> 0%
where the time goes in v1:
time: 63.4 us; the launch traced here: 62.9 us
  waiting for transfers between devices  28.6 us (45%)
  starting transfers between devices  19.3 us (30%)
  Pallas kernels  8.3 us (13%)
  local copies, waits for them, and re-layouts  3.54 us (6%)
  other arithmetic  2.44 us (4%)
  between operations  0.74 us (1%)
    all_to_all x1, waiting for transfers between devices, per_device(): lax.all_to_all(filtered, 'lon', split_axis=0, concat_axis=0, tiled=True)  14.1 us
    all_to_all x1, waiting for transfers between devices, per_device(): lax.all_to_all(blocks, 'lon', split_axis=0, concat_axis=0, tiled=True)  12.9 us
    all_to_all x1, starting transfers between devices, per_device(): lax.all_to_all(blocks, 'lon', split_axis=0, concat_axis=0, tiled=True)  10.4 us
    pallas_call x1, Pallas kernels, filter_rows(): pl.pallas_call(filter_kernel, out_shape=jax.ShapeDtypeStruct((blocks.shap...  5.51 us
    all_to_all x1, starting transfers between devices, per_device(): lax.all_to_all(filtered, 'lon', split_axis=0, concat_axis=0, tiled=True)  3.76 us
    ppermute x1, starting transfers between devices, per_device(): second = lax.ppermute(jnp.where(even, low, high), ('lat', 'lon'), pairs[1])  3.11 us
    pallas_call x1, Pallas kernels, stencil(): pl.pallas_call(functools.partial(stencil_kernel, ratio), out_shape=(jax.S...  2.79 us
    reshape x1, other arithmetic, per_device(): blocks = flat.reshape(lon_size, 4 * row_count // lon_size, width)  2.15 us
  transfers between devices with their start and end apart: 4, of which 3 were waited for; matrix products, arithmetic and copies ran while one was open for 2% of the time, Pallas kernels for 0%

profile of v1, /device:TPU:1, one launch (start us, length us, event | category | flops | bytes accessed | tf_op | source)
XLA Modules:
  0.0 62.9 jit_solution(18106681632545921646)
XLA Ops:
  0.6 2.1 %maximum_bitcast_fusion = f32[32,8,720]{2,1,0:T(8,128)} fusion(f32[64,720]{1,0:T(8,128)} %param.10, f32[64,720]{1,0:T(8,128)} %param.9, f32[128,720]{1,0:T(8,128)} %bitcast.24), kind=kLoop, calls=%fused_computation | loop fusion | flops 368640 | bytes 1474560 | tf_op jit(solution)/shard_map/reshape | solution.py:344
  2.8 10.4 %all-to-all-start = ((f32[32,8,720]{2,1,0:T(8,128)}), f32[32,8,720]{2,1,0:T(8,128)S(1)}, u32[]{:S(2)}, u32[]{:S(2)}) async-start(f32[32,8,720]{2,1,0:T(8,128)} %maximum_bitcast_fusion), calls=%async_computation | async-start | bytes 1572864 | tf_op jit(solution)/shard_map/all_to_all | solution.py:345
  13.2 0.0 copy-start.5
  13.2 0.6 %copy-done.5 = s32[64]{0:T(128)S(1)} copy-done((s32[64]{0:T(128)S(1)}, s32[64]{0:T(128)}, u32[]{:S(2)}) %copy-start.5) | copy-done | bytes 280
  13.9 0.7 %copy-done.4 = f32[64]{0:T(128)S(1)} copy-done((f32[64]{0:T(128)S(1)}, f32[64]{0:T(128)}, u32[]{:S(2)}) %copy-start.4) | copy-done | bytes 280
  14.5 0.1 fusion.3
  14.6 12.9 %all-to-all-done.x_ref = f32[32,8,720]{2,1,0:T(8,128)S(1)} async-done(((f32[32,8,720]{2,1,0:T(8,128)}), f32[32,8,720]{2,1,0:T(8,128)S(1)}, u32[]{:S(2)}, u32[]{:S(2)}) %all-to-all-start) | async-done | bytes 737312 | tf_op jit(solution)/shard_map/all_to_all | solution.py:345
  27.5 0.8 %broadcast_in_dim.22.cut_ref = f32[2,8,128]{2,1,0:T(8,128)} broadcast(f32[2,8]{1,0:T(2,128)S(1)} %pad_maximum_fusion.3), dimensions={0,1} | broadcast | bytes 8256 | tf_op jit(solution)/shard_map/broadcast_in_dim | solution.py:353
  28.3 0.1 copy-done.1
  28.4 5.5 %polar_filter.1 = f32[32,8,768]{2,1,0:T(8,128)} custom-call(f32[32,8,720]{2,1,0:T(8,128)} %copy-done.1, f32[2,8,128]{2,1,0:T(8,128)} %broadcast_in_dim.22.cut_ref, f32[4,91,128]{2,1,0:T(8,128)} %constant.67.clone.rows_ref, f32[256,256]{1,0:T(8,128)} %constant.68.clone.forward_ref, f32[256,256]{1,0:T(8,128)} %constant.69.clone.inverse_ref), custom_call_target="tpu_custom_call" | custom-call | tf_op jit(solution)/shard_map/polar_filter/pallas_call | solution.py:259
  33.9 3.8 %all-to-all-start.1 = ((f32[32,8,768]{2,1,0:T(8,128)}), f32[32,8,768]{2,1,0:T(8,128)S(1)}, u32[]{:S(2)}, u32[]{:S(2)}) async-start(f32[32,8,768]{2,1,0:T(8,128)} %polar_filter.1), calls=%async_computation.1 | async-start | bytes 1572864 | tf_op jit(solution)/shard_map/all_to_all | solution.py:356
  37.8 0.1 cosine_divide_fusion
  37.8 0.1 multiply_bitcast_fusion.1
  37.9 14.1 %all-to-all-done.1.field_ref = f32[32,8,768]{2,1,0:T(8,128)S(1)} async-done(((f32[32,8,768]{2,1,0:T(8,128)}), f32[32,8,768]{2,1,0:T(8,128)S(1)}, u32[]{:S(2)}, u32[]{:S(2)}) %all-to-all-start.1) | async-done | bytes 786464 | tf_op jit(solution)/shard_map/all_to_all | solution.py:356
  52.0 3.1 %collective-permute-start.1 = (f32[3,768]{1,0:T(4,128)S(1)}, f32[3,768]{1,0:T(4,128)S(1)}, u32[]{:S(2)}, u32[]{:S(2)}) collective-permute-start(f32[3,768]{1,0:T(4,128)S(1)} %get-tuple-element.9), channel_id=1, source_target_pairs={{0,16},{1,17},{2,18},{3,19},{4,20},{5,21},{6,22},{7,23},{8,24},{9,... | collective-permute-start | bytes 27656 | tf_op jit(solution)/shard_map/ppermute | solution.py:372
  55.1 2.1 %collective-permute-start = (f32[3,768]{1,0:T(4,128)S(1)}, f32[3,768]{1,0:T(4,128)S(1)}, u32[]{:S(2)}, u32[]{:S(2)}) collective-permute-start(f32[3,768]{1,0:T(4,128)S(1)} %get-tuple-element.10), channel_id=1, source_target_pairs={{0,32},{1,33},{2,34},{3,35},{4,36},{5,37},{6,38},{7,39},{8,40},{9,... | collective-permute-start | bytes 27656 | tf_op jit(solution)/shard_map/ppermute | solution.py:371
  57.2 0.1 copy.13
  57.3 0.6 pad.4.coef_ref
  57.9 0.0 collective-permute-done.1.second_ref
  57.9 1.6 %collective-permute-done.first_ref = f32[3,768]{1,0:T(4,128)S(1)} collective-permute-done((f32[3,768]{1,0:T(4,128)S(1)}, f32[3,768]{1,0:T(4,128)S(1)}, u32[]{:S(2)}, u32[]{:S(2)}) %collective-permute-start) | collective-permute-done | bytes 9248 | tf_op jit(solution)/shard_map/ppermute | solution.py:371
  59.5 0.0 copy-done
  59.6 0.0 copy-done.2
  59.6 0.6 copy-done.3
  60.1 2.8 %stencil.1 = (f32[2,64,720]{2,1,0:T(8,128)}, f32[64,720]{1,0:T(8,128)}, f32[64,720]{1,0:T(8,128)}) custom-call(s32[1]{0:T(128)} %bitcast.even_ref, f32[32,8,768]{2,1,0:T(8,128)} %copy-done, f32[3,768]{1,0:T(4,128)} %copy-done.3, f32[3,768]{1,0:T(4,128)} %copy-done.2, f32[64,128]{1,0:T(8,128)} %pad.4.coef_ref), custom_call_target="tpu_custom_call" | custom-call | tf_op jit(solution)/shard_map/stencil/pallas_call | solution.py:321
  (11 shorter events, 0.1 us)
Async XLA Ops:
  2.8 24.7 %all-to-all-start = ((f32[32,8,720]{2,1,0:T(8,128)}), f32[32,8,720]{2,1,0:T(8,128)S(1)}, u32[]{:S(2)}, u32[]{:S(2)}) async-start(f32[32,8,720]{2,1,0:T(8,128)} %maximum_bitcast_fusion), calls=%async_computation | async-start | bytes 1572864 | tf_op jit(solution)/shard_map/all_to_all | solution.py:345
  13.2 0.7 %copy-start.5 = (s32[64]{0:T(128)S(1)}, s32[64]{0:T(128)}, u32[]{:S(2)}) copy-start(s32[64]{0:T(128)} %param.11) | copy-start | bytes 772
  13.9 0.7 %copy-start.4 = (f32[64]{0:T(128)S(1)}, f32[64]{0:T(128)}, u32[]{:S(2)}) copy-start(f32[64]{0:T(128)} %param.12) | copy-start | bytes 772
  27.5 0.9 %copy-start.1 = (f32[32,8,720]{2,1,0:T(8,128)}, f32[32,8,720]{2,1,0:T(8,128)S(1)}, u32[]{:S(2)}) copy-start(f32[32,8,720]{2,1,0:T(8,128)S(1)} %all-to-all-done.x_ref) | copy-start | bytes 2211844
  33.9 18.0 %all-to-all-start.1 = ((f32[32,8,768]{2,1,0:T(8,128)}), f32[32,8,768]{2,1,0:T(8,128)S(1)}, u32[]{:S(2)}, u32[]{:S(2)}) async-start(f32[32,8,768]{2,1,0:T(8,128)} %polar_filter.1), calls=%async_computation.1 | async-start | bytes 1572864 | tf_op jit(solution)/shard_map/all_to_all | solution.py:356
  51.9 7.6 %copy-start = (f32[32,8,768]{2,1,0:T(8,128)}, f32[32,8,768]{2,1,0:T(8,128)S(1)}, u32[]{:S(2)}) copy-start(f32[32,8,768]{2,1,0:T(8,128)S(1)} %all-to-all-done.1.field_ref) | copy-start | bytes 2359300
  52.0 6.0 %collective-permute-start.1 = (f32[3,768]{1,0:T(4,128)S(1)}, f32[3,768]{1,0:T(4,128)S(1)}, u32[]{:S(2)}, u32[]{:S(2)}) collective-permute-start(f32[3,768]{1,0:T(4,128)S(1)} %get-tuple-element.9), channel_id=1, source_target_pairs={{0,16},{1,17},{2,18},{3,19},{4,20},{5,21},{6,22},{7,23},{8,24},{9,... | collective-permute-start | bytes 27656 | tf_op jit(solution)/shard_map/ppermute | solution.py:372
  55.1 4.4 %collective-permute-start = (f32[3,768]{1,0:T(4,128)S(1)}, f32[3,768]{1,0:T(4,128)S(1)}, u32[]{:S(2)}, u32[]{:S(2)}) collective-permute-start(f32[3,768]{1,0:T(4,128)S(1)} %get-tuple-element.10), channel_id=1, source_target_pairs={{0,32},{1,33},{2,34},{3,35},{4,36},{5,37},{6,38},{7,39},{8,40},{9,... | collective-permute-start | bytes 27656 | tf_op jit(solution)/shard_map/ppermute | solution.py:371
  57.9 1.6 %copy-start.2 = (f32[3,768]{1,0:T(4,128)}, f32[3,768]{1,0:T(4,128)S(1)}, u32[]{:S(2)}) copy-start(f32[3,768]{1,0:T(4,128)S(1)} %collective-permute-done.1.second_ref) | copy-start | bytes 27652
  59.5 0.6 copy-start.3

commit v2 on v1

--- a/solution.py
+++ b/solution.py
@@ -14,6 +14,7 @@
 LANE = 128
 TILES = NLON * LEV // LANE
 STEP = LANE // LEV
+SMALL_GRANT = 12 << 20
 WIDE = 768
 
 
@@ -64,8 +65,35 @@
     return out
 
 
+def three(values, sign):
+    (ar, ai), (br, bi), (cr, ci) = values
+    tr, ti = br + cr, bi + ci
+    mr, mi = ar - np.float32(0.5) * tr, ai - np.float32(0.5) * ti
+    root = np.float32(sign * math.sqrt(0.75))
+    er, ei = root * (br - cr), root * (bi - ci)
+    return [(ar + tr, ai + ti), (mr - ei, mi + er), (mr + ei, mi - er)]
+
+
+def nine(values, sign):
+    inner = [three([values[n], values[n + 3], values[n + 6]], sign) for n in range(3)]
+    out = [None] * 9
+    for k in range(3):
+        column = [inner[0][k]]
+        for n in (1, 2):
+            re, im = inner[n][k]
+            if k:
+                c = np.float32(math.cos(2.0 * math.pi * n * k / 9))
+                s = np.float32(sign * math.sin(2.0 * math.pi * n * k / 9))
+                re, im = re * c - im * s, re * s + im * c
+            column.append((re, im))
+        out[k], out[k + 3], out[k + 6] = three(column, sign)
+    return out
+
+
 def odd_complex(values, sign):
     size = len(values)
+    if size == 9:
+        return nine(values, sign)
     half, angle = _odd_tables(size)
     out = [None] * size
     plus = [(values[j][0] + values[size - j][0], values[j][1] + values[size - j][1]) for j in range(1, half + 1)]
@@ -133,17 +161,50 @@
     cosines = np.cos(angle) * same
     sines = np.sin(angle) * same
     forward = np.block([[cosines, -sines], [sines, cosines]]).astype(np.float32)
-    return rows, forward, forward.T.copy()
-
-
-GROUP = 13
+
+    def split(matrix):
+        high = matrix.astype(jnp.bfloat16)
+        low = (matrix - high.astype(np.float32)).astype(jnp.bfloat16)
+        return np.concatenate([high, high, low], axis=0)
+
+    return rows, split(forward), split(forward.T)
+
+
+def split_dot(value, matrix):
+    high = value.astype(jnp.bfloat16)
+    low = (value - high.astype(jnp.float32)).astype(jnp.bfloat16)
+    return jnp.dot(jnp.concatenate([high, low, high], axis=1), matrix, preferred_element_type=jnp.float32)
+
+
+GROUP = 91
 
 
 def filter_kernel(x_ref, cut_ref, rows_ref, forward_ref, inverse_ref, out_ref, full, mid, stage):
     sectors = x_ref.shape[0]
     span = x_ref.shape[2]
-    for d in range(sectors):
-        full[:, LANE + d * span : LANE + (d + 1) * span] = x_ref[d]
+    lane = lax.broadcasted_iota(jnp.int32, (8, LANE), 1)
+    turned = {}
+
+    def source(d, t):
+        if (d, t) not in turned:
+            value = x_ref[d, :, LANE * t : min(LANE * (t + 1), span)]
+            if value.shape[1] < LANE:
+                value = jnp.concatenate([value, jnp.zeros((8, LANE - value.shape[1]), jnp.float32)], axis=1)
+            shift = d * span % LANE
+            turned[(d, t)] = pltpu.roll(value, shift, 1) if shift else value
+        return turned[(d, t)]
+
+    for p in range(TILES):
+        edges = []
+        for j in range(0, LANE, LEV):
+            d, rest = divmod(LANE * p + j, span)
+            key = (d, rest // LANE)
+            if not edges or edges[-1][1:] != key:
+                edges.append((j,) + key)
+        value = source(*edges[-1][1:])
+        for (_, d, t), (stop, _, _) in reversed(list(zip(edges[:-1], edges[1:]))):
+            value = jnp.where(lane < stop, source(d, t), value)
+        full[:, LANE * (p + 1) : LANE * (p + 2)] = value
 
     def tile(p):
         return slice(LANE * (p + 1), LANE * (p + 2))
@@ -185,13 +246,11 @@
         for gamma, value in enumerate(odd_complex([(mid[row, c], mid[row + 1, c]) for c in range(9)], -1)):
             put(SLOT[(key[0], key[1], gamma)], value)
 
-    cut = cut_ref[0]
-    gain = cut_ref[1]
+    cut = jnp.broadcast_to(cut_ref[:, 0:1], (8, LANE))
+    gain = jnp.broadcast_to(cut_ref[:, 1:2], (8, LANE))
     for start in range(0, COUNT, GROUP):
         where = slice(8 * start, 8 * (start + GROUP))
-        spectrum = jnp.dot(
-            stage[where, :], forward_ref[...], precision=lax.Precision.HIGHEST, preferred_element_type=jnp.float32
-        )
+        spectrum = split_dot(stage[where, :], forward_ref[...])
         scaled = []
         for index in range(GROUP):
             slot = start + index
@@ -200,12 +259,7 @@
             factor = jnp.where(wave > cut, gain * decay, np.float32(1.0 / NLON))
             part = spectrum[8 * index : 8 * index + 8, :]
             scaled.append(part * jnp.concatenate([factor, factor], axis=1))
-        stage[where, :] = jnp.dot(
-            jnp.concatenate(scaled, axis=0),
-            inverse_ref[...],
-            precision=lax.Precision.HIGHEST,
-            preferred_element_type=jnp.float32,
-        )
+        stage[where, :] = split_dot(jnp.concatenate(scaled, axis=0), inverse_ref[...])
 
     def take(slot, real):
         cos_row = rows_ref[0, slot : slot + 1, :]
@@ -248,10 +302,17 @@
                     full[:, tile(-1)] = values[a]
 
     for d in range(sectors):
-        first = LANE + d * span
-        out_ref[d, :, 0 : span + LEV] = full[:, first : first + span + LEV]
-        out_ref[d, :, span + LEV : WIDE - LEV] = jnp.zeros((8, WIDE - span - 2 * LEV), jnp.float32)
-        out_ref[d, :, WIDE - LEV : WIDE] = full[:, first - LEV : first]
+        first, shift = divmod(LANE + d * span, LANE)
+        pieces = []
+        for t in range(span // LANE + 2):
+            piece = full[:, LANE * (first + t) : LANE * (first + t + 1)]
+            pieces.append(pltpu.roll(piece, LANE - shift, 1) if shift else piece)
+        west = pieces[0] if shift else full[:, LANE * (first - 1) : LANE * first]
+        for t in range(WIDE // LANE):
+            value = jnp.where(lane < LANE - shift, pieces[t], pieces[t + 1]) if shift else pieces[t]
+            if t == WIDE // LANE - 1:
+                value = jnp.where(lane < LANE - LEV, value, west)
+            out_ref[d, :, LANE * t : LANE * (t + 1)] = value
 
 
 def filter_rows(blocks, cuts):
@@ -266,8 +327,52 @@
             pltpu.VMEM((20, 9, 8, LANE), jnp.float32),
             pltpu.VMEM((8 * COUNT, 2 * LANE), jnp.float32),
         ],
+        compiler_params=pltpu.CompilerParams(vmem_limit_bytes=SMALL_GRANT),
         name="polar_filter",
     )(blocks, cuts, jnp.asarray(rows), jnp.asarray(forward), jnp.asarray(inverse))
+
+
+def pack_kernel(pieces, winds_ref, layer_ref, tracer_ref, out_ref, buffer, in_sem, out_sem):
+    blocks = layer_ref.shape[0]
+    sources = [(winds_ref, 2 * blocks, 0), (layer_ref, blocks, 2 * blocks), (tracer_ref, blocks, 3 * blocks)]
+    size = 4 * blocks // pieces
+    inward, outward = [], []
+    for ref, count, base in sources:
+        for start in range(0, count, size):
+            index = (base + start) // size
+            here = slice(base + start, base + start + size)
+            inward.append(pltpu.make_async_copy(ref.at[start : start + size], buffer.at[here], in_sem.at[index]))
+            outward.append(pltpu.make_async_copy(buffer.at[here], out_ref.at[here], out_sem.at[index]))
+    for copy in inward:
+        copy.start()
+    for first, then in zip(inward, outward):
+        first.wait()
+        then.start()
+    for copy in outward:
+        copy.wait()
+
+
+def pack(winds, thickness, tracer):
+    row_count, width = thickness.shape
+    blocks = row_count // 8
+    pieces = 4
+    anywhere = pl.BlockSpec(memory_space=pl.ANY)
+    return pl.pallas_call(
+        functools.partial(pack_kernel, pieces),
+        out_shape=jax.ShapeDtypeStruct((4 * blocks, 8, width), jnp.float32),
+        in_specs=[anywhere, anywhere, anywhere],
+        out_specs=anywhere,
+        scratch_shapes=[
+            pltpu.VMEM((4 * blocks, 8, width), jnp.float32),
+            pltpu.SemaphoreType.DMA((pieces,)),
+            pltpu.SemaphoreType.DMA((pieces,)),
+        ],
+        name="pack",
+    )(
+        winds.reshape(2 * blocks, 8, width),
+        thickness.reshape(blocks, 8, width),
+        tracer.reshape(blocks, 8, width),
+    )
 
 
 def stencil_kernel(ratio, even_ref, field_ref, first_ref, second_ref, coef_ref, winds_ref, layer_ref, tracer_ref, tall):
@@ -328,6 +433,7 @@
         in_specs=[pl.BlockSpec(memory_space=pltpu.SMEM), vmem, vmem, vmem, vmem],
         out_specs=(vmem, vmem, vmem),
         scratch_shapes=[pltpu.VMEM((3, row_count + 16, WIDE), jnp.float32)],
+        compiler_params=pltpu.CompilerParams(vmem_limit_bytes=SMALL_GRANT),
         name="stencil",
     )(even, fields, first, second, coef)
 
@@ -340,8 +446,7 @@
     row_count, width = thickness.shape
     nlat = row_count * lat_size
 
-    flat = jnp.concatenate([winds.reshape(2 * row_count, width), thickness, tracer], axis=0)
-    blocks = flat.reshape(lon_size, 4 * row_count // lon_size, width)
+    blocks = pack(winds, thickness, tracer)
     owned = lax.all_to_all(blocks, "lon", split_axis=0, concat_axis=0, tiled=True)
 
     is_polar = (band < lat_size // 4) | (band >= lat_size - lat_size // 4)
@@ -350,7 +455,7 @@
     damp = lax.dynamic_slice_in_dim(damping, group * 8, 8)
     gain = damp * cut * cut
     cut = jnp.where(is_polar, cut, jnp.float32(NLON))
-    cuts = jnp.broadcast_to(jnp.stack([cut, gain])[:, :, None], (2, 8, LANE))
+    cuts = jnp.stack([cut, gain], axis=1)
 
     filtered = filter_rows(owned, cuts)
     fields = lax.all_to_all(filtered, "lon", split_axis=0, concat_axis=0, tiled=True)
@@ -384,7 +489,6 @@
     coef = jnp.stack(
         [quarter, aspect * quarter * cos_face[1:], aspect * quarter * cos_face[:-1], 2.0 * quarter], axis=1
     )
-    coef = jnp.pad(coef, ((0, 0), (0, LANE - 4)))
     return stencil(
         even.astype(jnp.int32)[None], fields, first, second, coef, lon_step / (2.0 * lat_step), row_count, width
     )

time: 63.4 us -> 58.1 us (0.916)
  other arithmetic: 2.44 us -> 0.29 us
  local copies, waits for them, and re-layouts: 3.54 us -> 1.52 us
  Pallas kernels: 8.3 us -> 6.5 us
    pallas_call x1, Pallas kernels: 5.51 us -> 2.89 us  [filter_rows(): pl.pallas_call(filter_kernel, out_shape=jax.ShapeDtypeStruct((blocks.shap...]
    reshape x1 -> x0, other arithmetic: 2.15 us -> none  [per_device(): blocks = flat.reshape(lon_size, 4 * row_count // lon_size, width)]
    pallas_call x0 -> x1, Pallas kernels: none -> 1.97 us  [pack(): pl.pallas_call(functools.partial(pack_kernel, pieces), out_shape=jax.Shap...]
    pallas_call x1, Pallas kernels: 2.79 us -> 1.64 us  [stencil(): pl.pallas_call(functools.partial(stencil_kernel, ratio), out_shape=(jax.S...]
    broadcast_in_dim x1 -> x0, local copies, waits for them, and re-layouts: 0.76 us -> none  [per_device(): cuts = jnp.broadcast_to(jnp.stack([cut, gain])[:, :, None], (2, 8, LANE))]
    unnamed x12 -> x10, local copies, waits for them, and re-layouts: 2.04 us -> 1.32 us
  transfers between devices with their start and end apart: 4 -> 4, of which waited for: 3 -> 4; matrix products, arithmetic and copies ran while one was open for 2% -> 1% of each run, Pallas kernels for 0% -> 0%
where the time goes in v2:
time: 58.1 us; the launch traced here: 57.7 us
  waiting for transfers between devices  29.1 us (50%)
  starting transfers between devices  19.5 us (34%)
  Pallas kernels  6.5 us (11%)
  local copies, waits for them, and re-layouts  1.52 us (3%)
  between operations  0.77 us (1%)
    all_to_all x1, waiting for transfers between devices, per_device(): lax.all_to_all(filtered, 'lon', split_axis=0, concat_axis=0, tiled=True)  14.1 us
    all_to_all x1, waiting for transfers between devices, per_device(): lax.all_to_all(blocks, 'lon', split_axis=0, concat_axis=0, tiled=True)  12.8 us
    all_to_all x1, starting transfers between devices, per_device(): lax.all_to_all(blocks, 'lon', split_axis=0, concat_axis=0, tiled=True)  10.5 us
    all_to_all x1, starting transfers between devices, per_device(): lax.all_to_all(filtered, 'lon', split_axis=0, concat_axis=0, tiled=True)  3.75 us
    ppermute x1, starting transfers between devices, per_device(): second = lax.ppermute(jnp.where(even, low, high), ('lat', 'lon'), pairs[1])  3.11 us
    pallas_call x1, Pallas kernels, filter_rows(): pl.pallas_call(filter_kernel, out_shape=jax.ShapeDtypeStruct((blocks.shap...  2.89 us
    ppermute x1, starting transfers between devices, per_device(): first = lax.ppermute(jnp.where(even, high, low), ('lat', 'lon'), pairs[0])  2.08 us
    pallas_call x1, Pallas kernels, pack(): pl.pallas_call(functools.partial(pack_kernel, pieces), out_shape=jax.Shap...  1.97 us
  transfers between devices with their start and end apart: 4, of which 4 were waited for; matrix products, arithmetic and copies ran while one was open for 1% of the time, Pallas kernels for 0%

profile of v2, /device:TPU:1, one launch (start us, length us, event | category | flops | bytes accessed | tf_op | source)
XLA Modules:
  0.0 57.7 jit_solution(8676972858491748095)
XLA Ops:
  0.6 2.0 %pack.1 = f32[32,8,720]{2,1,0:T(8,128)} custom-call(f32[16,8,720]{2,1,0:T(8,128)} %bitcast.24, f32[8,8,720]{2,1,0:T(8,128)} %bitcast.25, f32[8,8,720]{2,1,0:T(8,128)} %bitcast.26), custom_call_target="tpu_custom_call" | custom-call | tf_op jit(solution)/shard_map/pack/pallas_call | solution.py:360
  2.6 0.0 copy-start
  2.6 0.0 copy-start.1
  2.6 0.0 copy-start.2
  2.6 10.5 %all-to-all-start = ((f32[32,8,720]{2,1,0:T(8,128)}), f32[32,8,720]{2,1,0:T(8,128)S(1)}, u32[]{:S(2)}, u32[]{:S(2)}) async-start(f32[32,8,720]{2,1,0:T(8,128)} %pack.1), calls=%async_computation | async-start | bytes 1572864 | tf_op jit(solution)/shard_map/all_to_all | solution.py:450
  13.2 0.0 copy-start.4
  13.2 0.6 %copy-done.4 = s32[64]{0:T(128)S(1)} copy-done((s32[64]{0:T(128)S(1)}, s32[64]{0:T(128)}, u32[]{:S(2)}) %copy-start.4) | copy-done | bytes 280
  13.9 0.7 %copy-done.3 = f32[64]{0:T(128)S(1)} copy-done((f32[64]{0:T(128)S(1)}, f32[64]{0:T(128)}, u32[]{:S(2)}) %copy-start.3) | copy-done | bytes 280
  14.5 0.1 fusion.3
  14.6 0.1 copy.15.cut_ref
  14.7 12.8 %all-to-all-done.x_ref = f32[32,8,720]{2,1,0:T(8,128)S(1)} async-done(((f32[32,8,720]{2,1,0:T(8,128)}), f32[32,8,720]{2,1,0:T(8,128)S(1)}, u32[]{:S(2)}, u32[]{:S(2)}) %all-to-all-start) | async-done | bytes 737312 | tf_op jit(solution)/shard_map/all_to_all | solution.py:450
  27.5 0.0 copy-done
  27.5 0.0 copy-done.1
  27.5 2.9 %polar_filter.1 = f32[32,8,768]{2,1,0:T(8,128)} custom-call(f32[32,8,720]{2,1,0:T(8,128)S(1)} %all-to-all-done.x_ref, f32[8,2]{1,0:T(8,128)S(1)} %copy.15.cut_ref, f32[4,91,128]{2,1,0:T(8,128)S(1)} %copy-done.2, bf16[768,256]{1,0:T(8,128)(2,1)S(1)} %copy-done.1, bf16[768,256]{1,0:T(8,128)(2,1)S(1)} %copy-done), custom_call_target="tpu_custom_call" | custom-call | tf_op jit(solution)/shard_map/polar_filter/pallas_call | solution.py:320
  30.4 3.8 %all-to-all-start.1 = ((f32[32,8,768]{2,1,0:T(8,128)}), f32[32,8,768]{2,1,0:T(8,128)S(1)}, u32[]{:S(2)}, u32[]{:S(2)}) async-start(f32[32,8,768]{2,1,0:T(8,128)} %polar_filter.1), calls=%async_computation.1 | async-start | bytes 1572864 | tf_op jit(solution)/shard_map/all_to_all | solution.py:461
  34.3 0.1 cosine_divide_fusion
  34.3 0.1 multiply_bitcast_fusion.1
  34.4 14.1 %all-to-all-done.1.field_ref = f32[32,8,768]{2,1,0:T(8,128)S(1)} async-done(((f32[32,8,768]{2,1,0:T(8,128)}), f32[32,8,768]{2,1,0:T(8,128)S(1)}, u32[]{:S(2)}, u32[]{:S(2)}) %all-to-all-start.1) | async-done | bytes 786464 | tf_op jit(solution)/shard_map/all_to_all | solution.py:461
  48.5 3.1 %collective-permute-start.1 = (f32[3,768]{1,0:T(4,128)S(1)}, f32[3,768]{1,0:T(4,128)S(1)}, u32[]{:S(2)}, u32[]{:S(2)}) collective-permute-start(f32[3,768]{1,0:T(4,128)S(1)} %get-tuple-element.9), channel_id=1, source_target_pairs={{0,16},{1,17},{2,18},{3,19},{4,20},{5,21},{6,22},{7,23},{8,24},{9,... | collective-permute-start | bytes 27656 | tf_op jit(solution)/shard_map/ppermute | solution.py:477
  51.6 2.1 %collective-permute-start = (f32[3,768]{1,0:T(4,128)S(1)}, f32[3,768]{1,0:T(4,128)S(1)}, u32[]{:S(2)}, u32[]{:S(2)}) collective-permute-start(f32[3,768]{1,0:T(4,128)S(1)} %get-tuple-element.10), channel_id=1, source_target_pairs={{0,32},{1,33},{2,34},{3,35},{4,36},{5,37},{6,38},{7,39},{8,40},{9,... | collective-permute-start | bytes 27656 | tf_op jit(solution)/shard_map/ppermute | solution.py:476
  53.7 0.1 copy.16.coef_ref
  53.8 0.6 %collective-permute-done.1.second_ref = f32[3,768]{1,0:T(4,128)S(1)} collective-permute-done((f32[3,768]{1,0:T(4,128)S(1)}, f32[3,768]{1,0:T(4,128)S(1)}, u32[]{:S(2)}, u32[]{:S(2)}) %collective-permute-start.1) | collective-permute-done | bytes 9248 | tf_op jit(solution)/shard_map/ppermute | solution.py:477
  54.4 1.6 %collective-permute-done.first_ref = f32[3,768]{1,0:T(4,128)S(1)} collective-permute-done((f32[3,768]{1,0:T(4,128)S(1)}, f32[3,768]{1,0:T(4,128)S(1)}, u32[]{:S(2)}, u32[]{:S(2)}) %collective-permute-start) | collective-permute-done | bytes 9248 | tf_op jit(solution)/shard_map/ppermute | solution.py:476
  56.0 1.6 %stencil.1 = (f32[2,64,720]{2,1,0:T(8,128)}, f32[64,720]{1,0:T(8,128)}, f32[64,720]{1,0:T(8,128)}) custom-call(s32[1]{0:T(128)} %bitcast.even_ref, f32[32,8,768]{2,1,0:T(8,128)S(1)} %all-to-all-done.1.field_ref, f32[3,768]{1,0:T(4,128)S(1)} %collective-permute-done.first_ref, f32[3,768]{1,0:T(4,128)S(1)} %collective-permute-done.1.second_ref, ...), custom_call_target="tpu_custom_call" | custom-call | tf_op jit(solution)/shard_map/stencil/pallas_call | solution.py:426
  (8 shorter events, 0.1 us)
Async XLA Ops:
  2.6 24.9 %copy-start = (bf16[768,256]{1,0:T(8,128)(2,1)S(1)}, bf16[768,256]{1,0:T(8,128)(2,1)}, u32[]{:S(2)}) copy-start(bf16[768,256]{1,0:T(8,128)(2,1)} %constant.68.clone.inverse_ref) | copy-start | bytes 1179652
  2.6 24.9 %copy-start.1 = (bf16[768,256]{1,0:T(8,128)(2,1)S(1)}, bf16[768,256]{1,0:T(8,128)(2,1)}, u32[]{:S(2)}) copy-start(bf16[768,256]{1,0:T(8,128)(2,1)} %constant.67.clone.forward_ref) | copy-start | bytes 1179652
  2.6 24.9 %copy-start.2 = (f32[4,91,128]{2,1,0:T(8,128)S(1)}, f32[4,91,128]{2,1,0:T(8,128)}, u32[]{:S(2)}) copy-start(f32[4,91,128]{2,1,0:T(8,128)} %constant.66.clone.rows_ref) | copy-start | bytes 559108
  2.6 24.9 %all-to-all-start = ((f32[32,8,720]{2,1,0:T(8,128)}), f32[32,8,720]{2,1,0:T(8,128)S(1)}, u32[]{:S(2)}, u32[]{:S(2)}) async-start(f32[32,8,720]{2,1,0:T(8,128)} %pack.1), calls=%async_computation | async-start | bytes 1572864 | tf_op jit(solution)/shard_map/all_to_all | solution.py:450
  13.2 0.7 %copy-start.4 = (s32[64]{0:T(128)S(1)}, s32[64]{0:T(128)}, u32[]{:S(2)}) copy-start(s32[64]{0:T(128)} %param.11) | copy-start | bytes 772
  13.9 0.7 %copy-start.3 = (f32[64]{0:T(128)S(1)}, f32[64]{0:T(128)}, u32[]{:S(2)}) copy-start(f32[64]{0:T(128)} %param.12) | copy-start | bytes 772
  30.4 18.0 %all-to-all-start.1 = ((f32[32,8,768]{2,1,0:T(8,128)}), f32[32,8,768]{2,1,0:T(8,128)S(1)}, u32[]{:S(2)}, u32[]{:S(2)}) async-start(f32[32,8,768]{2,1,0:T(8,128)} %polar_filter.1), calls=%async_computation.1 | async-start | bytes 1572864 | tf_op jit(solution)/shard_map/all_to_all | solution.py:461
  48.5 5.9 %collective-permute-start.1 = (f32[3,768]{1,0:T(4,128)S(1)}, f32[3,768]{1,0:T(4,128)S(1)}, u32[]{:S(2)}, u32[]{:S(2)}) collective-permute-start(f32[3,768]{1,0:T(4,128)S(1)} %get-tuple-element.9), channel_id=1, source_target_pairs={{0,16},{1,17},{2,18},{3,19},{4,20},{5,21},{6,22},{7,23},{8,24},{9,... | collective-permute-start | bytes 27656 | tf_op jit(solution)/shard_map/ppermute | solution.py:477
  51.6 4.4 %collective-permute-start = (f32[3,768]{1,0:T(4,128)S(1)}, f32[3,768]{1,0:T(4,128)S(1)}, u32[]{:S(2)}, u32[]{:S(2)}) collective-permute-start(f32[3,768]{1,0:T(4,128)S(1)} %get-tuple-element.10), channel_id=1, source_target_pairs={{0,32},{1,33},{2,34},{3,35},{4,36},{5,37},{6,38},{7,39},{8,40},{9,... | collective-permute-start | bytes 27656 | tf_op jit(solution)/shard_map/ppermute | solution.py:476

commit v3 on v2

--- a/solution.py
+++ b/solution.py
@@ -14,6 +14,7 @@
 LANE = 128
 TILES = NLON * LEV // LANE
 STEP = LANE // LEV
+BATCH = 4
 SMALL_GRANT = 12 << 20
 WIDE = 768
 
@@ -176,10 +177,12 @@
     return jnp.dot(jnp.concatenate([high, low, high], axis=1), matrix, preferred_element_type=jnp.float32)
 
 
-GROUP = 91
-
-
-def filter_kernel(x_ref, cut_ref, rows_ref, forward_ref, inverse_ref, out_ref, full, mid, stage):
+ALL_CLASSES = [(0, 0), (2, 0)] + COMPLEX_CLASSES
+CLASS_CUTS = (0, 4, 6, 8, 11)
+CLASS_GROUPS = [ALL_CLASSES[first:last] for first, last in zip(CLASS_CUTS[:-1], CLASS_CUTS[1:])]
+
+
+def filter_kernel(x_ref, cut_ref, rows_ref, forward_ref, inverse_ref, out_ref, full, mid, stage, result, sem):
     sectors = x_ref.shape[0]
     span = x_ref.shape[2]
     lane = lax.broadcasted_iota(jnp.int32, (8, LANE), 1)
@@ -239,28 +242,6 @@
             stage[where, :LANE] = value[0] * cos_row + value[1] * sin_row
             stage[where, LANE:] = value[1] * cos_row - value[0] * sin_row
 
-    for key, row in REAL_ROWS.items():
-        for gamma, value in enumerate(odd_real_forward([mid[row, c] for c in range(9)])):
-            put(SLOT[(key[0], key[1], gamma)], value)
-    for key, row in COMPLEX_ROWS.items():
-        for gamma, value in enumerate(odd_complex([(mid[row, c], mid[row + 1, c]) for c in range(9)], -1)):
-            put(SLOT[(key[0], key[1], gamma)], value)
-
-    cut = jnp.broadcast_to(cut_ref[:, 0:1], (8, LANE))
-    gain = jnp.broadcast_to(cut_ref[:, 1:2], (8, LANE))
-    for start in range(0, COUNT, GROUP):
-        where = slice(8 * start, 8 * (start + GROUP))
-        spectrum = split_dot(stage[where, :], forward_ref[...])
-        scaled = []
-        for index in range(GROUP):
-            slot = start + index
-            wave = rows_ref[2, slot : slot + 1, :]
-            decay = rows_ref[3, slot : slot + 1, :]
-            factor = jnp.where(wave > cut, gain * decay, np.float32(1.0 / NLON))
-            part = spectrum[8 * index : 8 * index + 8, :]
-            scaled.append(part * jnp.concatenate([factor, factor], axis=1))
-        stage[where, :] = split_dot(jnp.concatenate(scaled, axis=0), inverse_ref[...])
-
     def take(slot, real):
         cos_row = rows_ref[0, slot : slot + 1, :]
         sin_row = rows_ref[1, slot : slot + 1, :]
@@ -270,15 +251,43 @@
             return (re * cos_row - im * sin_row, None)
         return (re * cos_row - im * sin_row, im * cos_row + re * sin_row)
 
-    for key, row in REAL_ROWS.items():
-        values = odd_real_inverse([take(SLOT[(key[0], key[1], gamma)], gamma == 0) for gamma in range(5)])
-        for c in range(9):
-            mid[row, c] = values[c]
-    for key, row in COMPLEX_ROWS.items():
-        values = odd_complex([take(SLOT[(key[0], key[1], gamma)], False) for gamma in range(9)], 1)
-        for c in range(9):
-            mid[row, c] = values[c][0]
-            mid[row + 1, c] = values[c][1]
+    cut = jnp.broadcast_to(cut_ref[:, 0:1], (8, LANE))
+    gain = jnp.broadcast_to(cut_ref[:, 1:2], (8, LANE))
+    for classes in CLASS_GROUPS:
+        slots = [SLOT[key] for key in BINS if key[:2] in classes]
+        start, count = slots[0], len(slots)
+        for key in classes:
+            if key in REAL_ROWS:
+                row = REAL_ROWS[key]
+                values = odd_real_forward([mid[row, c] for c in range(9)])
+            else:
+                row = COMPLEX_ROWS[key]
+                values = odd_complex([(mid[row, c], mid[row + 1, c]) for c in range(9)], -1)
+            for gamma, value in enumerate(values):
+                put(SLOT[key + (gamma,)], value)
+        where = slice(8 * start, 8 * (start + count))
+        spectrum = split_dot(stage[where, :], forward_ref[...])
+        scaled = []
+        for index in range(count):
+            slot = start + index
+            wave = rows_ref[2, slot : slot + 1, :]
+            decay = rows_ref[3, slot : slot + 1, :]
+            factor = jnp.where(wave > cut, gain * decay, np.float32(1.0 / NLON))
+            part = spectrum[8 * index : 8 * index + 8, :]
+            scaled.append(part * jnp.concatenate([factor, factor], axis=1))
+        stage[where, :] = split_dot(jnp.concatenate(scaled, axis=0), inverse_ref[...])
+        for key in classes:
+            if key in REAL_ROWS:
+                row = REAL_ROWS[key]
+                values = odd_real_inverse([take(SLOT[key + (gamma,)], gamma == 0) for gamma in range(5)])
+                for c in range(9):
+                    mid[row, c] = values[c]
+            else:
+                row = COMPLEX_ROWS[key]
+                values = odd_complex([take(SLOT[key + (gamma,)], False) for gamma in range(9)], 1)
+                for c in range(9):
+                    mid[row, c] = values[c][0]
+                    mid[row + 1, c] = values[c][1]
 
     for c in range(9):
 
@@ -301,6 +310,7 @@
                 if p == TILES - 1:
                     full[:, tile(-1)] = values[a]
 
+    writes = []
     for d in range(sectors):
         first, shift = divmod(LANE + d * span, LANE)
         pieces = []
@@ -312,7 +322,13 @@
             value = jnp.where(lane < LANE - shift, pieces[t], pieces[t + 1]) if shift else pieces[t]
             if t == WIDE // LANE - 1:
                 value = jnp.where(lane < LANE - LEV, value, west)
-            out_ref[d, :, LANE * t : LANE * (t + 1)] = value
+            result[d, :, LANE * t : LANE * (t + 1)] = value
+        if d % BATCH == BATCH - 1:
+            here = slice(d + 1 - BATCH, d + 1)
+            writes.append(pltpu.make_async_copy(result.at[here], out_ref.at[here], sem.at[d // BATCH]))
+            writes[-1].start()
+    for write in writes:
+        write.wait()
 
 
 def filter_rows(blocks, cuts):
@@ -321,11 +337,13 @@
         filter_kernel,
         out_shape=jax.ShapeDtypeStruct((blocks.shape[0], 8, WIDE), jnp.float32),
         in_specs=[pl.BlockSpec(memory_space=pltpu.VMEM)] * 5,
-        out_specs=pl.BlockSpec(memory_space=pltpu.VMEM),
+        out_specs=pl.BlockSpec(memory_space=pl.ANY),
         scratch_shapes=[
             pltpu.VMEM((8, (TILES + 2) * LANE), jnp.float32),
             pltpu.VMEM((20, 9, 8, LANE), jnp.float32),
             pltpu.VMEM((8 * COUNT, 2 * LANE), jnp.float32),
+            pltpu.VMEM((blocks.shape[0], 8, WIDE), jnp.float32),
+            pltpu.SemaphoreType.DMA((blocks.shape[0] // BATCH,)),
         ],
         compiler_params=pltpu.CompilerParams(vmem_limit_bytes=SMALL_GRANT),
         name="polar_filter",
@@ -375,67 +393,122 @@
     )
 
 
-def stencil_kernel(ratio, even_ref, field_ref, first_ref, second_ref, coef_ref, winds_ref, layer_ref, tracer_ref, tall):
-    is_even = even_ref[0] > 0
-    first = first_ref[...]
-    second = second_ref[...]
-    south = jnp.where(is_even, second, first)
-    north = jnp.where(is_even, first, second)
-    for f in range(3):
-        tall[f, 7:8, :] = south[f : f + 1, :]
-        tall[f, 72:73, :] = north[f : f + 1, :]
-        for g in range(8):
-            tall[f, 8 + 8 * g : 16 + 8 * g, :] = field_ref[8 * (f + 1) + g]
-
-    def east(x):
-        return pltpu.roll(x, WIDE - LEV, 1)
-
-    def west(x):
-        return pltpu.roll(x, LEV, 1)
-
+def east(x):
+    return pltpu.roll(x, WIDE - LEV, 1)
+
+
+def west(x):
+    return pltpu.roll(x, LEV, 1)
+
+
+def update(ratio, u, mid_rows, south_rows, north_rows, coef):
+    v, h, q = mid_rows
+    v_s, h_s, q_s = south_rows
+    v_n, h_n, q_n = north_rows
+    zonal, to_north, to_south, slope = (coef[:, k : k + 1] for k in range(4))
+    h_e = east(h)
+    su = u + east(u)
+    fx = su * (h + h_e)
+    gx = su * (q + east(q))
+    wind_n = (v + v_n) * to_north
+    wind_s = (v_s + v) * to_south
+    new_h = h - (zonal * (fx - west(fx)) + (wind_n * (h + h_n) - wind_s * (h_s + h)))
+    new_q = q - (zonal * (gx - west(gx)) + (wind_n * (q + q_n) - wind_s * (q_s + q)))
+    new_v = v - np.float32(ratio) * (h_n - h_s)
+    return slope * (h_e - west(h)), new_v, new_h, new_q
+
+
+def main_kernel(ratio, field_ref, coef_ref, winds_ref, layer_ref, tracer_ref):
+    groups = field_ref.shape[0] // 4
     span = layer_ref.shape[1]
-    for g in range(8):
+    sub = lax.broadcasted_iota(jnp.int32, (8, WIDE), 0)
+
+    def shifted(f, g):
+        x = field_ref[groups * f + g]
+        below = field_ref[groups * f + max(g - 1, 0)]
+        above = field_ref[groups * f + min(g + 1, groups - 1)]
+        south = jnp.where(sub == 0, pltpu.roll(below, 1, 0), pltpu.roll(x, 1, 0))
+        north = jnp.where(sub == 7, pltpu.roll(above, 7, 0), pltpu.roll(x, 7, 0))
+        return x, south, north
+
+    for g in range(groups):
         rows = slice(8 * g, 8 * g + 8)
-        at = 8 + 8 * g
         u = field_ref[g]
-        v, h, q = (tall[f, at : at + 8, :] for f in range(3))
-        v_s, h_s, q_s = (tall[f, at - 1 : at + 7, :] for f in range(3))
-        v_n, h_n, q_n = (tall[f, at + 1 : at + 9, :] for f in range(3))
-        zonal = coef_ref[rows, 0:1]
-        to_north = coef_ref[rows, 1:2]
-        to_south = coef_ref[rows, 2:3]
-        slope = coef_ref[rows, 3:4]
-        h_e = east(h)
-        su = u + east(u)
-        fx = su * (h + h_e)
-        gx = su * (q + east(q))
-        wind_n = (v + v_n) * to_north
-        wind_s = (v_s + v) * to_south
-        new_h = h - (zonal * (fx - west(fx)) + (wind_n * (h + h_n) - wind_s * (h_s + h)))
-        new_q = q - (zonal * (gx - west(gx)) + (wind_n * (q + q_n) - wind_s * (q_s + q)))
-        new_u = u - slope * (h_e - west(h))
-        new_v = v - np.float32(ratio) * (h_n - h_s)
-        winds_ref[0, rows, :] = new_u[:, :span]
+        mid_rows, south_rows, north_rows = zip(*(shifted(f, g) for f in (1, 2, 3)))
+        du, new_v, new_h, new_q = update(ratio, u, mid_rows, south_rows, north_rows, coef_ref[rows, :])
+        winds_ref[0, rows, :] = (u - du)[:, :span]
         winds_ref[1, rows, :] = new_v[:, :span]
         layer_ref[rows, :] = new_h[:, :span]
         tracer_ref[rows, :] = new_q[:, :span]
 
 
-def stencil(even, fields, first, second, coef, ratio, row_count, width):
+def edge_kernel(
+    ratio, even_ref, field_ref, first_ref, second_ref, coef_ref, w_in, l_in, t_in, winds_ref, layer_ref, tracer_ref, out, sem
+):
+    del w_in, l_in, t_in
+    groups = field_ref.shape[0] // 4
+    is_even = even_ref[0] > 0
+    span = layer_ref.shape[1]
+    sub = lax.broadcasted_iota(jnp.int32, (8, WIDE), 0)
+    writes = []
+    for side, g in enumerate((0, groups - 1)):
+        rows = slice(8 * g, 8 * g + 8)
+        near, far = (second_ref, first_ref) if side == 0 else (first_ref, second_ref)
+        mid_rows, south_rows, north_rows = [], [], []
+        for f in (1, 2, 3):
+            x = field_ref[groups * f + g]
+            halo = jnp.where(is_even, near[f - 1 : f, :], far[f - 1 : f, :])
+            if side == 0:
+                south = jnp.where(sub == 0, halo, pltpu.roll(x, 1, 0))
+                north = jnp.where(sub == 7, pltpu.roll(field_ref[groups * f + g + 1], 7, 0), pltpu.roll(x, 7, 0))
+            else:
+                south = jnp.where(sub == 0, pltpu.roll(field_ref[groups * f + g - 1], 1, 0), pltpu.roll(x, 1, 0))
+                north = jnp.where(sub == 7, halo, pltpu.roll(x, 7, 0))
+            mid_rows.append(x)
+            south_rows.append(south)
+            north_rows.append(north)
+        _, new_v, new_h, new_q = update(ratio, field_ref[g], mid_rows, south_rows, north_rows, coef_ref[rows, :])
+        for k, (value, target) in enumerate(
+            ((new_v, winds_ref.at[1, rows]), (new_h, layer_ref.at[rows]), (new_q, tracer_ref.at[rows]))
+        ):
+            out[side, k] = value[:, :span]
+            writes.append(pltpu.make_async_copy(out.at[side, k], target, sem.at[side, k]))
+            writes[-1].start()
+    for write in writes:
+        write.wait()
+
+
+def stencil_main(fields, coef, ratio, row_count, width):
     vmem = pl.BlockSpec(memory_space=pltpu.VMEM)
     return pl.pallas_call(
-        functools.partial(stencil_kernel, ratio),
+        functools.partial(main_kernel, ratio),
         out_shape=(
             jax.ShapeDtypeStruct((2, row_count, width), jnp.float32),
             jax.ShapeDtypeStruct((row_count, width), jnp.float32),
             jax.ShapeDtypeStruct((row_count, width), jnp.float32),
         ),
-        in_specs=[pl.BlockSpec(memory_space=pltpu.SMEM), vmem, vmem, vmem, vmem],
+        in_specs=[vmem, vmem],
         out_specs=(vmem, vmem, vmem),
-        scratch_shapes=[pltpu.VMEM((3, row_count + 16, WIDE), jnp.float32)],
         compiler_params=pltpu.CompilerParams(vmem_limit_bytes=SMALL_GRANT),
-        name="stencil",
-    )(even, fields, first, second, coef)
+        cost_estimate=pl.CostEstimate(flops=10_000_000, bytes_accessed=1_600_000, transcendentals=0),
+        name="stencil_main",
+    )(fields, coef)
+
+
+def stencil_edge(even, fields, first, second, coef, outs, ratio):
+    vmem = pl.BlockSpec(memory_space=pltpu.VMEM)
+    anywhere = pl.BlockSpec(memory_space=pl.ANY)
+    width = outs[1].shape[1]
+    return pl.pallas_call(
+        functools.partial(edge_kernel, ratio),
+        out_shape=tuple(jax.ShapeDtypeStruct(out.shape, jnp.float32) for out in outs),
+        in_specs=[pl.BlockSpec(memory_space=pltpu.SMEM), vmem, vmem, vmem, vmem, anywhere, anywhere, anywhere],
+        out_specs=(anywhere, anywhere, anywhere),
+        scratch_shapes=[pltpu.VMEM((2, 3, 8, width), jnp.float32), pltpu.SemaphoreType.DMA((2, 3))],
+        input_output_aliases={5: 0, 6: 1, 7: 2},
+        compiler_params=pltpu.CompilerParams(vmem_limit_bytes=SMALL_GRANT),
+        name="stencil_edge",
+    )(even, fields, first, second, coef, *outs)
 
 
 def per_device(winds, thickness, tracer, cutoff, damping):
@@ -489,9 +562,9 @@
     coef = jnp.stack(
         [quarter, aspect * quarter * cos_face[1:], aspect * quarter * cos_face[:-1], 2.0 * quarter], axis=1
     )
-    return stencil(
-        even.astype(jnp.int32)[None], fields, first, second, coef, lon_step / (2.0 * lat_step), row_count, width
-    )
+    ratio = lon_step / (2.0 * lat_step)
+    outs = stencil_main(fields, coef, ratio, row_count, width)
+    return stencil_edge(even.astype(jnp.int32)[None], fields, first, second, coef, outs, ratio)
 
 
 def solution(mesh):

time: 58.1 us -> 57 us (0.981)
  waiting for transfers between devices: 29.1 us -> 27.5 us
    ppermute x1, waiting for transfers between devices: 1.62 us -> 0.62 us  [per_device(): first = lax.ppermute(jnp.where(even, high, low), ('lat', 'lon'), pairs[0])]
    pallas_call x1 -> x2, Pallas kernels: 1.64 us -> 2.46 us  [the longest x1 1.61 us: stencil_main(): pl.pallas_call(functools.partial(main_kernel, ratio), out_shape=(jax.Shap...]
    ppermute x1, waiting for transfers between devices: 0.62 us -> 0.01 us  [per_device(): second = lax.ppermute(jnp.where(even, low, high), ('lat', 'lon'), pairs[1])]
  transfers between devices with their start and end apart: 4 -> 4, of which waited for: 4 -> 3; matrix products, arithmetic and copies ran while one was open for 1% -> 1% of each run, Pallas kernels for 0% -> 3%
where the time goes in v3:
time: 57 us; the launch traced here: 56.6 us
  waiting for transfers between devices  27.5 us (48%)
  starting transfers between devices  19.5 us (34%)
  Pallas kernels  7.01 us (12%)
  local copies, waits for them, and re-layouts  1.52 us (3%)
  between operations  0.78 us (1%)
    all_to_all x1, waiting for transfers between devices, per_device(): lax.all_to_all(filtered, 'lon', split_axis=0, concat_axis=0, tiled=True)  14.1 us
    all_to_all x1, waiting for transfers between devices, per_device(): lax.all_to_all(blocks, 'lon', split_axis=0, concat_axis=0, tiled=True)  12.8 us
    all_to_all x1, starting transfers between devices, per_device(): lax.all_to_all(blocks, 'lon', split_axis=0, concat_axis=0, tiled=True)  10.5 us
    all_to_all x1, starting transfers between devices, per_device(): lax.all_to_all(filtered, 'lon', split_axis=0, concat_axis=0, tiled=True)  3.77 us
    ppermute x1, starting transfers between devices, per_device(): second = lax.ppermute(jnp.where(even, low, high), ('lat', 'lon'), pairs[1])  3.11 us
    pallas_call x1, Pallas kernels, filter_rows(): pl.pallas_call(filter_kernel, out_shape=jax.ShapeDtypeStruct((blocks.shap...  2.59 us
    ppermute x1, starting transfers between devices, per_device(): first = lax.ppermute(jnp.where(even, high, low), ('lat', 'lon'), pairs[0])  2.08 us
    pallas_call x1, Pallas kernels, pack(): pl.pallas_call(functools.partial(pack_kernel, pieces), out_shape=jax.Shap...  1.96 us
  transfers between devices with their start and end apart: 4, of which 3 were waited for; matrix products, arithmetic and copies ran while one was open for 1% of the time, Pallas kernels for 3%

profile of v3, /device:TPU:1, one launch (start us, length us, event | category | flops | bytes accessed | tf_op | source)
XLA Modules:
  0.0 56.6 jit_solution(10776871032165971462)
XLA Ops:
  0.6 2.0 %pack.1 = f32[32,8,720]{2,1,0:T(8,128)} custom-call(f32[16,8,720]{2,1,0:T(8,128)} %bitcast.24, f32[8,8,720]{2,1,0:T(8,128)} %bitcast.25, f32[8,8,720]{2,1,0:T(8,128)} %bitcast.26), custom_call_target="tpu_custom_call" | custom-call | tf_op jit(solution)/shard_map/pack/pallas_call | solution.py:378
  2.6 0.0 copy-start
  2.6 0.0 copy-start.1
  2.6 0.0 copy-start.2
  2.6 10.5 %all-to-all-start = ((f32[32,8,720]{2,1,0:T(8,128)}), f32[32,8,720]{2,1,0:T(8,128)S(1)}, u32[]{:S(2)}, u32[]{:S(2)}) async-start(f32[32,8,720]{2,1,0:T(8,128)} %pack.1), calls=%async_computation | async-start | bytes 1572864 | tf_op jit(solution)/shard_map/all_to_all | solution.py:523
  13.2 0.0 copy-start.4
  13.2 0.6 %copy-done.4 = s32[64]{0:T(128)S(1)} copy-done((s32[64]{0:T(128)S(1)}, s32[64]{0:T(128)}, u32[]{:S(2)}) %copy-start.4) | copy-done | bytes 280
  13.9 0.7 %copy-done.3 = f32[64]{0:T(128)S(1)} copy-done((f32[64]{0:T(128)S(1)}, f32[64]{0:T(128)}, u32[]{:S(2)}) %copy-start.3) | copy-done | bytes 280
  14.5 0.1 fusion.3
  14.6 0.1 copy.18.cut_ref
  14.7 12.8 %all-to-all-done.x_ref = f32[32,8,720]{2,1,0:T(8,128)S(1)} async-done(((f32[32,8,720]{2,1,0:T(8,128)}), f32[32,8,720]{2,1,0:T(8,128)S(1)}, u32[]{:S(2)}, u32[]{:S(2)}) %all-to-all-start) | async-done | bytes 737312 | tf_op jit(solution)/shard_map/all_to_all | solution.py:523
  27.5 0.0 copy-done.1
  27.5 2.6 %polar_filter.1 = f32[32,8,768]{2,1,0:T(8,128)} custom-call(f32[32,8,720]{2,1,0:T(8,128)S(1)} %all-to-all-done.x_ref, f32[8,2]{1,0:T(8,128)S(1)} %copy.18.cut_ref, f32[4,91,128]{2,1,0:T(8,128)S(1)} %copy-done.2, bf16[768,256]{1,0:T(8,128)(2,1)S(1)} %copy-done.1, bf16[768,256]{1,0:T(8,128)(2,1)S(1)} %copy-done), custom_call_target="tpu_custom_call" | custom-call | tf_op jit(solution)/shard_map/polar_filter/pallas_call | solution.py:336
  30.1 3.8 %all-to-all-start.1 = ((f32[32,8,768]{2,1,0:T(8,128)}), f32[32,8,768]{2,1,0:T(8,128)S(1)}, u32[]{:S(2)}, u32[]{:S(2)}) async-start(f32[32,8,768]{2,1,0:T(8,128)} %polar_filter.1), calls=%async_computation.1 | async-start | bytes 1572864 | tf_op jit(solution)/shard_map/all_to_all | solution.py:534
  34.0 0.1 cosine_divide_fusion
  34.0 0.1 multiply_bitcast_fusion.1
  34.1 14.1 %all-to-all-done.1.field_ref = f32[32,8,768]{2,1,0:T(8,128)S(1)} async-done(((f32[32,8,768]{2,1,0:T(8,128)}), f32[32,8,768]{2,1,0:T(8,128)S(1)}, u32[]{:S(2)}, u32[]{:S(2)}) %all-to-all-start.1) | async-done | bytes 786464 | tf_op jit(solution)/shard_map/all_to_all | solution.py:534
  48.2 3.1 %collective-permute-start.1 = (f32[3,768]{1,0:T(4,128)S(1)}, f32[3,768]{1,0:T(4,128)S(1)}, u32[]{:S(2)}, u32[]{:S(2)}) collective-permute-start(f32[3,768]{1,0:T(4,128)S(1)} %get-tuple-element.15), channel_id=1, source_target_pairs={{0,16},{1,17},{2,18},{3,19},{4,20},{5,21},{6,22},{7,23},{8,24},{9,... | collective-permute-start | bytes 27656 | tf_op jit(solution)/shard_map/ppermute | solution.py:550
  51.3 2.1 %collective-permute-start = (f32[3,768]{1,0:T(4,128)S(1)}, f32[3,768]{1,0:T(4,128)S(1)}, u32[]{:S(2)}, u32[]{:S(2)}) collective-permute-start(f32[3,768]{1,0:T(4,128)S(1)} %get-tuple-element.16), channel_id=1, source_target_pairs={{0,32},{1,33},{2,34},{3,35},{4,36},{5,37},{6,38},{7,39},{8,40},{9,... | collective-permute-start | bytes 27656 | tf_op jit(solution)/shard_map/ppermute | solution.py:549
  53.4 0.1 copy.20.coef_ref
  53.5 1.6 %stencil_main.1 = (f32[2,64,720]{2,1,0:T(8,128)}, f32[64,720]{1,0:T(8,128)}, f32[64,720]{1,0:T(8,128)}) custom-call(f32[32,8,768]{2,1,0:T(8,128)S(1)} %all-to-all-done.1.field_ref, f32[64,4]{1,0:T(8,128)S(1)} %copy.20.coef_ref), custom_call_target="tpu_custom_call" | custom-call | flops 10000000 | bytes 1600000 | tf_op jit(solution)/shard_map/stencil_main/pallas_call | solution.py:483
  55.1 0.0 collective-permute-done.1.second_ref
  55.1 0.6 %collective-permute-done.first_ref = f32[3,768]{1,0:T(4,128)S(1)} collective-permute-done((f32[3,768]{1,0:T(4,128)S(1)}, f32[3,768]{1,0:T(4,128)S(1)}, u32[]{:S(2)}, u32[]{:S(2)}) %collective-permute-start) | collective-permute-done | bytes 9248 | tf_op jit(solution)/shard_map/ppermute | solution.py:549
  55.8 0.9 %stencil_edge.1 = (f32[2,64,720]{2,1,0:T(8,128)}, f32[64,720]{1,0:T(8,128)}, f32[64,720]{1,0:T(8,128)}) custom-call(s32[1]{0:T(128)} %bitcast.even_ref, f32[32,8,768]{2,1,0:T(8,128)S(1)} %all-to-all-done.1.field_ref, f32[3,768]{1,0:T(4,128)S(1)} %collective-permute-done.first_ref, ...), custom_call_target="tpu_custom_call", output_to_operand_aliasing={{0}: (5, {}), {1}: (6, {}), {2}: (7, {})} | custom-call | tf_op jit(solution)/shard_map/stencil_edge/pallas_call | solution.py:502
  (9 shorter events, 0.1 us)
Async XLA Ops:
  2.6 24.9 %copy-start = (bf16[768,256]{1,0:T(8,128)(2,1)S(1)}, bf16[768,256]{1,0:T(8,128)(2,1)}, u32[]{:S(2)}) copy-start(bf16[768,256]{1,0:T(8,128)(2,1)} %constant.68.clone.inverse_ref) | copy-start | bytes 1179652
  2.6 24.9 %copy-start.1 = (bf16[768,256]{1,0:T(8,128)(2,1)S(1)}, bf16[768,256]{1,0:T(8,128)(2,1)}, u32[]{:S(2)}) copy-start(bf16[768,256]{1,0:T(8,128)(2,1)} %constant.67.clone.forward_ref) | copy-start | bytes 1179652
  2.6 24.9 %copy-start.2 = (f32[4,91,128]{2,1,0:T(8,128)S(1)}, f32[4,91,128]{2,1,0:T(8,128)}, u32[]{:S(2)}) copy-start(f32[4,91,128]{2,1,0:T(8,128)} %constant.66.clone.rows_ref) | copy-start | bytes 559108
  2.6 24.9 %all-to-all-start = ((f32[32,8,720]{2,1,0:T(8,128)}), f32[32,8,720]{2,1,0:T(8,128)S(1)}, u32[]{:S(2)}, u32[]{:S(2)}) async-start(f32[32,8,720]{2,1,0:T(8,128)} %pack.1), calls=%async_computation | async-start | bytes 1572864 | tf_op jit(solution)/shard_map/all_to_all | solution.py:523
  13.2 0.7 %copy-start.4 = (s32[64]{0:T(128)S(1)}, s32[64]{0:T(128)}, u32[]{:S(2)}) copy-start(s32[64]{0:T(128)} %param.11) | copy-start | bytes 772
  13.9 0.7 %copy-start.3 = (f32[64]{0:T(128)S(1)}, f32[64]{0:T(128)}, u32[]{:S(2)}) copy-start(f32[64]{0:T(128)} %param.12) | copy-start | bytes 772
  30.1 18.0 %all-to-all-start.1 = ((f32[32,8,768]{2,1,0:T(8,128)}), f32[32,8,768]{2,1,0:T(8,128)S(1)}, u32[]{:S(2)}, u32[]{:S(2)}) async-start(f32[32,8,768]{2,1,0:T(8,128)} %polar_filter.1), calls=%async_computation.1 | async-start | bytes 1572864 | tf_op jit(solution)/shard_map/all_to_all | solution.py:534
  48.2 6.9 %collective-permute-start.1 = (f32[3,768]{1,0:T(4,128)S(1)}, f32[3,768]{1,0:T(4,128)S(1)}, u32[]{:S(2)}, u32[]{:S(2)}) collective-permute-start(f32[3,768]{1,0:T(4,128)S(1)} %get-tuple-element.15), channel_id=1, source_target_pairs={{0,16},{1,17},{2,18},{3,19},{4,20},{5,21},{6,22},{7,23},{8,24},{9,... | collective-permute-start | bytes 27656 | tf_op jit(solution)/shard_map/ppermute | solution.py:550
  51.3 4.4 %collective-permute-start = (f32[3,768]{1,0:T(4,128)S(1)}, f32[3,768]{1,0:T(4,128)S(1)}, u32[]{:S(2)}, u32[]{:S(2)}) collective-permute-start(f32[3,768]{1,0:T(4,128)S(1)} %get-tuple-element.16), channel_id=1, source_target_pairs={{0,32},{1,33},{2,34},{3,35},{4,36},{5,37},{6,38},{7,39},{8,40},{9,... | collective-permute-start | bytes 27656 | tf_op jit(solution)/shard_map/ppermute | solution.py:549

commit v4 on v3

--- a/solution.py
+++ b/solution.py
@@ -418,32 +418,42 @@
     return slope * (h_e - west(h)), new_v, new_h, new_q
 
 
-def main_kernel(ratio, field_ref, coef_ref, winds_ref, layer_ref, tracer_ref):
+def main_kernel(ratio, field_ref, coef_ref, winds_ref, layer_ref, tracer_ref, out, sem):
     groups = field_ref.shape[0] // 4
     span = layer_ref.shape[1]
     sub = lax.broadcasted_iota(jnp.int32, (8, WIDE), 0)
+    writes = []
+
+    def write(k, g, value, target):
+        out[k, g] = value[:, :span]
+        writes.append(pltpu.make_async_copy(out.at[k, g], target, sem.at[k, g]))
+        writes[-1].start()
 
     def shifted(f, g):
         x = field_ref[groups * f + g]
-        below = field_ref[groups * f + max(g - 1, 0)]
-        above = field_ref[groups * f + min(g + 1, groups - 1)]
-        south = jnp.where(sub == 0, pltpu.roll(below, 1, 0), pltpu.roll(x, 1, 0))
-        north = jnp.where(sub == 7, pltpu.roll(above, 7, 0), pltpu.roll(x, 7, 0))
+        south = jnp.where(sub == 0, pltpu.roll(field_ref[groups * f + g - 1], 1, 0), pltpu.roll(x, 1, 0))
+        north = jnp.where(sub == 7, pltpu.roll(field_ref[groups * f + g + 1], 7, 0), pltpu.roll(x, 7, 0))
         return x, south, north
 
     for g in range(groups):
         rows = slice(8 * g, 8 * g + 8)
         u = field_ref[g]
-        mid_rows, south_rows, north_rows = zip(*(shifted(f, g) for f in (1, 2, 3)))
-        du, new_v, new_h, new_q = update(ratio, u, mid_rows, south_rows, north_rows, coef_ref[rows, :])
-        winds_ref[0, rows, :] = (u - du)[:, :span]
-        winds_ref[1, rows, :] = new_v[:, :span]
-        layer_ref[rows, :] = new_h[:, :span]
-        tracer_ref[rows, :] = new_q[:, :span]
+        if 0 < g < groups - 1:
+            mid_rows, south_rows, north_rows = zip(*(shifted(f, g) for f in (1, 2, 3)))
+            du, new_v, new_h, new_q = update(ratio, u, mid_rows, south_rows, north_rows, coef_ref[rows, :])
+            write(1, g, new_v, winds_ref.at[1, rows])
+            write(2, g, new_h, layer_ref.at[rows])
+            write(3, g, new_q, tracer_ref.at[rows])
+        else:
+            h = field_ref[2 * groups + g]
+            du = coef_ref[rows, 3:4] * (east(h) - west(h))
+        write(0, g, u - du, winds_ref.at[0, rows])
+    for copy in writes:
+        copy.wait()
 
 
 def edge_kernel(
-    ratio, even_ref, field_ref, first_ref, second_ref, coef_ref, w_in, l_in, t_in, winds_ref, layer_ref, tracer_ref, out, sem
+    ratio, even_ref, field_ref, second_ref, first_ref, coef_ref, w_in, l_in, t_in, winds_ref, layer_ref, tracer_ref, out, sem
 ):
     del w_in, l_in, t_in
     groups = field_ref.shape[0] // 4
@@ -480,6 +490,7 @@
 
 def stencil_main(fields, coef, ratio, row_count, width):
     vmem = pl.BlockSpec(memory_space=pltpu.VMEM)
+    anywhere = pl.BlockSpec(memory_space=pl.ANY)
     return pl.pallas_call(
         functools.partial(main_kernel, ratio),
         out_shape=(
@@ -488,7 +499,11 @@
             jax.ShapeDtypeStruct((row_count, width), jnp.float32),
         ),
         in_specs=[vmem, vmem],
-        out_specs=(vmem, vmem, vmem),
+        out_specs=(anywhere, anywhere, anywhere),
+        scratch_shapes=[
+            pltpu.VMEM((4, row_count // 8, 8, width), jnp.float32),
+            pltpu.SemaphoreType.DMA((4, row_count // 8)),
+        ],
         compiler_params=pltpu.CompilerParams(vmem_limit_bytes=SMALL_GRANT),
         cost_estimate=pl.CostEstimate(flops=10_000_000, bytes_accessed=1_600_000, transcendentals=0),
         name="stencil_main",
@@ -508,7 +523,7 @@
         input_output_aliases={5: 0, 6: 1, 7: 2},
         compiler_params=pltpu.CompilerParams(vmem_limit_bytes=SMALL_GRANT),
         name="stencil_edge",
-    )(even, fields, first, second, coef, *outs)
+    )(even, fields, second, first, coef, *outs)
 
 
 def per_device(winds, thickness, tracer, cutoff, damping):

time: 57 us -> 57.3 us (level)
    ppermute x1, waiting for transfers between devices: 0.01 us -> 0.93 us  [per_device(): second = lax.ppermute(jnp.where(even, low, high), ('lat', 'lon'), pairs[1])]
    ppermute x1, waiting for transfers between devices: 0.62 us -> 0.01 us  [per_device(): first = lax.ppermute(jnp.where(even, high, low), ('lat', 'lon'), pairs[0])]
where the time goes in v4:
time: 57.3 us; the launch traced here: 56.9 us
  waiting for transfers between devices  27.8 us (49%)
  starting transfers between devices  19.3 us (34%)
  Pallas kernels  7.16 us (12%)
  local copies, waits for them, and re-layouts  1.52 us (3%)
  between operations  0.79 us (1%)
    all_to_all x1, waiting for transfers between devices, per_device(): lax.all_to_all(filtered, 'lon', split_axis=0, concat_axis=0, tiled=True)  14.1 us
    all_to_all x1, waiting for transfers between devices, per_device(): lax.all_to_all(blocks, 'lon', split_axis=0, concat_axis=0, tiled=True)  12.8 us
    all_to_all x1, starting transfers between devices, per_device(): lax.all_to_all(blocks, 'lon', split_axis=0, concat_axis=0, tiled=True)  10.5 us
    all_to_all x1, starting transfers between devices, per_device(): lax.all_to_all(filtered, 'lon', split_axis=0, concat_axis=0, tiled=True)  3.77 us
    ppermute x1, starting transfers between devices, per_device(): second = lax.ppermute(jnp.where(even, low, high), ('lat', 'lon'), pairs[1])  3.11 us
    pallas_call x1, Pallas kernels, filter_rows(): pl.pallas_call(filter_kernel, out_shape=jax.ShapeDtypeStruct((blocks.shap...  2.59 us
    pallas_call x1, Pallas kernels, pack(): pl.pallas_call(functools.partial(pack_kernel, pieces), out_shape=jax.Shap...  1.96 us
    ppermute x1, starting transfers between devices, per_device(): first = lax.ppermute(jnp.where(even, high, low), ('lat', 'lon'), pairs[0])  1.92 us
  transfers between devices with their start and end apart: 4, of which 3 were waited for; matrix products, arithmetic and copies ran while one was open for 1% of the time, Pallas kernels for 3%

profile of v4, /device:TPU:1, one launch (start us, length us, event | category | flops | bytes accessed | tf_op | source)
XLA Modules:
  0.0 56.9 jit_solution(17554001916531326690)
XLA Ops:
  0.6 2.0 %pack.1 = f32[32,8,720]{2,1,0:T(8,128)} custom-call(f32[16,8,720]{2,1,0:T(8,128)} %bitcast.24, f32[8,8,720]{2,1,0:T(8,128)} %bitcast.25, f32[8,8,720]{2,1,0:T(8,128)} %bitcast.26), custom_call_target="tpu_custom_call" | custom-call | tf_op jit(solution)/shard_map/pack/pallas_call | solution.py:378
  2.6 0.0 copy-start
  2.6 0.0 copy-start.1
  2.6 0.0 copy-start.2
  2.6 10.5 %all-to-all-start = ((f32[32,8,720]{2,1,0:T(8,128)}), f32[32,8,720]{2,1,0:T(8,128)S(1)}, u32[]{:S(2)}, u32[]{:S(2)}) async-start(f32[32,8,720]{2,1,0:T(8,128)} %pack.1), calls=%async_computation | async-start | bytes 1572864 | tf_op jit(solution)/shard_map/all_to_all | solution.py:538
  13.2 0.0 copy-start.4
  13.2 0.6 %copy-done.4 = s32[64]{0:T(128)S(1)} copy-done((s32[64]{0:T(128)S(1)}, s32[64]{0:T(128)}, u32[]{:S(2)}) %copy-start.4) | copy-done | bytes 280
  13.9 0.7 %copy-done.3 = f32[64]{0:T(128)S(1)} copy-done((f32[64]{0:T(128)S(1)}, f32[64]{0:T(128)}, u32[]{:S(2)}) %copy-start.3) | copy-done | bytes 280
  14.5 0.1 fusion.3
  14.6 0.1 copy.18.cut_ref
  14.7 12.8 %all-to-all-done.x_ref = f32[32,8,720]{2,1,0:T(8,128)S(1)} async-done(((f32[32,8,720]{2,1,0:T(8,128)}), f32[32,8,720]{2,1,0:T(8,128)S(1)}, u32[]{:S(2)}, u32[]{:S(2)}) %all-to-all-start) | async-done | bytes 737312 | tf_op jit(solution)/shard_map/all_to_all | solution.py:538
  27.5 0.0 copy-done.1
  27.5 2.6 %polar_filter.1 = f32[32,8,768]{2,1,0:T(8,128)} custom-call(f32[32,8,720]{2,1,0:T(8,128)S(1)} %all-to-all-done.x_ref, f32[8,2]{1,0:T(8,128)S(1)} %copy.18.cut_ref, f32[4,91,128]{2,1,0:T(8,128)S(1)} %copy-done.2, bf16[768,256]{1,0:T(8,128)(2,1)S(1)} %copy-done.1, bf16[768,256]{1,0:T(8,128)(2,1)S(1)} %copy-done), custom_call_target="tpu_custom_call" | custom-call | tf_op jit(solution)/shard_map/polar_filter/pallas_call | solution.py:336
  30.1 3.8 %all-to-all-start.1 = ((f32[32,8,768]{2,1,0:T(8,128)}), f32[32,8,768]{2,1,0:T(8,128)S(1)}, u32[]{:S(2)}, u32[]{:S(2)}) async-start(f32[32,8,768]{2,1,0:T(8,128)} %polar_filter.1), calls=%async_computation.1 | async-start | bytes 1572864 | tf_op jit(solution)/shard_map/all_to_all | solution.py:549
  34.0 0.1 cosine_divide_fusion
  34.0 0.1 multiply_bitcast_fusion.1
  34.1 14.1 %all-to-all-done.1.field_ref = f32[32,8,768]{2,1,0:T(8,128)S(1)} async-done(((f32[32,8,768]{2,1,0:T(8,128)}), f32[32,8,768]{2,1,0:T(8,128)S(1)}, u32[]{:S(2)}, u32[]{:S(2)}) %all-to-all-start.1) | async-done | bytes 786464 | tf_op jit(solution)/shard_map/all_to_all | solution.py:549
  48.2 1.9 %collective-permute-start.1 = (f32[3,768]{1,0:T(4,128)S(1)}, f32[3,768]{1,0:T(4,128)S(1)}, u32[]{:S(2)}, u32[]{:S(2)}) collective-permute-start(f32[3,768]{1,0:T(4,128)S(1)} %get-tuple-element.15), channel_id=1, source_target_pairs={{0,32},{1,33},{2,34},{3,35},{4,36},{5,37},{6,38},{7,39},{8,40},{9,... | collective-permute-start | bytes 27656 | tf_op jit(solution)/shard_map/ppermute | solution.py:564
  50.1 3.1 %collective-permute-start = (f32[3,768]{1,0:T(4,128)S(1)}, f32[3,768]{1,0:T(4,128)S(1)}, u32[]{:S(2)}, u32[]{:S(2)}) collective-permute-start(f32[3,768]{1,0:T(4,128)S(1)} %get-tuple-element.16), channel_id=1, source_target_pairs={{0,16},{1,17},{2,18},{3,19},{4,20},{5,21},{6,22},{7,23},{8,24},{9,... | collective-permute-start | bytes 27656 | tf_op jit(solution)/shard_map/ppermute | solution.py:565
  53.3 0.1 copy.20.coef_ref
  53.4 1.8 %stencil_main.1 = (f32[2,64,720]{2,1,0:T(8,128)}, f32[64,720]{1,0:T(8,128)}, f32[64,720]{1,0:T(8,128)}) custom-call(f32[32,8,768]{2,1,0:T(8,128)S(1)} %all-to-all-done.1.field_ref, f32[64,4]{1,0:T(8,128)S(1)} %copy.20.coef_ref), custom_call_target="tpu_custom_call" | custom-call | flops 10000000 | bytes 1600000 | tf_op jit(solution)/shard_map/stencil_main/pallas_call | solution.py:494
  55.1 0.0 collective-permute-done.1.first_ref
  55.1 0.9 %collective-permute-done.second_ref = f32[3,768]{1,0:T(4,128)S(1)} collective-permute-done((f32[3,768]{1,0:T(4,128)S(1)}, f32[3,768]{1,0:T(4,128)S(1)}, u32[]{:S(2)}, u32[]{:S(2)}) %collective-permute-start) | collective-permute-done | bytes 9248 | tf_op jit(solution)/shard_map/ppermute | solution.py:565
  56.1 0.9 %stencil_edge.1 = (f32[2,64,720]{2,1,0:T(8,128)}, f32[64,720]{1,0:T(8,128)}, f32[64,720]{1,0:T(8,128)}) custom-call(s32[1]{0:T(128)} %bitcast.even_ref, f32[32,8,768]{2,1,0:T(8,128)S(1)} %all-to-all-done.1.field_ref, f32[3,768]{1,0:T(4,128)S(1)} %collective-permute-done.second_ref, ...), custom_call_target="tpu_custom_call", output_to_operand_aliasing={{0}: (5, {}), {1}: (6, {}), {2}: (7, {})} | custom-call | tf_op jit(solution)/shard_map/stencil_edge/pallas_call | solution.py:517
  (9 shorter events, 0.1 us)
Async XLA Ops:
  2.6 24.9 %copy-start = (bf16[768,256]{1,0:T(8,128)(2,1)S(1)}, bf16[768,256]{1,0:T(8,128)(2,1)}, u32[]{:S(2)}) copy-start(bf16[768,256]{1,0:T(8,128)(2,1)} %constant.68.clone.inverse_ref) | copy-start | bytes 1179652
  2.6 24.9 %copy-start.1 = (bf16[768,256]{1,0:T(8,128)(2,1)S(1)}, bf16[768,256]{1,0:T(8,128)(2,1)}, u32[]{:S(2)}) copy-start(bf16[768,256]{1,0:T(8,128)(2,1)} %constant.67.clone.forward_ref) | copy-start | bytes 1179652
  2.6 24.9 %copy-start.2 = (f32[4,91,128]{2,1,0:T(8,128)S(1)}, f32[4,91,128]{2,1,0:T(8,128)}, u32[]{:S(2)}) copy-start(f32[4,91,128]{2,1,0:T(8,128)} %constant.66.clone.rows_ref) | copy-start | bytes 559108
  2.6 24.9 %all-to-all-start = ((f32[32,8,720]{2,1,0:T(8,128)}), f32[32,8,720]{2,1,0:T(8,128)S(1)}, u32[]{:S(2)}, u32[]{:S(2)}) async-start(f32[32,8,720]{2,1,0:T(8,128)} %pack.1), calls=%async_computation | async-start | bytes 1572864 | tf_op jit(solution)/shard_map/all_to_all | solution.py:538
  13.2 0.7 %copy-start.4 = (s32[64]{0:T(128)S(1)}, s32[64]{0:T(128)}, u32[]{:S(2)}) copy-start(s32[64]{0:T(128)} %param.11) | copy-start | bytes 772
  13.9 0.7 %copy-start.3 = (f32[64]{0:T(128)S(1)}, f32[64]{0:T(128)}, u32[]{:S(2)}) copy-start(f32[64]{0:T(128)} %param.12) | copy-start | bytes 772
  30.1 18.0 %all-to-all-start.1 = ((f32[32,8,768]{2,1,0:T(8,128)}), f32[32,8,768]{2,1,0:T(8,128)S(1)}, u32[]{:S(2)}, u32[]{:S(2)}) async-start(f32[32,8,768]{2,1,0:T(8,128)} %polar_filter.1), calls=%async_computation.1 | async-start | bytes 1572864 | tf_op jit(solution)/shard_map/all_to_all | solution.py:549
  48.2 6.9 %collective-permute-start.1 = (f32[3,768]{1,0:T(4,128)S(1)}, f32[3,768]{1,0:T(4,128)S(1)}, u32[]{:S(2)}, u32[]{:S(2)}) collective-permute-start(f32[3,768]{1,0:T(4,128)S(1)} %get-tuple-element.15), channel_id=1, source_target_pairs={{0,32},{1,33},{2,34},{3,35},{4,36},{5,37},{6,38},{7,39},{8,40},{9,... | collective-permute-start | bytes 27656 | tf_op jit(solution)/shard_map/ppermute | solution.py:564
  50.1 5.9 %collective-permute-start = (f32[3,768]{1,0:T(4,128)S(1)}, f32[3,768]{1,0:T(4,128)S(1)}, u32[]{:S(2)}, u32[]{:S(2)}) collective-permute-start(f32[3,768]{1,0:T(4,128)S(1)} %get-tuple-element.16), channel_id=1, source_target_pairs={{0,16},{1,17},{2,18},{3,19},{4,20},{5,21},{6,22},{7,23},{8,24},{9,... | collective-permute-start | bytes 27656 | tf_op jit(solution)/shard_map/ppermute | solution.py:565

commit v5 on v4

--- a/solution.py
+++ b/solution.py
@@ -182,7 +182,8 @@
 CLASS_GROUPS = [ALL_CLASSES[first:last] for first, last in zip(CLASS_CUTS[:-1], CLASS_CUTS[1:])]
 
 
-def filter_kernel(x_ref, cut_ref, rows_ref, forward_ref, inverse_ref, out_ref, full, mid, stage, result, sem):
+def filter_kernel(x_ref, cut_ref, rows_ref, forward_ref, inverse_ref, early_ref, out_ref, full, mid, stage, result, sem):
+    del early_ref
     sectors = x_ref.shape[0]
     span = x_ref.shape[2]
     lane = lax.broadcasted_iota(jnp.int32, (8, LANE), 1)
@@ -331,12 +332,12 @@
         write.wait()
 
 
-def filter_rows(blocks, cuts):
+def filter_rows(blocks, cuts, early):
     rows, forward, inverse = tables()
     return pl.pallas_call(
         filter_kernel,
         out_shape=jax.ShapeDtypeStruct((blocks.shape[0], 8, WIDE), jnp.float32),
-        in_specs=[pl.BlockSpec(memory_space=pltpu.VMEM)] * 5,
+        in_specs=[pl.BlockSpec(memory_space=pltpu.VMEM)] * 5 + [pl.BlockSpec(memory_space=pl.ANY)],
         out_specs=pl.BlockSpec(memory_space=pl.ANY),
         scratch_shapes=[
             pltpu.VMEM((8, (TILES + 2) * LANE), jnp.float32),
@@ -347,7 +348,7 @@
         ],
         compiler_params=pltpu.CompilerParams(vmem_limit_bytes=SMALL_GRANT),
         name="polar_filter",
-    )(blocks, cuts, jnp.asarray(rows), jnp.asarray(forward), jnp.asarray(inverse))
+    )(blocks, cuts, jnp.asarray(rows), jnp.asarray(forward), jnp.asarray(inverse), early)
 
 
 def pack_kernel(pieces, winds_ref, layer_ref, tracer_ref, out_ref, buffer, in_sem, out_sem):
@@ -424,11 +425,6 @@
     sub = lax.broadcasted_iota(jnp.int32, (8, WIDE), 0)
     writes = []
 
-    def write(k, g, value, target):
-        out[k, g] = value[:, :span]
-        writes.append(pltpu.make_async_copy(out.at[k, g], target, sem.at[k, g]))
-        writes[-1].start()
-
     def shifted(f, g):
         x = field_ref[groups * f + g]
         south = jnp.where(sub == 0, pltpu.roll(field_ref[groups * f + g - 1], 1, 0), pltpu.roll(x, 1, 0))
@@ -441,19 +437,33 @@
         if 0 < g < groups - 1:
             mid_rows, south_rows, north_rows = zip(*(shifted(f, g) for f in (1, 2, 3)))
             du, new_v, new_h, new_q = update(ratio, u, mid_rows, south_rows, north_rows, coef_ref[rows, :])
-            write(1, g, new_v, winds_ref.at[1, rows])
-            write(2, g, new_h, layer_ref.at[rows])
-            write(3, g, new_q, tracer_ref.at[rows])
+            out[1, rows, :] = new_v[:, :span]
+            out[2, rows, :] = new_h[:, :span]
+            out[3, rows, :] = new_q[:, :span]
         else:
             h = field_ref[2 * groups + g]
             du = coef_ref[rows, 3:4] * (east(h) - west(h))
-        write(0, g, u - du, winds_ref.at[0, rows])
+        out[0, rows, :] = (u - du)[:, :span]
+        if g in (groups // 2 - 1, groups - 1):
+            part = len(writes) // 4
+            half = groups // 2
+            all_rows = slice(8 * half * part, 8 * half * (part + 1))
+            inner = slice(8, 8 * half) if part == 0 else slice(8 * half, 8 * (groups - 1))
+            targets = (
+                (0, all_rows, winds_ref.at[0, all_rows]),
+                (1, inner, winds_ref.at[1, inner]),
+                (2, inner, layer_ref.at[inner]),
+                (3, inner, tracer_ref.at[inner]),
+            )
+            for k, where, target in targets:
+                writes.append(pltpu.make_async_copy(out.at[k, where], target, sem.at[part, k]))
+                writes[-1].start()
     for copy in writes:
         copy.wait()
 
 
 def edge_kernel(
-    ratio, even_ref, field_ref, second_ref, first_ref, coef_ref, w_in, l_in, t_in, winds_ref, layer_ref, tracer_ref, out, sem
+    ratio, even_ref, field_ref, first_ref, second_ref, coef_ref, w_in, l_in, t_in, winds_ref, layer_ref, tracer_ref, out, sem
 ):
     del w_in, l_in, t_in
     groups = field_ref.shape[0] // 4
@@ -501,8 +511,8 @@
         in_specs=[vmem, vmem],
         out_specs=(anywhere, anywhere, anywhere),
         scratch_shapes=[
-            pltpu.VMEM((4, row_count // 8, 8, width), jnp.float32),
-            pltpu.SemaphoreType.DMA((4, row_count // 8)),
+            pltpu.VMEM((4, row_count, width), jnp.float32),
+            pltpu.SemaphoreType.DMA((2, 4)),
         ],
         compiler_params=pltpu.CompilerParams(vmem_limit_bytes=SMALL_GRANT),
         cost_estimate=pl.CostEstimate(flops=10_000_000, bytes_accessed=1_600_000, transcendentals=0),
@@ -523,7 +533,7 @@
         input_output_aliases={5: 0, 6: 1, 7: 2},
         compiler_params=pltpu.CompilerParams(vmem_limit_bytes=SMALL_GRANT),
         name="stencil_edge",
-    )(even, fields, second, first, coef, *outs)
+    )(even, fields, first, second, coef, *outs)
 
 
 def per_device(winds, thickness, tracer, cutoff, damping):
@@ -545,7 +555,21 @@
     cut = jnp.where(is_polar, cut, jnp.float32(NLON))
     cuts = jnp.stack([cut, gain], axis=1)
 
-    filtered = filter_rows(owned, cuts)
+    lon_step = 2.0 * math.pi / NLON
+    lat_step = math.pi / nlat
+    rows = (band * row_count + jnp.arange(row_count, dtype=jnp.int32)).astype(jnp.float32)
+    center = jnp.cos(-math.pi / 2 + (rows + 0.5) * lat_step)
+    face = band * row_count + jnp.arange(row_count + 1, dtype=jnp.int32)
+    cos_face = jnp.where(
+        (face == 0) | (face == nlat), 0.0, jnp.cos(-math.pi / 2 + face.astype(jnp.float32) * lat_step)
+    )
+    quarter = 0.25 / center
+    aspect = lon_step / lat_step
+    coef = jnp.stack(
+        [quarter, aspect * quarter * cos_face[1:], aspect * quarter * cos_face[:-1], 2.0 * quarter], axis=1
+    )
+
+    filtered = filter_rows(owned, cuts, coef)
     fields = lax.all_to_all(filtered, "lon", split_axis=0, concat_axis=0, tiled=True)
 
     even = band % 2 == 0
@@ -564,19 +588,6 @@
     first = lax.ppermute(jnp.where(even, high, low), ("lat", "lon"), pairs[0])
     second = lax.ppermute(jnp.where(even, low, high), ("lat", "lon"), pairs[1])
 
-    lon_step = 2.0 * math.pi / NLON
-    lat_step = math.pi / nlat
-    rows = (band * row_count + jnp.arange(row_count, dtype=jnp.int32)).astype(jnp.float32)
-    center = jnp.cos(-math.pi / 2 + (rows + 0.5) * lat_step)
-    face = band * row_count + jnp.arange(row_count + 1, dtype=jnp.int32)
-    cos_face = jnp.where(
-        (face == 0) | (face == nlat), 0.0, jnp.cos(-math.pi / 2 + face.astype(jnp.float32) * lat_step)
-    )
-    quarter = 0.25 / center
-    aspect = lon_step / lat_step
-    coef = jnp.stack(
-        [quarter, aspect * quarter * cos_face[1:], aspect * quarter * cos_face[:-1], 2.0 * quarter], axis=1
-    )
     ratio = lon_step / (2.0 * lat_step)
     outs = stencil_main(fields, coef, ratio, row_count, width)
     return stencil_edge(even.astype(jnp.int32)[None], fields, first, second, coef, outs, ratio)

time: 57.3 us -> 57 us (level)
    ppermute x1, waiting for transfers between devices: 0.93 us -> 0.01 us  [per_device(): second = lax.ppermute(jnp.where(even, low, high), ('lat', 'lon'), pairs[1])]
    ppermute x1, waiting for transfers between devices: 0.01 us -> 0.85 us  [per_device(): first = lax.ppermute(jnp.where(even, high, low), ('lat', 'lon'), pairs[0])]
where the time goes in v5:
time: 57 us; the launch traced here: 56.6 us
  waiting for transfers between devices  27.6 us (48%)
  starting transfers between devices  19.5 us (34%)
  Pallas kernels  6.88 us (12%)
  local copies, waits for them, and re-layouts  1.52 us (3%)
  between operations  0.79 us (1%)
    all_to_all x1, waiting for transfers between devices, per_device(): lax.all_to_all(filtered, 'lon', split_axis=0, concat_axis=0, tiled=True)  14.2 us
    all_to_all x1, waiting for transfers between devices, per_device(): lax.all_to_all(blocks, 'lon', split_axis=0, concat_axis=0, tiled=True)  12.5 us
    all_to_all x1, starting transfers between devices, per_device(): lax.all_to_all(blocks, 'lon', split_axis=0, concat_axis=0, tiled=True)  10.5 us
    all_to_all x1, starting transfers between devices, per_device(): lax.all_to_all(filtered, 'lon', split_axis=0, concat_axis=0, tiled=True)  3.77 us
    ppermute x1, starting transfers between devices, per_device(): second = lax.ppermute(jnp.where(even, low, high), ('lat', 'lon'), pairs[1])  3.11 us
    pallas_call x1, Pallas kernels, filter_rows(): pl.pallas_call(filter_kernel, out_shape=jax.ShapeDtypeStruct((blocks.shap...  2.59 us
    ppermute x1, starting transfers between devices, per_device(): first = lax.ppermute(jnp.where(even, high, low), ('lat', 'lon'), pairs[0])  2.08 us
    pallas_call x1, Pallas kernels, pack(): pl.pallas_call(functools.partial(pack_kernel, pieces), out_shape=jax.Shap...  1.96 us
  transfers between devices with their start and end apart: 4, of which 3 were waited for; matrix products, arithmetic and copies ran while one was open for 1% of the time, Pallas kernels for 3%

profile of v5, /device:TPU:1, one launch (start us, length us, event | category | flops | bytes accessed | tf_op | source)
XLA Modules:
  0.0 56.6 jit_solution(15876526566143196565)
XLA Ops:
  0.6 2.0 %pack.1 = f32[32,8,720]{2,1,0:T(8,128)} custom-call(f32[16,8,720]{2,1,0:T(8,128)} %bitcast.24, f32[8,8,720]{2,1,0:T(8,128)} %bitcast.25, f32[8,8,720]{2,1,0:T(8,128)} %bitcast.26), custom_call_target="tpu_custom_call" | custom-call | tf_op jit(solution)/shard_map/pack/pallas_call | solution.py:379
  2.6 0.0 copy-start
  2.6 0.0 copy-start.1
  2.6 0.0 copy-start.2
  2.6 10.5 %all-to-all-start = ((f32[32,8,720]{2,1,0:T(8,128)}), f32[32,8,720]{2,1,0:T(8,128)S(1)}, u32[]{:S(2)}, u32[]{:S(2)}) async-start(f32[32,8,720]{2,1,0:T(8,128)} %pack.1), calls=%async_computation | async-start | bytes 1572864 | tf_op jit(solution)/shard_map/all_to_all | solution.py:548
  13.2 0.0 copy-start.4
  13.2 0.6 %copy-done.4 = s32[64]{0:T(128)S(1)} copy-done((s32[64]{0:T(128)S(1)}, s32[64]{0:T(128)}, u32[]{:S(2)}) %copy-start.4) | copy-done | bytes 280
  13.9 0.7 %copy-done.3 = f32[64]{0:T(128)S(1)} copy-done((f32[64]{0:T(128)S(1)}, f32[64]{0:T(128)}, u32[]{:S(2)}) %copy-start.3) | copy-done | bytes 280
  14.5 0.1 fusion.3
  14.6 0.1 copy.18.cut_ref
  14.7 0.1 cosine_divide_fusion
  14.8 0.1 multiply_bitcast_fusion.1
  14.9 0.1 copy.19.early_ref.coef_ref
  15.0 12.5 %all-to-all-done.x_ref = f32[32,8,720]{2,1,0:T(8,128)S(1)} async-done(((f32[32,8,720]{2,1,0:T(8,128)}), f32[32,8,720]{2,1,0:T(8,128)S(1)}, u32[]{:S(2)}, u32[]{:S(2)}) %all-to-all-start) | async-done | bytes 737312 | tf_op jit(solution)/shard_map/all_to_all | solution.py:548
  27.5 0.0 copy-done.2
  27.5 2.6 %polar_filter.1 = f32[32,8,768]{2,1,0:T(8,128)} custom-call(f32[32,8,720]{2,1,0:T(8,128)S(1)} %all-to-all-done.x_ref, f32[8,2]{1,0:T(8,128)S(1)} %copy.18.cut_ref, f32[4,91,128]{2,1,0:T(8,128)S(1)} %copy-done.2, bf16[768,256]{1,0:T(8,128)(2,1)S(1)} %copy-done.1, bf16[768,256]{1,0:T(8,128)(2,1)S(1)} %copy-done, f32[64,4]{1,0:T(8,128)S(1)} %copy.19.early_ref.coef_ref), custom_call_target="tpu_custom_call" | custom-call | tf_op jit(solution)/shard_map/polar_filter/pallas_call | solution.py:337
  30.1 3.8 %all-to-all-start.1 = ((f32[32,8,768]{2,1,0:T(8,128)}), f32[32,8,768]{2,1,0:T(8,128)S(1)}, u32[]{:S(2)}, u32[]{:S(2)}) async-start(f32[32,8,768]{2,1,0:T(8,128)} %polar_filter.1), calls=%async_computation.1 | async-start | bytes 1572864 | tf_op jit(solution)/shard_map/all_to_all | solution.py:573
  33.9 14.2 %all-to-all-done.1.field_ref = f32[32,8,768]{2,1,0:T(8,128)S(1)} async-done(((f32[32,8,768]{2,1,0:T(8,128)}), f32[32,8,768]{2,1,0:T(8,128)S(1)}, u32[]{:S(2)}, u32[]{:S(2)}) %all-to-all-start.1) | async-done | bytes 786464 | tf_op jit(solution)/shard_map/all_to_all | solution.py:573
  48.2 3.1 %collective-permute-start.1 = (f32[3,768]{1,0:T(4,128)S(1)}, f32[3,768]{1,0:T(4,128)S(1)}, u32[]{:S(2)}, u32[]{:S(2)}) collective-permute-start(f32[3,768]{1,0:T(4,128)S(1)} %get-tuple-element.15), channel_id=1, source_target_pairs={{0,16},{1,17},{2,18},{3,19},{4,20},{5,21},{6,22},{7,23},{8,24},{9,... | collective-permute-start | bytes 27656 | tf_op jit(solution)/shard_map/ppermute | solution.py:589
  51.3 2.1 %collective-permute-start = (f32[3,768]{1,0:T(4,128)S(1)}, f32[3,768]{1,0:T(4,128)S(1)}, u32[]{:S(2)}, u32[]{:S(2)}) collective-permute-start(f32[3,768]{1,0:T(4,128)S(1)} %get-tuple-element.16), channel_id=1, source_target_pairs={{0,32},{1,33},{2,34},{3,35},{4,36},{5,37},{6,38},{7,39},{8,40},{9,... | collective-permute-start | bytes 27656 | tf_op jit(solution)/shard_map/ppermute | solution.py:588
  53.4 1.5 %stencil_main.1 = (f32[2,64,720]{2,1,0:T(8,128)}, f32[64,720]{1,0:T(8,128)}, f32[64,720]{1,0:T(8,128)}) custom-call(f32[32,8,768]{2,1,0:T(8,128)S(1)} %all-to-all-done.1.field_ref, f32[64,4]{1,0:T(8,128)S(1)} %copy.19.early_ref.coef_ref), custom_call_target="tpu_custom_call" | custom-call | flops 10000000 | bytes 1600000 | tf_op jit(solution)/shard_map/stencil_main/pallas_call | solution.py:504
  54.9 0.0 collective-permute-done.1.second_ref
  54.9 0.9 %collective-permute-done.first_ref = f32[3,768]{1,0:T(4,128)S(1)} collective-permute-done((f32[3,768]{1,0:T(4,128)S(1)}, f32[3,768]{1,0:T(4,128)S(1)}, u32[]{:S(2)}, u32[]{:S(2)}) %collective-permute-start) | collective-permute-done | bytes 9248 | tf_op jit(solution)/shard_map/ppermute | solution.py:588
  55.8 0.9 %stencil_edge.1 = (f32[2,64,720]{2,1,0:T(8,128)}, f32[64,720]{1,0:T(8,128)}, f32[64,720]{1,0:T(8,128)}) custom-call(s32[1]{0:T(128)} %bitcast.even_ref, f32[32,8,768]{2,1,0:T(8,128)S(1)} %all-to-all-done.1.field_ref, f32[3,768]{1,0:T(4,128)S(1)} %collective-permute-done.first_ref, ...), custom_call_target="tpu_custom_call", output_to_operand_aliasing={{0}: (5, {}), {1}: (6, {}), {2}: (7, {})} | custom-call | tf_op jit(solution)/shard_map/stencil_edge/pallas_call | solution.py:527
  (9 shorter events, 0.1 us)
Async XLA Ops:
  2.6 24.9 %copy-start = (bf16[768,256]{1,0:T(8,128)(2,1)S(1)}, bf16[768,256]{1,0:T(8,128)(2,1)}, u32[]{:S(2)}) copy-start(bf16[768,256]{1,0:T(8,128)(2,1)} %constant.68.clone.inverse_ref) | copy-start | bytes 1179652
  2.6 24.9 %copy-start.1 = (bf16[768,256]{1,0:T(8,128)(2,1)S(1)}, bf16[768,256]{1,0:T(8,128)(2,1)}, u32[]{:S(2)}) copy-start(bf16[768,256]{1,0:T(8,128)(2,1)} %constant.67.clone.forward_ref) | copy-start | bytes 1179652
  2.6 24.9 %copy-start.2 = (f32[4,91,128]{2,1,0:T(8,128)S(1)}, f32[4,91,128]{2,1,0:T(8,128)}, u32[]{:S(2)}) copy-start(f32[4,91,128]{2,1,0:T(8,128)} %constant.66.clone.rows_ref) | copy-start | bytes 559108
  2.6 24.9 %all-to-all-start = ((f32[32,8,720]{2,1,0:T(8,128)}), f32[32,8,720]{2,1,0:T(8,128)S(1)}, u32[]{:S(2)}, u32[]{:S(2)}) async-start(f32[32,8,720]{2,1,0:T(8,128)} %pack.1), calls=%async_computation | async-start | bytes 1572864 | tf_op jit(solution)/shard_map/all_to_all | solution.py:548
  13.2 0.7 %copy-start.4 = (s32[64]{0:T(128)S(1)}, s32[64]{0:T(128)}, u32[]{:S(2)}) copy-start(s32[64]{0:T(128)} %param.11) | copy-start | bytes 772
  13.9 0.7 %copy-start.3 = (f32[64]{0:T(128)S(1)}, f32[64]{0:T(128)}, u32[]{:S(2)}) copy-start(f32[64]{0:T(128)} %param.12) | copy-start | bytes 772
  30.1 18.0 %all-to-all-start.1 = ((f32[32,8,768]{2,1,0:T(8,128)}), f32[32,8,768]{2,1,0:T(8,128)S(1)}, u32[]{:S(2)}, u32[]{:S(2)}) async-start(f32[32,8,768]{2,1,0:T(8,128)} %polar_filter.1), calls=%async_computation.1 | async-start | bytes 1572864 | tf_op jit(solution)/shard_map/all_to_all | solution.py:573
  48.2 6.7 %collective-permute-start.1 = (f32[3,768]{1,0:T(4,128)S(1)}, f32[3,768]{1,0:T(4,128)S(1)}, u32[]{:S(2)}, u32[]{:S(2)}) collective-permute-start(f32[3,768]{1,0:T(4,128)S(1)} %get-tuple-element.15), channel_id=1, source_target_pairs={{0,16},{1,17},{2,18},{3,19},{4,20},{5,21},{6,22},{7,23},{8,24},{9,... | collective-permute-start | bytes 27656 | tf_op jit(solution)/shard_map/ppermute | solution.py:589
  51.3 4.4 %collective-permute-start = (f32[3,768]{1,0:T(4,128)S(1)}, f32[3,768]{1,0:T(4,128)S(1)}, u32[]{:S(2)}, u32[]{:S(2)}) collective-permute-start(f32[3,768]{1,0:T(4,128)S(1)} %get-tuple-element.16), channel_id=1, source_target_pairs={{0,32},{1,33},{2,34},{3,35},{4,36},{5,37},{6,38},{7,39},{8,40},{9,... | collective-permute-start | bytes 27656 | tf_op jit(solution)/shard_map/ppermute | solution.py:588

commit v6 on v5

--- a/solution.py
+++ b/solution.py
@@ -8,6 +8,7 @@
 from jax.experimental import pallas as pl
 from jax.experimental.pallas import tpu as pltpu
 from jax.sharding import PartitionSpec as P
+
 
 LEV = 8
 NLON = 2880
@@ -182,20 +183,19 @@
 CLASS_GROUPS = [ALL_CLASSES[first:last] for first, last in zip(CLASS_CUTS[:-1], CLASS_CUTS[1:])]
 
 
-def filter_kernel(x_ref, cut_ref, rows_ref, forward_ref, inverse_ref, early_ref, out_ref, full, mid, stage, result, sem):
-    del early_ref
-    sectors = x_ref.shape[0]
-    span = x_ref.shape[2]
+def circle_filter(source_tile, span, cut_ref, rows_ref, forward_ref, inverse_ref, full, mid, stage):
     lane = lax.broadcasted_iota(jnp.int32, (8, LANE), 1)
     turned = {}
 
     def source(d, t):
         if (d, t) not in turned:
-            value = x_ref[d, :, LANE * t : min(LANE * (t + 1), span)]
-            if value.shape[1] < LANE:
-                value = jnp.concatenate([value, jnp.zeros((8, LANE - value.shape[1]), jnp.float32)], axis=1)
+            value = source_tile(d, t)
             shift = d * span % LANE
-            turned[(d, t)] = pltpu.roll(value, shift, 1) if shift else value
+            if value is None:
+                value = jnp.zeros((8, LANE), jnp.float32)
+            elif shift:
+                value = pltpu.roll(value, shift, 1)
+            turned[(d, t)] = value
         return turned[(d, t)]
 
     for p in range(TILES):
@@ -311,6 +311,17 @@
                 if p == TILES - 1:
                     full[:, tile(-1)] = values[a]
 
+
+def filter_kernel(x_ref, cut_ref, rows_ref, forward_ref, inverse_ref, early_ref, out_ref, full, mid, stage, result, sem):
+    del early_ref
+    sectors = x_ref.shape[0]
+    span = NLON * LEV // sectors
+    lane = lax.broadcasted_iota(jnp.int32, (8, LANE), 1)
+
+    def source_tile(d, t):
+        return x_ref[d, :, LANE * t : LANE * (t + 1)]
+
+    circle_filter(source_tile, span, cut_ref, rows_ref, forward_ref, inverse_ref, full, mid, stage)
     writes = []
     for d in range(sectors):
         first, shift = divmod(LANE + d * span, LANE)
@@ -332,6 +343,75 @@
         write.wait()
 
 
+PIECE = 48
+AHEAD = 6
+WINDOW = 10
+
+
+def pole_kernel(where_ref, x_ref, cut_ref, rows_ref, forward_ref, inverse_ref, out_ref, full, mid, stage, wide, window):
+    sectors = x_ref.shape[0]
+    span = NLON * LEV // sectors
+    lane = lax.broadcasted_iota(jnp.int32, (8, LANE), 1)
+
+    def source_tile(d, t):
+        if t:
+            return None
+        value = pltpu.roll(x_ref[d, :, WIDE - LANE : WIDE], PIECE, 1)
+        return jnp.where(lane < PIECE, value, 0.0)
+
+    circle_filter(source_tile, span, cut_ref, rows_ref, forward_ref, inverse_ref, full, mid, stage)
+    wide[:, LANE * AHEAD : LANE * (AHEAD + TILES)] = full[:, LANE : LANE * (TILES + 1)]
+    wide[:, : LANE * AHEAD] = full[:, LANE * (TILES + 1 - AHEAD) : LANE * (TILES + 1)]
+    wide[:, LANE * (AHEAD + TILES) :] = full[:, LANE : LANE * 5]
+    for k in range(2):
+        tile = where_ref[2 * k]
+        rest = where_ref[2 * k + 1]
+        start = pl.multiple_of(tile * LANE, LANE)
+        window[...] = pltpu.roll(wide[:, pl.ds(start, WINDOW * LANE)], WINDOW * LANE - rest, 1)
+        total = None
+        for r in range(8):
+            first = 7 * PIECE - PIECE * r
+            part = window[r : r + 1, first : first + span]
+            total = part if total is None else total + part
+        out_ref[k : k + 1, :span] = total
+
+
+def pole_rows(where, blocks, cuts):
+    rows, forward, inverse = tables()
+    vmem = pl.BlockSpec(memory_space=pltpu.VMEM)
+    return pl.pallas_call(
+        pole_kernel,
+        out_shape=jax.ShapeDtypeStruct((2, WIDE), jnp.float32),
+        in_specs=[pl.BlockSpec(memory_space=pltpu.SMEM)] + [vmem] * 5,
+        out_specs=vmem,
+        scratch_shapes=[
+            pltpu.VMEM((8, (TILES + 2) * LANE), jnp.float32),
+            pltpu.VMEM((20, 9, 8, LANE), jnp.float32),
+            pltpu.VMEM((8 * COUNT, 2 * LANE), jnp.float32),
+            pltpu.VMEM((8, (AHEAD + TILES + 4) * LANE), jnp.float32),
+            pltpu.VMEM((8, WINDOW * LANE), jnp.float32),
+        ],
+        compiler_params=pltpu.CompilerParams(vmem_limit_bytes=SMALL_GRANT),
+        name="pole_filter",
+    )(where, blocks, cuts, jnp.asarray(rows), jnp.asarray(forward), jnp.asarray(inverse))
+
+
+def add_kernel(mine_ref, theirs_ref, out_ref):
+    out_ref[...] = mine_ref[0:1, :] + theirs_ref[...]
+
+
+def add_halves(mine, theirs):
+    vmem = pl.BlockSpec(memory_space=pltpu.VMEM)
+    return pl.pallas_call(
+        add_kernel,
+        out_shape=jax.ShapeDtypeStruct((1, WIDE), jnp.float32),
+        in_specs=[vmem, vmem],
+        out_specs=vmem,
+        compiler_params=pltpu.CompilerParams(vmem_limit_bytes=SMALL_GRANT),
+        name="pole_sum",
+    )(mine, theirs)
+
+
 def filter_rows(blocks, cuts, early):
     rows, forward, inverse = tables()
     return pl.pallas_call(
@@ -351,43 +431,63 @@
     )(blocks, cuts, jnp.asarray(rows), jnp.asarray(forward), jnp.asarray(inverse), early)
 
 
-def pack_kernel(pieces, winds_ref, layer_ref, tracer_ref, out_ref, buffer, in_sem, out_sem):
+def pack_kernel(north_ref, winds_ref, layer_ref, tracer_ref, out_ref, buffer, last, pole, in_sem, out_sem):
     blocks = layer_ref.shape[0]
-    sources = [(winds_ref, 2 * blocks, 0), (layer_ref, blocks, 2 * blocks), (tracer_ref, blocks, 3 * blocks)]
-    size = 4 * blocks // pieces
-    inward, outward = [], []
-    for ref, count, base in sources:
-        for start in range(0, count, size):
-            index = (base + start) // size
-            here = slice(base + start, base + start + size)
-            inward.append(pltpu.make_async_copy(ref.at[start : start + size], buffer.at[here], in_sem.at[index]))
-            outward.append(pltpu.make_async_copy(buffer.at[here], out_ref.at[here], out_sem.at[index]))
-    for copy in inward:
-        copy.start()
-    for first, then in zip(inward, outward):
-        first.wait()
-        then.start()
+    span = layer_ref.shape[2]
+    whole = span // LANE * LANE
+    sources = [(layer_ref, 0, blocks, 2 * blocks), (winds_ref, 0, blocks, 0), (winds_ref, blocks, blocks, blocks), (tracer_ref, 0, blocks, 3 * blocks)]
+    inward = []
+    for index, (ref, start, count, base) in enumerate(sources):
+        inward.append(pltpu.make_async_copy(ref.at[start : start + count], buffer.at[base : base + count], in_sem.at[index]))
+        inward[-1].start()
+    outward = []
+    for index, (_, _, count, base) in enumerate(sources):
+        inward[index].wait()
+        here = slice(base, base + count)
+        outward.append(pltpu.make_async_copy(buffer.at[here, :, 0:whole], out_ref.at[here, :, 0:whole], out_sem.at[2 * index]))
+        outward[-1].start()
+        if index == 0:
+            row = jnp.where(
+                north_ref[0] > 0, buffer[3 * blocks - 1, 7:8, :], buffer[2 * blocks, 0:1, :]
+            )
+            pole[0:1, 0:span] = row
+            pole[0:1, span:WIDE] = jnp.zeros((1, WIDE - span), jnp.float32)
+            pieces = []
+            for c in range(2):
+                for r in range(8):
+                    first = span // 2 * c + PIECE * r
+                    stop = min(first + PIECE, span // 2 * (c + 1))
+                    pole[8 + 8 * c + r : 9 + 8 * c + r, 0:PIECE] = jnp.zeros((1, PIECE), jnp.float32)
+                    pole[8 + 8 * c + r : 9 + 8 * c + r, 0 : stop - first] = pole[0:1, first:stop]
+                pieces.append(pole[8 + 8 * c : 16 + 8 * c, 0:PIECE])
+        for w in range(base, base + count):
+            last[w, :, 0 : span - whole] = buffer[w, :, whole:span]
+            last[w, :, span - whole : LANE] = pieces[w % 2]
+        outward.append(pltpu.make_async_copy(last.at[here], out_ref.at[here, :, whole:WIDE], out_sem.at[2 * index + 1]))
+        outward[-1].start()
     for copy in outward:
         copy.wait()
 
 
-def pack(winds, thickness, tracer):
+def pack(north, winds, thickness, tracer):
     row_count, width = thickness.shape
     blocks = row_count // 8
-    pieces = 4
     anywhere = pl.BlockSpec(memory_space=pl.ANY)
     return pl.pallas_call(
-        functools.partial(pack_kernel, pieces),
-        out_shape=jax.ShapeDtypeStruct((4 * blocks, 8, width), jnp.float32),
-        in_specs=[anywhere, anywhere, anywhere],
+        pack_kernel,
+        out_shape=jax.ShapeDtypeStruct((4 * blocks, 8, WIDE), jnp.float32),
+        in_specs=[pl.BlockSpec(memory_space=pltpu.SMEM), anywhere, anywhere, anywhere],
         out_specs=anywhere,
         scratch_shapes=[
             pltpu.VMEM((4 * blocks, 8, width), jnp.float32),
-            pltpu.SemaphoreType.DMA((pieces,)),
-            pltpu.SemaphoreType.DMA((pieces,)),
+            pltpu.VMEM((4 * blocks, 8, LANE), jnp.float32),
+            pltpu.VMEM((24, WIDE), jnp.float32),
+            pltpu.SemaphoreType.DMA((4,)),
+            pltpu.SemaphoreType.DMA((8,)),
         ],
         name="pack",
     )(
+        north,
         winds.reshape(2 * blocks, 8, width),
         thickness.reshape(blocks, 8, width),
         tracer.reshape(blocks, 8, width),
@@ -463,7 +563,7 @@
 
 
 def edge_kernel(
-    ratio, even_ref, field_ref, first_ref, second_ref, coef_ref, w_in, l_in, t_in, winds_ref, layer_ref, tracer_ref, out, sem
+    ratio, even_ref, field_ref, first_ref, second_ref, across_ref, coef_ref, w_in, l_in, t_in, winds_ref, layer_ref, tracer_ref, out, sem
 ):
     del w_in, l_in, t_in
     groups = field_ref.shape[0] // 4
@@ -478,6 +578,8 @@
         for f in (1, 2, 3):
             x = field_ref[groups * f + g]
             halo = jnp.where(is_even, near[f - 1 : f, :], far[f - 1 : f, :])
+            if f == 2:
+                halo = jnp.where(even_ref[1] == side + 1, across_ref[...], halo)
             if side == 0:
                 south = jnp.where(sub == 0, halo, pltpu.roll(x, 1, 0))
                 north = jnp.where(sub == 7, pltpu.roll(field_ref[groups * f + g + 1], 7, 0), pltpu.roll(x, 7, 0))
@@ -520,20 +622,20 @@
     )(fields, coef)
 
 
-def stencil_edge(even, fields, first, second, coef, outs, ratio):
+def stencil_edge(even, fields, first, second, across, coef, outs, ratio):
     vmem = pl.BlockSpec(memory_space=pltpu.VMEM)
     anywhere = pl.BlockSpec(memory_space=pl.ANY)
     width = outs[1].shape[1]
     return pl.pallas_call(
         functools.partial(edge_kernel, ratio),
         out_shape=tuple(jax.ShapeDtypeStruct(out.shape, jnp.float32) for out in outs),
-        in_specs=[pl.BlockSpec(memory_space=pltpu.SMEM), vmem, vmem, vmem, vmem, anywhere, anywhere, anywhere],
+        in_specs=[pl.BlockSpec(memory_space=pltpu.SMEM), vmem, vmem, vmem, vmem, vmem, anywhere, anywhere, anywhere],
         out_specs=(anywhere, anywhere, anywhere),
         scratch_shapes=[pltpu.VMEM((2, 3, 8, width), jnp.float32), pltpu.SemaphoreType.DMA((2, 3))],
-        input_output_aliases={5: 0, 6: 1, 7: 2},
+        input_output_aliases={6: 0, 7: 1, 8: 2},
         compiler_params=pltpu.CompilerParams(vmem_limit_bytes=SMALL_GRANT),
         name="stencil_edge",
-    )(even, fields, first, second, coef, *outs)
+    )(even, fields, first, second, across, coef, *outs)
 
 
 def per_device(winds, thickness, tracer, cutoff, damping):
@@ -544,7 +646,8 @@
     row_count, width = thickness.shape
     nlat = row_count * lat_size
 
-    blocks = pack(winds, thickness, tracer)
+    is_north = band == lat_size - 1
+    blocks = pack(is_north.astype(jnp.int32)[None], winds, thickness, tracer)
     owned = lax.all_to_all(blocks, "lon", split_axis=0, concat_axis=0, tiled=True)
 
     is_polar = (band < lat_size // 4) | (band >= lat_size - lat_size // 4)
@@ -571,6 +674,16 @@
 
     filtered = filter_rows(owned, cuts, coef)
     fields = lax.all_to_all(filtered, "lon", split_axis=0, concat_axis=0, tiled=True)
+    core = sector % 2
+    opposite = [(x + lon_size // 2) % lon_size for x in (sector, sector + 1 - 2 * core)]
+    starts = [width * x - (width // 2) * core + LANE * AHEAD - 7 * PIECE for x in opposite]
+    where = jnp.stack([starts[0] // LANE, starts[0] % LANE, starts[1] // LANE, starts[1] % LANE]).astype(jnp.int32)
+    pole_cut = jnp.where(is_north, cutoff[-1], cutoff[0]).astype(jnp.float32)
+    pole_damp = jnp.where(is_north, damping[-1], damping[0])
+    pole_cuts = jnp.broadcast_to(jnp.stack([pole_cut, pole_damp * pole_cut * pole_cut])[None, :], (8, 2))
+    halves = pole_rows(where, owned, pole_cuts)
+    theirs = lax.ppermute(halves[1:2], "lon", [(x, x ^ 1) for x in range(lon_size)])
+    across = add_halves(halves, theirs)
 
     even = band % 2 == 0
     groups = row_count // 8
@@ -580,17 +693,17 @@
     for z in range(lat_size):
         for e in range(lon_size):
             here = z * lon_size + e
-            across = z * lon_size + (e + lon_size // 2) % lon_size
-            up = here + lon_size if z < lat_size - 1 else across
-            down = here - lon_size if z > 0 else across
+            up, down = here + lon_size, here - lon_size
             pairs[0].append((here, up if z % 2 == 0 else down))
-            pairs[1].append((here, down if z % 2 == 0 else up))
+            if 0 < z < lat_size - 1:
+                pairs[1].append((here, down if z % 2 == 0 else up))
     first = lax.ppermute(jnp.where(even, high, low), ("lat", "lon"), pairs[0])
     second = lax.ppermute(jnp.where(even, low, high), ("lat", "lon"), pairs[1])
 
     ratio = lon_step / (2.0 * lat_step)
     outs = stencil_main(fields, coef, ratio, row_count, width)
-    return stencil_edge(even.astype(jnp.int32)[None], fields, first, second, coef, outs, ratio)
+    state = jnp.stack([even.astype(jnp.int32), (band == 0).astype(jnp.int32) + 2 * is_north.astype(jnp.int32)])
+    return stencil_edge(state, fields, first, second, across, coef, outs, ratio)
 
 
 def solution(mesh):

time: 57 us -> 57.3 us (level)
  waiting for transfers between devices: 27.6 us -> 18.3 us
  Pallas kernels: 6.88 us -> 9.72 us
  between operations: 0.79 us -> 3.55 us
  starting transfers between devices: 19.5 us -> 21.6 us
  local copies, waits for them, and re-layouts: 1.52 us -> 2.69 us
    all_to_all x1, waiting for transfers between devices: 14.2 us -> 5.79 us  [per_device(): lax.all_to_all(filtered, 'lon', split_axis=0, concat_axis=0, tiled=True)]
    ppermute x1, starting transfers between devices: 3.11 us -> 0.66 us  [per_device(): second = lax.ppermute(jnp.where(even, low, high), ('lat', 'lon'), pairs[1])]
    ppermute x1, starting transfers between devices: 2.08 us -> 4.53 us  [per_device(): first = lax.ppermute(jnp.where(even, high, low), ('lat', 'lon'), pairs[0])]
    pallas_call x1 -> x3, Pallas kernels: 1.96 us -> 4.27 us  [the longest x1 2.23 us: pole_rows(): pl.pallas_call(pole_kernel, out_shape=jax.ShapeDtypeStruct((2, WIDE), jnp...]
    ppermute x0 -> x1, starting transfers between devices: none -> 2.15 us  [per_device(): lax.ppermute(halves[1:2], 'lon', [(x, x ^ 1) for x in range(lon_size)])]
    slice x0 -> x3, local copies, waits for them, and re-layouts: none -> 1.17 us  [the longest x1 0.58 us: per_device(): pole_damp = jnp.where(is_north, damping[-1], damping[0])]
    ppermute x1, waiting for transfers between devices: 0.85 us -> 0.01 us  [per_device(): first = lax.ppermute(jnp.where(even, high, low), ('lat', 'lon'), pairs[0])]
  transfers between devices with their start and end apart: 4 -> 5, of which waited for: 3 -> 2; matrix products, arithmetic and copies ran while one was open for 1% -> 3% of each run, Pallas kernels for 3% -> 7%
where the time goes in v6:
time: 57.3 us; the launch traced here: 56.5 us
  starting transfers between devices  21.6 us (38%)
  waiting for transfers between devices  18.3 us (32%)
  Pallas kernels  9.72 us (17%)
  between operations  3.55 us (6%)
  local copies, waits for them, and re-layouts  2.69 us (5%)
    all_to_all x1, waiting for transfers between devices, per_device(): lax.all_to_all(blocks, 'lon', split_axis=0, concat_axis=0, tiled=True)  12.5 us
    all_to_all x1, starting transfers between devices, per_device(): lax.all_to_all(blocks, 'lon', split_axis=0, concat_axis=0, tiled=True)  10.5 us
    all_to_all x1, waiting for transfers between devices, per_device(): lax.all_to_all(filtered, 'lon', split_axis=0, concat_axis=0, tiled=True)  5.79 us
    ppermute x1, starting transfers between devices, per_device(): first = lax.ppermute(jnp.where(even, high, low), ('lat', 'lon'), pairs[0])  4.53 us
    all_to_all x1, starting transfers between devices, per_device(): lax.all_to_all(filtered, 'lon', split_axis=0, concat_axis=0, tiled=True)  3.77 us
    pallas_call x1, Pallas kernels, filter_rows(): pl.pallas_call(filter_kernel, out_shape=jax.ShapeDtypeStruct((blocks.shap...  2.58 us
    pallas_call x1, Pallas kernels, pole_rows(): pl.pallas_call(pole_kernel, out_shape=jax.ShapeDtypeStruct((2, WIDE), jnp...  2.23 us
    ppermute x1, starting transfers between devices, per_device(): lax.ppermute(halves[1:2], 'lon', [(x, x ^ 1) for x in range(lon_size)])  2.15 us
  transfers between devices with their start and end apart: 5, of which 2 were waited for; matrix products, arithmetic and copies ran while one was open for 3% of the time, Pallas kernels for 7%

profile of v6, /device:TPU:1, one launch (start us, length us, event | category | flops | bytes accessed | tf_op | source)
XLA Modules:
  0.0 56.5 jit_solution(8067117287521032623)
XLA Ops:
  0.6 2.0 %pack.1 = f32[32,8,768]{2,1,0:T(8,128)} custom-call(s32[1]{0:T(128)} %bitcast.2.north_ref, f32[16,8,720]{2,1,0:T(8,128)} %bitcast.36, f32[8,8,720]{2,1,0:T(8,128)} %bitcast.37, f32[8,8,720]{2,1,0:T(8,128)} %bitcast.38), custom_call_target="tpu_custom_call" | custom-call | tf_op jit(solution)/shard_map/pack/pallas_call | solution.py:476
  2.7 10.5 %all-to-all-start = ((f32[32,8,768]{2,1,0:T(8,128)}), f32[32,8,768]{2,1,0:T(8,128)S(1)}, u32[]{:S(2)}, u32[]{:S(2)}) async-start(f32[32,8,768]{2,1,0:T(8,128)} %pack.1), calls=%async_computation | async-start | bytes 1572864 | tf_op jit(solution)/shard_map/all_to_all | solution.py:651
  13.3 0.6 %copy-done.4 = s32[64]{0:T(128)S(1)} copy-done((s32[64]{0:T(128)S(1)}, s32[64]{0:T(128)}, u32[]{:S(2)}) %copy-start.4) | copy-done | bytes 280
  14.0 0.7 %copy-done.3 = f32[64]{0:T(128)S(1)} copy-done((f32[64]{0:T(128)S(1)}, f32[64]{0:T(128)}, u32[]{:S(2)}) %copy-start.3) | copy-done | bytes 280
  14.6 0.1 fusion.3
  14.7 0.1 copy.18.cut_ref
  14.8 0.1 cosine_divide_fusion
  14.9 0.1 multiply_bitcast_fusion.1
  15.0 0.1 copy.19.early_ref.coef_ref
  15.1 12.5 %all-to-all-done.x_ref = f32[32,8,768]{2,1,0:T(8,128)S(1)} async-done(((f32[32,8,768]{2,1,0:T(8,128)}), f32[32,8,768]{2,1,0:T(8,128)S(1)}, u32[]{:S(2)}, u32[]{:S(2)}) %all-to-all-start) | async-done | bytes 786464 | tf_op jit(solution)/shard_map/all_to_all | solution.py:651
  27.6 2.6 %polar_filter.1 = f32[32,8,768]{2,1,0:T(8,128)} custom-call(f32[32,8,768]{2,1,0:T(8,128)S(1)} %all-to-all-done.x_ref, f32[8,2]{1,0:T(8,128)S(1)} %copy.18.cut_ref, f32[4,91,128]{2,1,0:T(8,128)S(1)} %copy-done.2, bf16[768,256]{1,0:T(8,128)(2,1)S(1)} %copy-done.1, bf16[768,256]{1,0:T(8,128)(2,1)S(1)} %copy-done, f32[64,4]{1,0:T(8,128)S(1)} %copy.19.early_ref.coef_ref), custom_call_target="tpu_custom_call" | custom-call | tf_op jit(solution)/shard_map/polar_filter/pallas_call | solution.py:417
  30.2 3.8 %all-to-all-start.1 = ((f32[32,8,768]{2,1,0:T(8,128)}), f32[32,8,768]{2,1,0:T(8,128)S(1)}, u32[]{:S(2)}, u32[]{:S(2)}) async-start(f32[32,8,768]{2,1,0:T(8,128)} %polar_filter.1), calls=%async_computation.1 | async-start | bytes 1572864 | tf_op jit(solution)/shard_map/all_to_all | solution.py:676
  34.1 0.6 %fusion.4 = (s32[1]{0:T(128)}, s32[1]{0:T(128)}) fusion(s32[64]{0:T(128)S(1)} %copy-done.4), kind=kLoop, calls=%fused_computation.25 | loop fusion | bytes 16 | tf_op jit(solution)/shard_map/slice | solution.py:681
  36.0 0.6 %fusion.5 = (f32[1]{0:T(128)}, f32[1]{0:T(128)}) fusion(f32[64]{0:T(128)S(1)} %copy-done.3), kind=kLoop, calls=%fused_computation.26 | loop fusion | bytes 16 | tf_op jit(solution)/shard_map/slice | solution.py:682
  37.9 0.1 pad_maximum_fusion.4
  38.0 0.1 pad_add_fusion.1.where_ref
  38.0 2.2 %pole_filter.1.mine_ref = f32[2,768]{1,0:T(2,128)S(1)} custom-call(s32[4]{0:T(128)S(1)} %pad_add_fusion.1.where_ref, f32[32,8,768]{2,1,0:T(8,128)S(1)} %all-to-all-done.x_ref, f32[8,2]{1,0:T(8,128)S(1)} %broadcast_in_dim.23.cut_ref, f32[4,91,128]{2,1,0:T(8,128)S(1)} %copy-done.2, bf16[768,256]{1,0:T(8,128)(2,1)S(1)} %copy-done.1, bf16[768,256]{1,0:T(8,128)(2,1)S(1)} %copy-done), custom_call_target="tpu_custom_call" | custom-call | tf_op jit(solution)/shard_map/pole_filter/pallas_call | solution.py:382
  40.3 2.1 %collective-permute-start.2 = (f32[1,768]{1,0:T(1,128)S(1)}, f32[1,768]{1,0:T(1,128)S(1)}, u32[]{:S(2)}, u32[]{:S(2)}) collective-permute-start(f32[1,768]{1,0:T(1,128)S(1)} %slice.58), channel_id=1, source_target_pairs={{0,1},{1,0},{2,3},{3,2},{4,5},{5,4},{6,7},{7,6},{8,9},{9,8},{10,11... | collective-permute-start | bytes 9224 | tf_op jit(solution)/shard_map/ppermute | solution.py:685
  42.4 5.8 %all-to-all-done.1.field_ref = f32[32,8,768]{2,1,0:T(8,128)S(1)} async-done(((f32[32,8,768]{2,1,0:T(8,128)}), f32[32,8,768]{2,1,0:T(8,128)S(1)}, u32[]{:S(2)}, u32[]{:S(2)}) %all-to-all-start.1) | async-done | bytes 786464 | tf_op jit(solution)/shard_map/all_to_all | solution.py:676
  48.3 0.7 %collective-permute-start.1 = (f32[3,768]{1,0:T(4,128)S(1)}, f32[3,768]{1,0:T(4,128)S(1)}, u32[]{:S(2)}, u32[]{:S(2)}) collective-permute-start(f32[3,768]{1,0:T(4,128)S(1)} %get-tuple-element.15), channel_id=1, source_target_pairs={{32,64},{33,65},{34,66},{35,67},{36,68},{37,69},{38,70},{39,71},{4... | collective-permute-start | bytes 27656 | tf_op jit(solution)/shard_map/ppermute | solution.py:701
  48.9 4.5 %collective-permute-start = (f32[3,768]{1,0:T(4,128)S(1)}, f32[3,768]{1,0:T(4,128)S(1)}, u32[]{:S(2)}, u32[]{:S(2)}) collective-permute-start(f32[3,768]{1,0:T(4,128)S(1)} %get-tuple-element.16), channel_id=1, source_target_pairs={{0,32},{1,33},{2,34},{3,35},{4,36},{5,37},{6,38},{7,39},{8,40},{9,... | collective-permute-start | bytes 27656 | tf_op jit(solution)/shard_map/ppermute | solution.py:700
  53.5 0.1 pad_add_fusion.even_ref
  53.6 1.5 %stencil_main.1 = (f32[2,64,720]{2,1,0:T(8,128)}, f32[64,720]{1,0:T(8,128)}, f32[64,720]{1,0:T(8,128)}) custom-call(f32[32,8,768]{2,1,0:T(8,128)S(1)} %all-to-all-done.1.field_ref, f32[64,4]{1,0:T(8,128)S(1)} %copy.19.early_ref.coef_ref), custom_call_target="tpu_custom_call" | custom-call | flops 10000000 | bytes 1600000 | tf_op jit(solution)/shard_map/stencil_main/pallas_call | solution.py:606
  55.1 1.4 %stencil_edge.1 = (f32[2,64,720]{2,1,0:T(8,128)}, f32[64,720]{1,0:T(8,128)}, f32[64,720]{1,0:T(8,128)}) custom-call(s32[2]{0:T(128)S(1)} %pad_add_fusion.even_ref, f32[32,8,768]{2,1,0:T(8,128)S(1)} %all-to-all-done.1.field_ref, f32[3,768]{1,0:T(4,128)S(1)} %collective-permute-done.first_ref, ...), custom_call_target="tpu_custom_call", output_to_operand_aliasing={{0}: (6, {}), {1}: (7, {}), {2}: (8, {})} | custom-call | tf_op jit(solution)/shard_map/stencil_edge/pallas_call | solution.py:629
  (20 shorter events, 0.2 us)
Async XLA Ops:
  2.7 24.9 %copy-start = (bf16[768,256]{1,0:T(8,128)(2,1)S(1)}, bf16[768,256]{1,0:T(8,128)(2,1)}, u32[]{:S(2)}) copy-start(bf16[768,256]{1,0:T(8,128)(2,1)} %constant.135.clone.inverse_ref) | copy-start | bytes 1179652
  2.7 24.9 %copy-start.1 = (bf16[768,256]{1,0:T(8,128)(2,1)S(1)}, bf16[768,256]{1,0:T(8,128)(2,1)}, u32[]{:S(2)}) copy-start(bf16[768,256]{1,0:T(8,128)(2,1)} %constant.134.clone.forward_ref) | copy-start | bytes 1179652
  2.7 24.9 %copy-start.2 = (f32[4,91,128]{2,1,0:T(8,128)S(1)}, f32[4,91,128]{2,1,0:T(8,128)}, u32[]{:S(2)}) copy-start(f32[4,91,128]{2,1,0:T(8,128)} %constant.133.clone.rows_ref) | copy-start | bytes 559108
  2.7 24.9 %all-to-all-start = ((f32[32,8,768]{2,1,0:T(8,128)}), f32[32,8,768]{2,1,0:T(8,128)S(1)}, u32[]{:S(2)}, u32[]{:S(2)}) async-start(f32[32,8,768]{2,1,0:T(8,128)} %pack.1), calls=%async_computation | async-start | bytes 1572864 | tf_op jit(solution)/shard_map/all_to_all | solution.py:651
  13.3 0.7 %copy-start.4 = (s32[64]{0:T(128)S(1)}, s32[64]{0:T(128)}, u32[]{:S(2)}) copy-start(s32[64]{0:T(128)} %param.11) | copy-start | bytes 772
  14.0 0.7 %copy-start.3 = (f32[64]{0:T(128)S(1)}, f32[64]{0:T(128)}, u32[]{:S(2)}) copy-start(f32[64]{0:T(128)} %param.12) | copy-start | bytes 772
  30.2 18.0 %all-to-all-start.1 = ((f32[32,8,768]{2,1,0:T(8,128)}), f32[32,8,768]{2,1,0:T(8,128)S(1)}, u32[]{:S(2)}, u32[]{:S(2)}) async-start(f32[32,8,768]{2,1,0:T(8,128)} %polar_filter.1), calls=%async_computation.1 | async-start | bytes 1572864 | tf_op jit(solution)/shard_map/all_to_all | solution.py:676
  40.3 13.3 %collective-permute-start.2 = (f32[1,768]{1,0:T(1,128)S(1)}, f32[1,768]{1,0:T(1,128)S(1)}, u32[]{:S(2)}, u32[]{:S(2)}) collective-permute-start(f32[1,768]{1,0:T(1,128)S(1)} %slice.58), channel_id=1, source_target_pairs={{0,1},{1,0},{2,3},{3,2},{4,5},{5,4},{6,7},{7,6},{8,9},{9,8},{10,11... | collective-permute-start | bytes 9224 | tf_op jit(solution)/shard_map/ppermute | solution.py:685
  48.3 6.8 %collective-permute-start.1 = (f32[3,768]{1,0:T(4,128)S(1)}, f32[3,768]{1,0:T(4,128)S(1)}, u32[]{:S(2)}, u32[]{:S(2)}) collective-permute-start(f32[3,768]{1,0:T(4,128)S(1)} %get-tuple-element.15), channel_id=1, source_target_pairs={{32,64},{33,65},{34,66},{35,67},{36,68},{37,69},{38,70},{39,71},{4... | collective-permute-start | bytes 27656 | tf_op jit(solution)/shard_map/ppermute | solution.py:701
  48.9 6.1 %collective-permute-start = (f32[3,768]{1,0:T(4,128)S(1)}, f32[3,768]{1,0:T(4,128)S(1)}, u32[]{:S(2)}, u32[]{:S(2)}) collective-permute-start(f32[3,768]{1,0:T(4,128)S(1)} %get-tuple-element.16), channel_id=1, source_target_pairs={{0,32},{1,33},{2,34},{3,35},{4,36},{5,37},{6,38},{7,39},{8,40},{9,... | collective-permute-start | bytes 27656 | tf_op jit(solution)/shard_map/ppermute | solution.py:700

commit v7 on v6

--- a/solution.py
+++ b/solution.py
@@ -563,11 +563,12 @@
 
 
 def edge_kernel(
-    ratio, even_ref, field_ref, first_ref, second_ref, across_ref, coef_ref, w_in, l_in, t_in, winds_ref, layer_ref, tracer_ref, out, sem
+    ratio, state_ref, field_ref, second_ref, first_ref, across_ref, coef_ref, w_in, l_in, t_in, winds_ref, layer_ref, tracer_ref, out, sem
 ):
     del w_in, l_in, t_in
     groups = field_ref.shape[0] // 4
-    is_even = even_ref[0] > 0
+    is_even = state_ref[0] % 2 > 0
+    pole = state_ref[0] // 2
     span = layer_ref.shape[1]
     sub = lax.broadcasted_iota(jnp.int32, (8, WIDE), 0)
     writes = []
@@ -579,7 +580,7 @@
             x = field_ref[groups * f + g]
             halo = jnp.where(is_even, near[f - 1 : f, :], far[f - 1 : f, :])
             if f == 2:
-                halo = jnp.where(even_ref[1] == side + 1, across_ref[...], halo)
+                halo = jnp.where(pole == side + 1, across_ref[...], halo)
             if side == 0:
                 south = jnp.where(sub == 0, halo, pltpu.roll(x, 1, 0))
                 north = jnp.where(sub == 7, pltpu.roll(field_ref[groups * f + g + 1], 7, 0), pltpu.roll(x, 7, 0))
@@ -622,7 +623,7 @@
     )(fields, coef)
 
 
-def stencil_edge(even, fields, first, second, across, coef, outs, ratio):
+def stencil_edge(state, fields, first, second, across, coef, outs, ratio):
     vmem = pl.BlockSpec(memory_space=pltpu.VMEM)
     anywhere = pl.BlockSpec(memory_space=pl.ANY)
     width = outs[1].shape[1]
@@ -635,7 +636,7 @@
         input_output_aliases={6: 0, 7: 1, 8: 2},
         compiler_params=pltpu.CompilerParams(vmem_limit_bytes=SMALL_GRANT),
         name="stencil_edge",
-    )(even, fields, first, second, across, coef, *outs)
+    )(state, fields, second, first, across, coef, *outs)
 
 
 def per_device(winds, thickness, tracer, cutoff, damping):
@@ -702,8 +703,8 @@
 
     ratio = lon_step / (2.0 * lat_step)
     outs = stencil_main(fields, coef, ratio, row_count, width)
-    state = jnp.stack([even.astype(jnp.int32), (band == 0).astype(jnp.int32) + 2 * is_north.astype(jnp.int32)])
-    return stencil_edge(state, fields, first, second, across, coef, outs, ratio)
+    state = even.astype(jnp.int32) + 2 * (band == 0).astype(jnp.int32) + 4 * is_north.astype(jnp.int32)
+    return stencil_edge(state[None], fields, first, second, across, coef, outs, ratio)
 
 
 def solution(mesh):

time: 57.3 us -> 62.2 us (1.086)
  the two profiles are of different devices: /device:TPU:1 before, /device:TPU:97 now
where the time goes in v7:
time: 62.2 us; the launch traced here: 61.8 us
  waiting for transfers between devices  23.5 us (38%)
  starting transfers between devices  22.4 us (36%)
  Pallas kernels  9.18 us (15%)
  between operations  3.55 us (6%)
  local copies, waits for them, and re-layouts  2.69 us (4%)
    all_to_all x1, waiting for transfers between devices, per_device(): lax.all_to_all(blocks, 'lon', split_axis=0, concat_axis=0, tiled=True)  12.4 us
    all_to_all x1, waiting for transfers between devices, per_device(): lax.all_to_all(filtered, 'lon', split_axis=0, concat_axis=0, tiled=True)  10.3 us
    all_to_all x1, starting transfers between devices, per_device(): lax.all_to_all(blocks, 'lon', split_axis=0, concat_axis=0, tiled=True)  7.9 us
    ppermute x1, starting transfers between devices, per_device(): second = lax.ppermute(jnp.where(even, low, high), ('lat', 'lon'), pairs[1])  6.38 us
    all_to_all x1, starting transfers between devices, per_device(): lax.all_to_all(filtered, 'lon', split_axis=0, concat_axis=0, tiled=True)  3.8 us
    pallas_call x1, Pallas kernels, filter_rows(): pl.pallas_call(filter_kernel, out_shape=jax.ShapeDtypeStruct((blocks.shap...  2.57 us
    ppermute x1, starting transfers between devices, per_device(): lax.ppermute(halves[1:2], 'lon', [(x, x ^ 1) for x in range(lon_size)])  2.39 us
    pallas_call x1, Pallas kernels, pole_rows(): pl.pallas_call(pole_kernel, out_shape=jax.ShapeDtypeStruct((2, WIDE), jnp...  2.23 us
  transfers between devices with their start and end apart: 5, of which 3 were waited for; matrix products, arithmetic and copies ran while one was open for 3% of the time, Pallas kernels for 6%

profile of v7, /device:TPU:97, one launch (start us, length us, event | category | flops | bytes accessed | tf_op | source)
XLA Modules:
  0.0 61.8 jit_solution(14086123503319781347)
XLA Ops:
  0.6 2.0 %pack.1 = f32[32,8,768]{2,1,0:T(8,128)} custom-call(s32[1]{0:T(128)} %bitcast.1.north_ref, f32[16,8,720]{2,1,0:T(8,128)} %bitcast.35, f32[8,8,720]{2,1,0:T(8,128)} %bitcast.36, f32[8,8,720]{2,1,0:T(8,128)} %bitcast.37), custom_call_target="tpu_custom_call" | custom-call | tf_op jit(solution)/shard_map/pack/pallas_call | solution.py:476
  2.7 7.9 %all-to-all-start = ((f32[32,8,768]{2,1,0:T(8,128)}), f32[32,8,768]{2,1,0:T(8,128)S(1)}, u32[]{:S(2)}, u32[]{:S(2)}) async-start(f32[32,8,768]{2,1,0:T(8,128)} %pack.1), calls=%async_computation | async-start | bytes 1572864 | tf_op jit(solution)/shard_map/all_to_all | solution.py:652
  10.7 0.6 %copy-done.4 = s32[64]{0:T(128)S(1)} copy-done((s32[64]{0:T(128)S(1)}, s32[64]{0:T(128)}, u32[]{:S(2)}) %copy-start.4) | copy-done | bytes 280
  11.3 0.7 %copy-done.3 = f32[64]{0:T(128)S(1)} copy-done((f32[64]{0:T(128)S(1)}, f32[64]{0:T(128)}, u32[]{:S(2)}) %copy-start.3) | copy-done | bytes 280
  12.0 0.1 fusion.3
  12.1 0.1 copy.18.cut_ref
  12.2 0.1 cosine_divide_fusion
  12.3 0.1 multiply_bitcast_fusion.1
  12.3 0.1 copy.19.early_ref.coef_ref
  12.4 12.4 %all-to-all-done.x_ref = f32[32,8,768]{2,1,0:T(8,128)S(1)} async-done(((f32[32,8,768]{2,1,0:T(8,128)}), f32[32,8,768]{2,1,0:T(8,128)S(1)}, u32[]{:S(2)}, u32[]{:S(2)}) %all-to-all-start) | async-done | bytes 786464 | tf_op jit(solution)/shard_map/all_to_all | solution.py:652
  24.9 2.6 %polar_filter.1 = f32[32,8,768]{2,1,0:T(8,128)} custom-call(f32[32,8,768]{2,1,0:T(8,128)S(1)} %all-to-all-done.x_ref, f32[8,2]{1,0:T(8,128)S(1)} %copy.18.cut_ref, f32[4,91,128]{2,1,0:T(8,128)S(1)} %copy-done.2, bf16[768,256]{1,0:T(8,128)(2,1)S(1)} %copy-done.1, bf16[768,256]{1,0:T(8,128)(2,1)S(1)} %copy-done, f32[64,4]{1,0:T(8,128)S(1)} %copy.19.early_ref.coef_ref), custom_call_target="tpu_custom_call" | custom-call | tf_op jit(solution)/shard_map/polar_filter/pallas_call | solution.py:417
  27.5 3.8 %all-to-all-start.1 = ((f32[32,8,768]{2,1,0:T(8,128)}), f32[32,8,768]{2,1,0:T(8,128)S(1)}, u32[]{:S(2)}, u32[]{:S(2)}) async-start(f32[32,8,768]{2,1,0:T(8,128)} %polar_filter.1), calls=%async_computation.1 | async-start | bytes 1572864 | tf_op jit(solution)/shard_map/all_to_all | solution.py:677
  31.4 0.6 fusion.4
  33.2 0.6 fusion.5
  35.2 0.1 pad_maximum_fusion.4
  35.2 10.3 %all-to-all-done.1.field_ref = f32[32,8,768]{2,1,0:T(8,128)S(1)} async-done(((f32[32,8,768]{2,1,0:T(8,128)}), f32[32,8,768]{2,1,0:T(8,128)S(1)}, u32[]{:S(2)}, u32[]{:S(2)}) %all-to-all-start.1) | async-done | bytes 786464 | tf_op jit(solution)/shard_map/all_to_all | solution.py:677
  45.6 1.9 %collective-permute-start.1 = (f32[3,768]{1,0:T(4,128)S(1)}, f32[3,768]{1,0:T(4,128)S(1)}, u32[]{:S(2)}, u32[]{:S(2)}) collective-permute-start(f32[3,768]{1,0:T(4,128)S(1)} %get-tuple-element.15), channel_id=1, source_target_pairs={{0,32},{1,33},{2,34},{3,35},{4,36},{5,37},{6,38},{7,39},{8,40},{9,... | collective-permute-start | bytes 27656 | tf_op jit(solution)/shard_map/ppermute | solution.py:701
  47.5 6.4 %collective-permute-start = (f32[3,768]{1,0:T(4,128)S(1)}, f32[3,768]{1,0:T(4,128)S(1)}, u32[]{:S(2)}, u32[]{:S(2)}) collective-permute-start(f32[3,768]{1,0:T(4,128)S(1)} %get-tuple-element.16), channel_id=1, source_target_pairs={{32,64},{33,65},{34,66},{35,67},{36,68},{37,69},{38,70},{39,71},{4... | collective-permute-start | bytes 27656 | tf_op jit(solution)/shard_map/ppermute | solution.py:702
  53.9 0.1 pad_add_fusion.where_ref
  54.0 2.2 %pole_filter.1.mine_ref = f32[2,768]{1,0:T(2,128)S(1)} custom-call(s32[4]{0:T(128)S(1)} %pad_add_fusion.where_ref, f32[32,8,768]{2,1,0:T(8,128)S(1)} %all-to-all-done.x_ref, f32[8,2]{1,0:T(8,128)S(1)} %broadcast_in_dim.27.cut_ref, f32[4,91,128]{2,1,0:T(8,128)S(1)} %copy-done.2, bf16[768,256]{1,0:T(8,128)(2,1)S(1)} %copy-done.1, bf16[768,256]{1,0:T(8,128)(2,1)S(1)} %copy-done), custom_call_target="tpu_custom_call" | custom-call | tf_op jit(solution)/shard_map/pole_filter/pallas_call | solution.py:382
  56.2 2.4 %collective-permute-start.2 = (f32[1,768]{1,0:T(1,128)S(1)}, f32[1,768]{1,0:T(1,128)S(1)}, u32[]{:S(2)}, u32[]{:S(2)}) collective-permute-start(f32[1,768]{1,0:T(1,128)S(1)} %slice.58), channel_id=1, source_target_pairs={{0,1},{1,0},{2,3},{3,2},{4,5},{5,4},{6,7},{7,6},{8,9},{9,8},{10,11... | collective-permute-start | bytes 9224 | tf_op jit(solution)/shard_map/ppermute | solution.py:686
  58.6 0.8 %collective-permute-done.2.theirs_ref = f32[1,768]{1,0:T(1,128)S(1)} collective-permute-done((f32[1,768]{1,0:T(1,128)S(1)}, f32[1,768]{1,0:T(1,128)S(1)}, u32[]{:S(2)}, u32[]{:S(2)}) %collective-permute-start.2) | collective-permute-done | bytes 3104 | tf_op jit(solution)/shard_map/ppermute | solution.py:686
  59.4 1.5 %stencil_main.1 = (f32[2,64,720]{2,1,0:T(8,128)}, f32[64,720]{1,0:T(8,128)}, f32[64,720]{1,0:T(8,128)}) custom-call(f32[32,8,768]{2,1,0:T(8,128)S(1)} %all-to-all-done.1.field_ref, f32[64,4]{1,0:T(8,128)S(1)} %copy.19.early_ref.coef_ref), custom_call_target="tpu_custom_call" | custom-call | flops 10000000 | bytes 1600000 | tf_op jit(solution)/shard_map/stencil_main/pallas_call | solution.py:607
  60.9 0.9 %stencil_edge.1 = (f32[2,64,720]{2,1,0:T(8,128)}, f32[64,720]{1,0:T(8,128)}, f32[64,720]{1,0:T(8,128)}) custom-call(s32[1]{0:T(128)} %bitcast.state_ref, f32[32,8,768]{2,1,0:T(8,128)S(1)} %all-to-all-done.1.field_ref, f32[3,768]{1,0:T(4,128)S(1)} %collective-permute-done.second_ref, ...), custom_call_target="tpu_custom_call", output_to_operand_aliasing={{0}: (6, {}), {1}: (7, {}), {2}: (8, {})} | custom-call | tf_op jit(solution)/shard_map/stencil_edge/pallas_call | solution.py:630
  (19 shorter events, 0.2 us)
Async XLA Ops:
  2.7 22.2 %copy-start = (bf16[768,256]{1,0:T(8,128)(2,1)S(1)}, bf16[768,256]{1,0:T(8,128)(2,1)}, u32[]{:S(2)}) copy-start(bf16[768,256]{1,0:T(8,128)(2,1)} %constant.136.clone.inverse_ref) | copy-start | bytes 1179652
  2.7 22.2 %copy-start.1 = (bf16[768,256]{1,0:T(8,128)(2,1)S(1)}, bf16[768,256]{1,0:T(8,128)(2,1)}, u32[]{:S(2)}) copy-start(bf16[768,256]{1,0:T(8,128)(2,1)} %constant.135.clone.forward_ref) | copy-start | bytes 1179652
  2.7 22.2 %copy-start.2 = (f32[4,91,128]{2,1,0:T(8,128)S(1)}, f32[4,91,128]{2,1,0:T(8,128)}, u32[]{:S(2)}) copy-start(f32[4,91,128]{2,1,0:T(8,128)} %constant.134.clone.rows_ref) | copy-start | bytes 559108
  2.7 22.1 %all-to-all-start = ((f32[32,8,768]{2,1,0:T(8,128)}), f32[32,8,768]{2,1,0:T(8,128)S(1)}, u32[]{:S(2)}, u32[]{:S(2)}) async-start(f32[32,8,768]{2,1,0:T(8,128)} %pack.1), calls=%async_computation | async-start | bytes 1572864 | tf_op jit(solution)/shard_map/all_to_all | solution.py:652
  10.7 0.7 %copy-start.4 = (s32[64]{0:T(128)S(1)}, s32[64]{0:T(128)}, u32[]{:S(2)}) copy-start(s32[64]{0:T(128)} %param.11) | copy-start | bytes 772
  11.3 0.7 %copy-start.3 = (f32[64]{0:T(128)S(1)}, f32[64]{0:T(128)}, u32[]{:S(2)}) copy-start(f32[64]{0:T(128)} %param.12) | copy-start | bytes 772
  27.5 18.0 %all-to-all-start.1 = ((f32[32,8,768]{2,1,0:T(8,128)}), f32[32,8,768]{2,1,0:T(8,128)S(1)}, u32[]{:S(2)}, u32[]{:S(2)}) async-start(f32[32,8,768]{2,1,0:T(8,128)} %polar_filter.1), calls=%async_computation.1 | async-start | bytes 1572864 | tf_op jit(solution)/shard_map/all_to_all | solution.py:677
  45.6 15.3 %collective-permute-start.1 = (f32[3,768]{1,0:T(4,128)S(1)}, f32[3,768]{1,0:T(4,128)S(1)}, u32[]{:S(2)}, u32[]{:S(2)}) collective-permute-start(f32[3,768]{1,0:T(4,128)S(1)} %get-tuple-element.15), channel_id=1, source_target_pairs={{0,32},{1,33},{2,34},{3,35},{4,36},{5,37},{6,38},{7,39},{8,40},{9,... | collective-permute-start | bytes 27656 | tf_op jit(solution)/shard_map/ppermute | solution.py:701
  47.5 13.4 %collective-permute-start = (f32[3,768]{1,0:T(4,128)S(1)}, f32[3,768]{1,0:T(4,128)S(1)}, u32[]{:S(2)}, u32[]{:S(2)}) collective-permute-start(f32[3,768]{1,0:T(4,128)S(1)} %get-tuple-element.16), channel_id=1, source_target_pairs={{32,64},{33,65},{34,66},{35,67},{36,68},{37,69},{38,70},{39,71},{4... | collective-permute-start | bytes 27656 | tf_op jit(solution)/shard_map/ppermute | solution.py:702
  56.2 3.2 %collective-permute-start.2 = (f32[1,768]{1,0:T(1,128)S(1)}, f32[1,768]{1,0:T(1,128)S(1)}, u32[]{:S(2)}, u32[]{:S(2)}) collective-permute-start(f32[1,768]{1,0:T(1,128)S(1)} %slice.58), channel_id=1, source_target_pairs={{0,1},{1,0},{2,3},{3,2},{4,5},{5,4},{6,7},{7,6},{8,9},{9,8},{10,11... | collective-permute-start | bytes 9224 | tf_op jit(solution)/shard_map/ppermute | solution.py:686

commit v8 on v7

--- a/solution.py
+++ b/solution.py
@@ -15,7 +15,7 @@
 LANE = 128
 TILES = NLON * LEV // LANE
 STEP = LANE // LEV
-BATCH = 4
+BATCH = 2
 SMALL_GRANT = 12 << 20
 WIDE = 768
 
@@ -179,7 +179,7 @@
 
 
 ALL_CLASSES = [(0, 0), (2, 0)] + COMPLEX_CLASSES
-CLASS_CUTS = (0, 4, 6, 8, 11)
+CLASS_CUTS = (0, 3, 5, 7, 9, 11)
 CLASS_GROUPS = [ALL_CLASSES[first:last] for first, last in zip(CLASS_CUTS[:-1], CLASS_CUTS[1:])]
 
 
@@ -322,7 +322,6 @@
         return x_ref[d, :, LANE * t : LANE * (t + 1)]
 
     circle_filter(source_tile, span, cut_ref, rows_ref, forward_ref, inverse_ref, full, mid, stage)
-    writes = []
     for d in range(sectors):
         first, shift = divmod(LANE + d * span, LANE)
         pieces = []
@@ -337,10 +336,8 @@
             result[d, :, LANE * t : LANE * (t + 1)] = value
         if d % BATCH == BATCH - 1:
             here = slice(d + 1 - BATCH, d + 1)
-            writes.append(pltpu.make_async_copy(result.at[here], out_ref.at[here], sem.at[d // BATCH]))
-            writes[-1].start()
-    for write in writes:
-        write.wait()
+            pltpu.make_async_copy(result.at[here], out_ref.at[here], sem).start()
+    pltpu.make_async_copy(result, out_ref, sem).wait()
 
 
 PIECE = 48
@@ -424,7 +421,7 @@
             pltpu.VMEM((20, 9, 8, LANE), jnp.float32),
             pltpu.VMEM((8 * COUNT, 2 * LANE), jnp.float32),
             pltpu.VMEM((blocks.shape[0], 8, WIDE), jnp.float32),
-            pltpu.SemaphoreType.DMA((blocks.shape[0] // BATCH,)),
+            pltpu.SemaphoreType.DMA,
         ],
         compiler_params=pltpu.CompilerParams(vmem_limit_bytes=SMALL_GRANT),
         name="polar_filter",
@@ -440,12 +437,10 @@
     for index, (ref, start, count, base) in enumerate(sources):
         inward.append(pltpu.make_async_copy(ref.at[start : start + count], buffer.at[base : base + count], in_sem.at[index]))
         inward[-1].start()
-    outward = []
     for index, (_, _, count, base) in enumerate(sources):
         inward[index].wait()
         here = slice(base, base + count)
-        outward.append(pltpu.make_async_copy(buffer.at[here, :, 0:whole], out_ref.at[here, :, 0:whole], out_sem.at[2 * index]))
-        outward[-1].start()
+        pltpu.make_async_copy(buffer.at[here, :, 0:whole], out_ref.at[here, :, 0:whole], out_sem.at[0]).start()
         if index == 0:
             row = jnp.where(
                 north_ref[0] > 0, buffer[3 * blocks - 1, 7:8, :], buffer[2 * blocks, 0:1, :]
@@ -463,10 +458,9 @@
         for w in range(base, base + count):
             last[w, :, 0 : span - whole] = buffer[w, :, whole:span]
             last[w, :, span - whole : LANE] = pieces[w % 2]
-        outward.append(pltpu.make_async_copy(last.at[here], out_ref.at[here, :, whole:WIDE], out_sem.at[2 * index + 1]))
-        outward[-1].start()
-    for copy in outward:
-        copy.wait()
+        pltpu.make_async_copy(last.at[here], out_ref.at[here, :, whole:WIDE], out_sem.at[1]).start()
+    pltpu.make_async_copy(buffer.at[:, :, 0:whole], out_ref.at[:, :, 0:whole], out_sem.at[0]).wait()
+    pltpu.make_async_copy(last, out_ref.at[:, :, whole:WIDE], out_sem.at[1]).wait()
 
 
 def pack(north, winds, thickness, tracer):
@@ -483,7 +477,7 @@
             pltpu.VMEM((4 * blocks, 8, LANE), jnp.float32),
             pltpu.VMEM((24, WIDE), jnp.float32),
             pltpu.SemaphoreType.DMA((4,)),
-            pltpu.SemaphoreType.DMA((8,)),
+            pltpu.SemaphoreType.DMA((2,)),
         ],
         name="pack",
     )(
@@ -571,7 +565,6 @@
     pole = state_ref[0] // 2
     span = layer_ref.shape[1]
     sub = lax.broadcasted_iota(jnp.int32, (8, WIDE), 0)
-    writes = []
     for side, g in enumerate((0, groups - 1)):
         rows = slice(8 * g, 8 * g + 8)
         near, far = (second_ref, first_ref) if side == 0 else (first_ref, second_ref)
@@ -594,11 +587,10 @@
         for k, (value, target) in enumerate(
             ((new_v, winds_ref.at[1, rows]), (new_h, layer_ref.at[rows]), (new_q, tracer_ref.at[rows]))
         ):
-            out[side, k] = value[:, :span]
-            writes.append(pltpu.make_async_copy(out.at[side, k], target, sem.at[side, k]))
-            writes[-1].start()
-    for write in writes:
-        write.wait()
+            piece = slice(8 * (3 * side + k), 8 * (3 * side + k) + 8)
+            out[piece, :] = value[:, :span]
+            pltpu.make_async_copy(out.at[piece], target, sem).start()
+    pltpu.make_async_copy(out, winds_ref.at[1, 0 : out.shape[0]], sem).wait()
 
 
 def stencil_main(fields, coef, ratio, row_count, width):
@@ -632,7 +624,7 @@
         out_shape=tuple(jax.ShapeDtypeStruct(out.shape, jnp.float32) for out in outs),
         in_specs=[pl.BlockSpec(memory_space=pltpu.SMEM), vmem, vmem, vmem, vmem, vmem, anywhere, anywhere, anywhere],
         out_specs=(anywhere, anywhere, anywhere),
-        scratch_shapes=[pltpu.VMEM((2, 3, 8, width), jnp.float32), pltpu.SemaphoreType.DMA((2, 3))],
+        scratch_shapes=[pltpu.VMEM((48, width), jnp.float32), pltpu.SemaphoreType.DMA],
         input_output_aliases={6: 0, 7: 1, 8: 2},
         compiler_params=pltpu.CompilerParams(vmem_limit_bytes=SMALL_GRANT),
         name="stencil_edge",

time: 62.2 us -> 62 us (level)
  no operation moved by 1% of the time
where the time goes in v8:
time: 62 us; the launch traced here: 61.5 us
  waiting for transfers between devices  23.5 us (38%)
  starting transfers between devices  22.4 us (36%)
  Pallas kernels  8.97 us (14%)
  between operations  3.55 us (6%)
  local copies, waits for them, and re-layouts  2.69 us (4%)
    all_to_all x1, waiting for transfers between devices, per_device(): lax.all_to_all(blocks, 'lon', split_axis=0, concat_axis=0, tiled=True)  12.4 us
    all_to_all x1, waiting for transfers between devices, per_device(): lax.all_to_all(filtered, 'lon', split_axis=0, concat_axis=0, tiled=True)  10.3 us
    all_to_all x1, starting transfers between devices, per_device(): lax.all_to_all(blocks, 'lon', split_axis=0, concat_axis=0, tiled=True)  7.9 us
    ppermute x1, starting transfers between devices, per_device(): second = lax.ppermute(jnp.where(even, low, high), ('lat', 'lon'), pairs[1])  6.38 us
    all_to_all x1, starting transfers between devices, per_device(): lax.all_to_all(filtered, 'lon', split_axis=0, concat_axis=0, tiled=True)  3.8 us
    pallas_call x1, Pallas kernels, filter_rows(): pl.pallas_call(filter_kernel, out_shape=jax.ShapeDtypeStruct((blocks.shap...  2.48 us
    ppermute x1, starting transfers between devices, per_device(): lax.ppermute(halves[1:2], 'lon', [(x, x ^ 1) for x in range(lon_size)])  2.38 us
    pallas_call x1, Pallas kernels, pole_rows(): pl.pallas_call(pole_kernel, out_shape=jax.ShapeDtypeStruct((2, WIDE), jnp...  2.21 us
  transfers between devices with their start and end apart: 5, of which 3 were waited for; matrix products, arithmetic and copies ran while one was open for 3% of the time, Pallas kernels for 6%

profile of v8, /device:TPU:97, one launch (start us, length us, event | category | flops | bytes accessed | tf_op | source)
XLA Modules:
  0.0 61.5 jit_solution(5928833024552199477)
XLA Ops:
  0.6 2.0 %pack.1 = f32[32,8,768]{2,1,0:T(8,128)} custom-call(s32[1]{0:T(128)} %bitcast.1.north_ref, f32[16,8,720]{2,1,0:T(8,128)} %bitcast.35, f32[8,8,720]{2,1,0:T(8,128)} %bitcast.36, f32[8,8,720]{2,1,0:T(8,128)} %bitcast.37), custom_call_target="tpu_custom_call" | custom-call | tf_op jit(solution)/shard_map/pack/pallas_call | solution.py:470
  2.7 7.9 %all-to-all-start = ((f32[32,8,768]{2,1,0:T(8,128)}), f32[32,8,768]{2,1,0:T(8,128)S(1)}, u32[]{:S(2)}, u32[]{:S(2)}) async-start(f32[32,8,768]{2,1,0:T(8,128)} %pack.1), calls=%async_computation | async-start | bytes 1572864 | tf_op jit(solution)/shard_map/all_to_all | solution.py:644
  10.6 0.6 %copy-done.4 = s32[64]{0:T(128)S(1)} copy-done((s32[64]{0:T(128)S(1)}, s32[64]{0:T(128)}, u32[]{:S(2)}) %copy-start.4) | copy-done | bytes 280
  11.3 0.7 %copy-done.3 = f32[64]{0:T(128)S(1)} copy-done((f32[64]{0:T(128)S(1)}, f32[64]{0:T(128)}, u32[]{:S(2)}) %copy-start.3) | copy-done | bytes 280
  11.9 0.1 fusion.3
  12.0 0.1 copy.18.cut_ref
  12.1 0.1 cosine_divide_fusion
  12.2 0.1 multiply_bitcast_fusion.1
  12.3 0.1 copy.19.early_ref.coef_ref
  12.4 12.4 %all-to-all-done.x_ref = f32[32,8,768]{2,1,0:T(8,128)S(1)} async-done(((f32[32,8,768]{2,1,0:T(8,128)}), f32[32,8,768]{2,1,0:T(8,128)S(1)}, u32[]{:S(2)}, u32[]{:S(2)}) %all-to-all-start) | async-done | bytes 786464 | tf_op jit(solution)/shard_map/all_to_all | solution.py:644
  24.8 2.5 %polar_filter.1 = f32[32,8,768]{2,1,0:T(8,128)} custom-call(f32[32,8,768]{2,1,0:T(8,128)S(1)} %all-to-all-done.x_ref, f32[8,2]{1,0:T(8,128)S(1)} %copy.18.cut_ref, f32[4,91,128]{2,1,0:T(8,128)S(1)} %copy-done.2, bf16[768,256]{1,0:T(8,128)(2,1)S(1)} %copy-done.1, bf16[768,256]{1,0:T(8,128)(2,1)S(1)} %copy-done, f32[64,4]{1,0:T(8,128)S(1)} %copy.19.early_ref.coef_ref), custom_call_target="tpu_custom_call" | custom-call | tf_op jit(solution)/shard_map/polar_filter/pallas_call | solution.py:414
  27.3 3.8 %all-to-all-start.1 = ((f32[32,8,768]{2,1,0:T(8,128)}), f32[32,8,768]{2,1,0:T(8,128)S(1)}, u32[]{:S(2)}, u32[]{:S(2)}) async-start(f32[32,8,768]{2,1,0:T(8,128)} %polar_filter.1), calls=%async_computation.1 | async-start | bytes 1572864 | tf_op jit(solution)/shard_map/all_to_all | solution.py:669
  31.2 0.6 fusion.4
  33.1 0.6 fusion.5
  35.0 0.1 pad_maximum_fusion.4
  35.1 10.3 %all-to-all-done.1.field_ref = f32[32,8,768]{2,1,0:T(8,128)S(1)} async-done(((f32[32,8,768]{2,1,0:T(8,128)}), f32[32,8,768]{2,1,0:T(8,128)S(1)}, u32[]{:S(2)}, u32[]{:S(2)}) %all-to-all-start.1) | async-done | bytes 786464 | tf_op jit(solution)/shard_map/all_to_all | solution.py:669
  45.4 1.9 %collective-permute-start.1 = (f32[3,768]{1,0:T(4,128)S(1)}, f32[3,768]{1,0:T(4,128)S(1)}, u32[]{:S(2)}, u32[]{:S(2)}) collective-permute-start(f32[3,768]{1,0:T(4,128)S(1)} %get-tuple-element.15), channel_id=1, source_target_pairs={{0,32},{1,33},{2,34},{3,35},{4,36},{5,37},{6,38},{7,39},{8,40},{9,... | collective-permute-start | bytes 27656 | tf_op jit(solution)/shard_map/ppermute | solution.py:693
  47.3 6.4 %collective-permute-start = (f32[3,768]{1,0:T(4,128)S(1)}, f32[3,768]{1,0:T(4,128)S(1)}, u32[]{:S(2)}, u32[]{:S(2)}) collective-permute-start(f32[3,768]{1,0:T(4,128)S(1)} %get-tuple-element.16), channel_id=1, source_target_pairs={{32,64},{33,65},{34,66},{35,67},{36,68},{37,69},{38,70},{39,71},{4... | collective-permute-start | bytes 27656 | tf_op jit(solution)/shard_map/ppermute | solution.py:694
  53.7 0.1 pad_add_fusion.where_ref
  53.8 2.2 %pole_filter.1.mine_ref = f32[2,768]{1,0:T(2,128)S(1)} custom-call(s32[4]{0:T(128)S(1)} %pad_add_fusion.where_ref, f32[32,8,768]{2,1,0:T(8,128)S(1)} %all-to-all-done.x_ref, f32[8,2]{1,0:T(8,128)S(1)} %broadcast_in_dim.27.cut_ref, f32[4,91,128]{2,1,0:T(8,128)S(1)} %copy-done.2, bf16[768,256]{1,0:T(8,128)(2,1)S(1)} %copy-done.1, bf16[768,256]{1,0:T(8,128)(2,1)S(1)} %copy-done), custom_call_target="tpu_custom_call" | custom-call | tf_op jit(solution)/shard_map/pole_filter/pallas_call | solution.py:379
  56.0 2.4 %collective-permute-start.2 = (f32[1,768]{1,0:T(1,128)S(1)}, f32[1,768]{1,0:T(1,128)S(1)}, u32[]{:S(2)}, u32[]{:S(2)}) collective-permute-start(f32[1,768]{1,0:T(1,128)S(1)} %slice.58), channel_id=1, source_target_pairs={{0,1},{1,0},{2,3},{3,2},{4,5},{5,4},{6,7},{7,6},{8,9},{9,8},{10,11... | collective-permute-start | bytes 9224 | tf_op jit(solution)/shard_map/ppermute | solution.py:678
  58.4 0.8 %collective-permute-done.2.theirs_ref = f32[1,768]{1,0:T(1,128)S(1)} collective-permute-done((f32[1,768]{1,0:T(1,128)S(1)}, f32[1,768]{1,0:T(1,128)S(1)}, u32[]{:S(2)}, u32[]{:S(2)}) %collective-permute-start.2) | collective-permute-done | bytes 3104 | tf_op jit(solution)/shard_map/ppermute | solution.py:678
  59.2 1.5 %stencil_main.1 = (f32[2,64,720]{2,1,0:T(8,128)}, f32[64,720]{1,0:T(8,128)}, f32[64,720]{1,0:T(8,128)}) custom-call(f32[32,8,768]{2,1,0:T(8,128)S(1)} %all-to-all-done.1.field_ref, f32[64,4]{1,0:T(8,128)S(1)} %copy.19.early_ref.coef_ref), custom_call_target="tpu_custom_call" | custom-call | flops 10000000 | bytes 1600000 | tf_op jit(solution)/shard_map/stencil_main/pallas_call | solution.py:599
  60.7 0.8 %stencil_edge.1 = (f32[2,64,720]{2,1,0:T(8,128)}, f32[64,720]{1,0:T(8,128)}, f32[64,720]{1,0:T(8,128)}) custom-call(s32[1]{0:T(128)} %bitcast.state_ref, f32[32,8,768]{2,1,0:T(8,128)S(1)} %all-to-all-done.1.field_ref, f32[3,768]{1,0:T(4,128)S(1)} %collective-permute-done.second_ref, ...), custom_call_target="tpu_custom_call", output_to_operand_aliasing={{0}: (6, {}), {1}: (7, {}), {2}: (8, {})} | custom-call | tf_op jit(solution)/shard_map/stencil_edge/pallas_call | solution.py:622
  (19 shorter events, 0.2 us)
Async XLA Ops:
  2.6 22.2 %copy-start = (bf16[768,256]{1,0:T(8,128)(2,1)S(1)}, bf16[768,256]{1,0:T(8,128)(2,1)}, u32[]{:S(2)}) copy-start(bf16[768,256]{1,0:T(8,128)(2,1)} %constant.136.clone.inverse_ref) | copy-start | bytes 1179652
  2.6 22.2 %copy-start.1 = (bf16[768,256]{1,0:T(8,128)(2,1)S(1)}, bf16[768,256]{1,0:T(8,128)(2,1)}, u32[]{:S(2)}) copy-start(bf16[768,256]{1,0:T(8,128)(2,1)} %constant.135.clone.forward_ref) | copy-start | bytes 1179652
  2.7 22.2 %copy-start.2 = (f32[4,91,128]{2,1,0:T(8,128)S(1)}, f32[4,91,128]{2,1,0:T(8,128)}, u32[]{:S(2)}) copy-start(f32[4,91,128]{2,1,0:T(8,128)} %constant.134.clone.rows_ref) | copy-start | bytes 559108
  2.7 22.1 %all-to-all-start = ((f32[32,8,768]{2,1,0:T(8,128)}), f32[32,8,768]{2,1,0:T(8,128)S(1)}, u32[]{:S(2)}, u32[]{:S(2)}) async-start(f32[32,8,768]{2,1,0:T(8,128)} %pack.1), calls=%async_computation | async-start | bytes 1572864 | tf_op jit(solution)/shard_map/all_to_all | solution.py:644
  10.6 0.7 %copy-start.4 = (s32[64]{0:T(128)S(1)}, s32[64]{0:T(128)}, u32[]{:S(2)}) copy-start(s32[64]{0:T(128)} %param.11) | copy-start | bytes 772
  11.3 0.7 %copy-start.3 = (f32[64]{0:T(128)S(1)}, f32[64]{0:T(128)}, u32[]{:S(2)}) copy-start(f32[64]{0:T(128)} %param.12) | copy-start | bytes 772
  27.3 18.0 %all-to-all-start.1 = ((f32[32,8,768]{2,1,0:T(8,128)}), f32[32,8,768]{2,1,0:T(8,128)S(1)}, u32[]{:S(2)}, u32[]{:S(2)}) async-start(f32[32,8,768]{2,1,0:T(8,128)} %polar_filter.1), calls=%async_computation.1 | async-start | bytes 1572864 | tf_op jit(solution)/shard_map/all_to_all | solution.py:669
  45.4 15.3 %collective-permute-start.1 = (f32[3,768]{1,0:T(4,128)S(1)}, f32[3,768]{1,0:T(4,128)S(1)}, u32[]{:S(2)}, u32[]{:S(2)}) collective-permute-start(f32[3,768]{1,0:T(4,128)S(1)} %get-tuple-element.15), channel_id=1, source_target_pairs={{0,32},{1,33},{2,34},{3,35},{4,36},{5,37},{6,38},{7,39},{8,40},{9,... | collective-permute-start | bytes 27656 | tf_op jit(solution)/shard_map/ppermute | solution.py:693
  47.3 13.4 %collective-permute-start = (f32[3,768]{1,0:T(4,128)S(1)}, f32[3,768]{1,0:T(4,128)S(1)}, u32[]{:S(2)}, u32[]{:S(2)}) collective-permute-start(f32[3,768]{1,0:T(4,128)S(1)} %get-tuple-element.16), channel_id=1, source_target_pairs={{32,64},{33,65},{34,66},{35,67},{36,68},{37,69},{38,70},{39,71},{4... | collective-permute-start | bytes 27656 | tf_op jit(solution)/shard_map/ppermute | solution.py:694
  56.0 3.2 %collective-permute-start.2 = (f32[1,768]{1,0:T(1,128)S(1)}, f32[1,768]{1,0:T(1,128)S(1)}, u32[]{:S(2)}, u32[]{:S(2)}) collective-permute-start(f32[1,768]{1,0:T(1,128)S(1)} %slice.58), channel_id=1, source_target_pairs={{0,1},{1,0},{2,3},{3,2},{4,5},{5,4},{6,7},{7,6},{8,9},{9,8},{10,11... | collective-permute-start | bytes 9224 | tf_op jit(solution)/shard_map/ppermute | solution.py:678
